TPU v7x, 32 devices: a whole 2x2x4 slice. The times are simulated.
32 devices in a mesh: dp: 4 (over y, x), fsdp: 8 (over z, core).
Axes of the slice: x: 2, y: 2, z: 4, core: 2. Of those that a mesh axis runs over, the one named last changes fastest.
Arguments:
- hidden_in: bfloat16 [6400, 2048], P(('dp', 'fsdp')), may hold values from -6 to 6
- segment_ids: int32 [6400], P(('dp', 'fsdp')), may hold values from 0 to 19, as said below
- parents: int32 [4, 20], P('dp'), may hold values from 0 to 19, as said below
- norm_gain: bfloat16 [2048], P(('dp', 'fsdp')), may hold values from 0.099609375 to 1.8984375
- w_qdown: bfloat16 [2048, 1024], P(('dp', 'fsdp')), may hold values from -0.125 to 0.125
- q_gain: bfloat16 [1024], P(('dp', 'fsdp')), may hold values from 0.099609375 to 1.8984375
- w_qup: bfloat16 [1024, 4096], P(('dp', 'fsdp')), may hold values from -0.375 to 0.375
- w_key: bfloat16 [2048, 256], P(('dp', 'fsdp')), may hold values from -0.125 to 0.125
- w_value: bfloat16 [2048, 256], P(('dp', 'fsdp')), may hold values from -0.125 to 0.125
- w_out: bfloat16 [4096, 2048], P(('dp', 'fsdp')), may hold values from -0.375 to 0.375
- ffn_gain: bfloat16 [2048], P(('dp', 'fsdp')), may hold values from 0.099609375 to 1.8984375
- w_gate: bfloat16 [2048, 5632], P(('dp', 'fsdp')), may hold values from -0.125 to 0.125
- w_up: bfloat16 [2048, 5632], P(('dp', 'fsdp')), may hold values from -0.125 to 0.125
- w_down: bfloat16 [5632, 2048], P(('dp', 'fsdp')), may hold values from -0.15625 to 0.15625
- cotangent: bfloat16 [6400, 2048], P(('dp', 'fsdp')), may hold values from -6 to 6
Outputs:
- layer_out: bfloat16 [6400, 2048], P(('dp', 'fsdp'))
- grad_in: bfloat16 [6400, 2048], P(('dp', 'fsdp'))
- grad_norm_gain: float32 [2048], P(('dp', 'fsdp'))
- grad_w_qdown: float32 [2048, 1024], P(('dp', 'fsdp'))
- grad_q_gain: float32 [1024], P(('dp', 'fsdp'))
- grad_w_qup: float32 [1024, 4096], P(('dp', 'fsdp'))
- grad_w_key: float32 [2048, 256], P(('dp', 'fsdp'))
- grad_w_value: float32 [2048, 256], P(('dp', 'fsdp'))
- grad_w_out: float32 [4096, 2048], P(('dp', 'fsdp'))
- grad_ffn_gain: float32 [2048], P(('dp', 'fsdp'))
- grad_w_gate: float32 [2048, 5632], P(('dp', 'fsdp'))
- grad_w_up: float32 [2048, 5632], P(('dp', 'fsdp'))
- grad_w_down: float32 [5632, 2048], P(('dp', 'fsdp'))
Inputs may be any that keep to these rules, and one draw needn't show every extreme that they name: `parents`: each tree has 20 segments: the root, whose parent number is its own, begins a chain of 8 segments; the last of the chain has 4 children, and each of these has 2 children that have none. Segment numbers are a permutation within each tree. `segment_ids`: each tree's tokens form 20 runs of 80 tokens, one segment a run; a segment's run comes after its parent's: the chain first in its order, then the 4 middle segments, then the 8 last ones.
All inputs are finite; a program needn't handle non-finite values.
Results may differ from a plain program's by a relative error of at most 0.025.
Values may be sent and summed in bfloat16 or wider, within the bound.
No kernel may reach another device: no remote copies, remote signals or barrier semaphores. Data moves between devices by JAX's collectives and lax.ppermute only.
A program may use at most 320 MiB of HBM per device.

v0:
```python
import jax
import jax.numpy as jnp
from jax import lax
from jax.sharding import PartitionSpec as P

H = 16
HD = 256
NSEG = 20


EPSILON = 1e-06
ROPE_BASE = 10000.0
HIGHEST = lax.Precision.HIGHEST
NEGATIVE = -1e30


def rotate(values, cosines, sine_table):
    half_width = values.shape[-1] // 2
    first_half = values[..., :half_width]
    second_half = values[..., half_width:]
    return jnp.concatenate(
        [
            first_half * cosines - second_half * sine_table,
            second_half * cosines + first_half * sine_table,
        ],
        axis=-1,
    )


def unrotate(gradient, cosines, sine_table):
    half_width = gradient.shape[-1] // 2
    first_half = gradient[..., :half_width]
    second_half = gradient[..., half_width:]
    return jnp.concatenate(
        [
            first_half * cosines + second_half * sine_table,
            second_half * cosines - first_half * sine_table,
        ],
        axis=-1,
    )


def rms_scale(values):
    return lax.rsqrt(jnp.mean(values * values, axis=-1, keepdims=True) + EPSILON)


def norm_back(upstream, normed, row_scale, gain_vec):
    scaled = upstream * gain_vec
    inner_mean = jnp.mean(scaled * normed, axis=-1, keepdims=True)
    return (row_scale * (scaled - normed * inner_mean), jnp.sum(upstream * normed, axis=0))


def outer_sum(left_rows, right_rows):
    return jnp.einsum("tr,tc->rc", left_rows, right_rows, preferred_element_type=jnp.float32)


def times_transposed(left_rows, weight):
    return jnp.einsum("tc,rc->tr", left_rows, weight, preferred_element_type=jnp.float32)


def grouped(values, groups_dp, groups_fsdp):
    lead_dims = values.shape[:-1]
    last_width = values.shape[-1]
    split_view = values.reshape(
        lead_dims + (groups_dp, groups_fsdp, last_width // (groups_dp * groups_fsdp))
    )
    return jnp.swapaxes(split_view, -3, -2).reshape(lead_dims + (last_width,))


def body(
    hidden_in,
    segment_ids,
    parents,
    norm_gain,
    w_qdown,
    q_gain,
    w_qup,
    w_key,
    w_value,
    w_out,
    ffn_gain,
    w_gate,
    w_up,
    w_down,
    cotangent,
):
    row_count = hidden_in.shape[0]
    groups_dp = lax.axis_size("dp")
    groups_fsdp = lax.axis_size("fsdp")
    tree_len = row_count * groups_fsdp
    seg_len = tree_len // NSEG
    block_len = tree_len // 4
    score_scale = HD ** (-0.5)

    def arrange(values):
        return grouped(values, groups_dp, groups_fsdp)

    labels = jnp.arange(NSEG, dtype=jnp.int32)
    parent_row = parents[0]

    def climb(step_index, state_pair):
        current, ancestry = state_pair
        current = parent_row[current]
        return (
            current,
            jnp.maximum(ancestry, (current[:, None] == labels[None, :]).astype(jnp.float32)),
        )

    ancestry = lax.fori_loop(
        0, NSEG - 1, climb, (labels, (labels[:, None] == labels[None, :]).astype(jnp.float32))
    )[1]
    seg_depth = jnp.sum(ancestry, axis=1) - 1.0
    own_hits = (segment_ids[:, None] == labels[None, :]).astype(jnp.float32)
    own_ancestors = jnp.dot(own_hits, ancestry, precision=HIGHEST)
    own_depth = jnp.dot(own_hits, seg_depth, precision=HIGHEST)
    own_rows = lax.axis_index("fsdp") * row_count + jnp.arange(row_count, dtype=jnp.int32)
    offsets = (own_rows % seg_len).astype(jnp.float32)
    positions = own_depth * seg_len + offsets
    inverse = ROPE_BASE ** (-(jnp.arange(HD // 2, dtype=jnp.float32) * 2.0) / HD)
    angles = positions[:, None] * inverse[None, :]
    cosines = jnp.cos(angles)
    sine_table = jnp.sin(angles)
    gain_one, down_full, gain_latent, up_full, key_full, value_full, out_full = (
        lax.all_gather(norm_gain, ("dp", "fsdp"), axis=0, tiled=True),
        lax.all_gather(w_qdown, ("dp", "fsdp"), axis=0, tiled=True),
        lax.all_gather(q_gain, ("dp", "fsdp"), axis=0, tiled=True),
        lax.all_gather(w_qup, ("dp", "fsdp"), axis=0, tiled=True),
        lax.all_gather(w_key, ("dp", "fsdp"), axis=0, tiled=True),
        lax.all_gather(w_value, ("dp", "fsdp"), axis=0, tiled=True),
        lax.all_gather(w_out, ("dp", "fsdp"), axis=0, tiled=True),
    )
    inputs = hidden_in.astype(jnp.float32)
    scale_one = rms_scale(inputs)
    normed_one = inputs * scale_one
    normed_in = (normed_one * gain_one.astype(jnp.float32)).astype(jnp.bfloat16)
    latent = jnp.dot(normed_in, down_full, preferred_element_type=jnp.float32)
    scale_latent = rms_scale(latent)
    normed_latent = latent * scale_latent
    latent_in = (normed_latent * gain_latent.astype(jnp.float32)).astype(jnp.bfloat16)
    queries = jnp.dot(latent_in, up_full, preferred_element_type=jnp.float32).reshape(
        row_count, H, HD
    )
    query_rot = rotate(queries, cosines[:, None, :], sine_table[:, None, :]).astype(jnp.bfloat16)
    key_rot = rotate(
        jnp.dot(normed_in, key_full, preferred_element_type=jnp.float32), cosines, sine_table
    ).astype(jnp.bfloat16)
    value_own = jnp.dot(normed_in, value_full, preferred_element_type=jnp.float32).astype(
        jnp.bfloat16
    )
    tree_keys, tree_values, tree_labels = (
        lax.all_gather(key_rot, "fsdp", axis=0, tiled=True),
        lax.all_gather(value_own, "fsdp", axis=0, tiled=True),
        lax.all_gather(segment_ids.astype(jnp.bfloat16), "fsdp", axis=0, tiled=True),
    )
    key_labels = tree_labels.astype(jnp.int32)
    key_hits = (key_labels[:, None] == labels[None, :]).astype(jnp.float32)
    key_rows = jnp.arange(tree_len, dtype=jnp.int32)
    reach_mask = jnp.einsum("qs,ks->qk", own_ancestors, key_hits, precision=HIGHEST) > 0.5
    causal = (segment_ids[:, None] != key_labels[None, :]) | (
        key_rows[None, :] <= own_rows[:, None]
    )
    visible = jnp.swapaxes((reach_mask & causal).reshape(row_count, 4, block_len), 0, 1)
    blocks = (tree_keys.reshape(4, block_len, HD), tree_values.reshape(4, block_len, HD), visible)

    def scores_of(key_block):
        return (
            jnp.einsum("qhd,kd->qhk", query_rot, key_block, preferred_element_type=jnp.float32)
            * score_scale
        )

    def total_pass(state_pair, block_data):
        running_max, running_sum = state_pair
        key_block, value_block, visible_block = block_data
        allowed = visible_block[:, None, :]
        scores = jnp.where(allowed, scores_of(key_block), NEGATIVE)
        new_max = jnp.maximum(running_max, jnp.max(scores, axis=-1))
        exp_terms = jnp.where(allowed, jnp.exp(scores - new_max[..., None]), 0.0)
        running_sum = running_sum * jnp.exp(running_max - new_max) + jnp.sum(exp_terms, axis=-1)
        return ((new_max, running_sum), None)

    start_pair = (
        jnp.full((row_count, H), NEGATIVE, jnp.float32),
        jnp.zeros((row_count, H), jnp.float32),
    )
    (final_max, final_sum), unused_out = lax.scan(total_pass, start_pair, blocks)
    log_total = final_max + jnp.log(final_sum)

    def value_pass(running_acc, block_data):
        key_block, value_block, visible_block = block_data
        scores = scores_of(key_block)
        probabilities = jnp.where(
            visible_block[:, None, :], jnp.exp(scores - log_total[..., None]), 0.0
        )
        return (
            running_acc
            + jnp.einsum(
                "qhk,kd->qhd",
                probabilities.astype(jnp.bfloat16),
                value_block,
                preferred_element_type=jnp.float32,
            ),
            None,
        )

    attended, unused_acc = lax.scan(value_pass, jnp.zeros((row_count, H, HD), jnp.float32), blocks)
    out_in = attended.reshape(row_count, H * HD).astype(jnp.bfloat16)
    mixed = inputs + jnp.dot(out_in, out_full, preferred_element_type=jnp.float32)
    gain_two, gate_full, up_proj, down_proj = (
        lax.all_gather(ffn_gain, ("dp", "fsdp"), axis=0, tiled=True),
        lax.all_gather(w_gate, ("dp", "fsdp"), axis=0, tiled=True),
        lax.all_gather(w_up, ("dp", "fsdp"), axis=0, tiled=True),
        lax.all_gather(w_down, ("dp", "fsdp"), axis=0, tiled=True),
    )
    scale_two = rms_scale(mixed)
    normed_two = mixed * scale_two
    normed_mid = (normed_two * gain_two.astype(jnp.float32)).astype(jnp.bfloat16)
    gate_pre = jnp.dot(normed_mid, gate_full, preferred_element_type=jnp.float32)
    up_pre = jnp.dot(normed_mid, up_proj, preferred_element_type=jnp.float32)
    gate_sig = jax.nn.sigmoid(gate_pre)
    activated = (gate_pre * gate_sig * up_pre).astype(jnp.bfloat16)
    layer_out = (mixed + jnp.dot(activated, down_proj, preferred_element_type=jnp.float32)).astype(
        jnp.bfloat16
    )
    gain_two, gate_full, up_proj, down_proj = (
        lax.all_gather(ffn_gain, ("dp", "fsdp"), axis=0, tiled=True),
        lax.all_gather(w_gate, ("dp", "fsdp"), axis=0, tiled=True),
        lax.all_gather(w_up, ("dp", "fsdp"), axis=0, tiled=True),
        lax.all_gather(w_down, ("dp", "fsdp"), axis=0, tiled=True),
    )
    upstream = cotangent.astype(jnp.float32)
    act_grad = times_transposed(cotangent, down_proj)
    gate_grad = (act_grad * up_pre * gate_sig * (1.0 + gate_pre * (1.0 - gate_sig))).astype(
        jnp.bfloat16
    )
    up_grad = (act_grad * gate_pre * gate_sig).astype(jnp.bfloat16)
    gate_rows, up_rows, out_rows = (
        lax.all_gather(gate_grad, "fsdp", axis=0, tiled=True),
        lax.all_gather(up_grad, "fsdp", axis=0, tiled=True),
        lax.all_gather(cotangent, "fsdp", axis=0, tiled=True),
    )
    mid_cols, act_cols = (
        lax.all_to_all(arrange(normed_mid), "fsdp", split_axis=1, concat_axis=0, tiled=True),
        lax.all_to_all(arrange(activated), "fsdp", split_axis=1, concat_axis=0, tiled=True),
    )
    gate_part = outer_sum(mid_cols, gate_rows)
    up_part = outer_sum(mid_cols, up_rows)
    down_part = outer_sum(act_cols, out_rows)
    ffn_grads = (
        lax.psum_scatter(
            gate_part.astype(jnp.bfloat16), "dp", scatter_dimension=0, tiled=True
        ).astype(jnp.float32),
        lax.psum_scatter(
            up_part.astype(jnp.bfloat16), "dp", scatter_dimension=0, tiled=True
        ).astype(jnp.float32),
        lax.psum_scatter(
            down_part.astype(jnp.bfloat16), "dp", scatter_dimension=0, tiled=True
        ).astype(jnp.float32),
    )
    mid_grad = times_transposed(gate_grad, gate_full) + times_transposed(up_grad, up_proj)
    mixed_back, gain_two_grad = norm_back(
        mid_grad, normed_two, scale_two, gain_two.astype(jnp.float32)
    )
    mixed_grad = upstream + mixed_back
    gain_one, down_full, gain_latent, up_full, key_full, value_full, out_full = (
        lax.all_gather(norm_gain, ("dp", "fsdp"), axis=0, tiled=True),
        lax.all_gather(w_qdown, ("dp", "fsdp"), axis=0, tiled=True),
        lax.all_gather(q_gain, ("dp", "fsdp"), axis=0, tiled=True),
        lax.all_gather(w_qup, ("dp", "fsdp"), axis=0, tiled=True),
        lax.all_gather(w_key, ("dp", "fsdp"), axis=0, tiled=True),
        lax.all_gather(w_value, ("dp", "fsdp"), axis=0, tiled=True),
        lax.all_gather(w_out, ("dp", "fsdp"), axis=0, tiled=True),
    )
    branch_grad = mixed_grad.astype(jnp.bfloat16)
    out_w_grad = outer_sum(arrange(out_in), branch_grad)
    attended_grad = (
        times_transposed(branch_grad, out_full).astype(jnp.bfloat16).reshape(row_count, H, HD)
    )
    row_delta = jnp.sum(attended_grad.astype(jnp.float32) * attended, axis=-1)

    def back_pass(query_acc, block_data):
        key_block, value_block, visible_block = block_data
        scores = scores_of(key_block)
        probabilities = jnp.where(
            visible_block[:, None, :], jnp.exp(scores - log_total[..., None]), 0.0
        )
        value_part = jnp.einsum(
            "qhk,qhd->kd",
            probabilities.astype(jnp.bfloat16),
            attended_grad,
            preferred_element_type=jnp.float32,
        )
        prob_grad = jnp.einsum(
            "qhd,kd->qhk", attended_grad, value_block, preferred_element_type=jnp.float32
        )
        score_grad = (probabilities * (prob_grad - row_delta[..., None])).astype(jnp.bfloat16)
        query_acc = (
            query_acc
            + jnp.einsum("qhk,kd->qhd", score_grad, key_block, preferred_element_type=jnp.float32)
            * score_scale
        )
        key_part = (
            jnp.einsum("qhk,qhd->kd", score_grad, query_rot, preferred_element_type=jnp.float32)
            * score_scale
        )
        return (query_acc, (key_part, value_part))

    query_grad, (key_parts, value_parts) = lax.scan(
        back_pass, jnp.zeros((row_count, H, HD), jnp.float32), blocks
    )
    key_own_grad, value_own_grad = (
        lax.psum_scatter(
            key_parts.reshape(tree_len, HD).astype(jnp.bfloat16),
            "fsdp",
            scatter_dimension=0,
            tiled=True,
        ).astype(jnp.float32),
        lax.psum_scatter(
            value_parts.reshape(tree_len, HD).astype(jnp.bfloat16),
            "fsdp",
            scatter_dimension=0,
            tiled=True,
        ).astype(jnp.float32),
    )
    key_in_grad = unrotate(key_own_grad, cosines, sine_table).astype(jnp.bfloat16)
    value_in_grad = value_own_grad.astype(jnp.bfloat16)
    query_in_grad = (
        unrotate(query_grad, cosines[:, None, :], sine_table[:, None, :])
        .reshape(row_count, H * HD)
        .astype(jnp.bfloat16)
    )
    qup_w_grad = outer_sum(arrange(latent_in), query_in_grad)
    latent_pre_grad = times_transposed(query_in_grad, up_full)
    latent_back, gain_latent_grad = norm_back(
        latent_pre_grad, normed_latent, scale_latent, gain_latent.astype(jnp.float32)
    )
    latent_grad = latent_back.astype(jnp.bfloat16)
    normed_cols = arrange(normed_in)
    qdown_w_grad = outer_sum(normed_cols, latent_grad)
    key_w_grad = outer_sum(normed_cols, key_in_grad)
    value_w_grad = outer_sum(normed_cols, value_in_grad)
    normed_grad = (
        times_transposed(latent_grad, down_full)
        + times_transposed(key_in_grad, key_full)
        + times_transposed(value_in_grad, value_full)
    )
    input_back, gain_one_grad = norm_back(
        normed_grad, normed_one, scale_one, gain_one.astype(jnp.float32)
    )
    grad_in = (mixed_grad + input_back).astype(jnp.bfloat16)
    attn_part = (
        lax.psum_scatter(
            arrange(gain_one_grad).astype(jnp.bfloat16), "fsdp", scatter_dimension=0, tiled=True
        ).astype(jnp.float32),
        lax.psum_scatter(
            qdown_w_grad.astype(jnp.bfloat16), "fsdp", scatter_dimension=0, tiled=True
        ).astype(jnp.float32),
        lax.psum_scatter(
            arrange(gain_latent_grad).astype(jnp.bfloat16), "fsdp", scatter_dimension=0, tiled=True
        ).astype(jnp.float32),
        lax.psum_scatter(
            qup_w_grad.astype(jnp.bfloat16), "fsdp", scatter_dimension=0, tiled=True
        ).astype(jnp.float32),
        lax.psum_scatter(
            key_w_grad.astype(jnp.bfloat16), "fsdp", scatter_dimension=0, tiled=True
        ).astype(jnp.float32),
        lax.psum_scatter(
            value_w_grad.astype(jnp.bfloat16), "fsdp", scatter_dimension=0, tiled=True
        ).astype(jnp.float32),
        lax.psum_scatter(
            out_w_grad.astype(jnp.bfloat16), "fsdp", scatter_dimension=0, tiled=True
        ).astype(jnp.float32),
        lax.psum_scatter(
            arrange(gain_two_grad).astype(jnp.bfloat16), "fsdp", scatter_dimension=0, tiled=True
        ).astype(jnp.float32),
    )
    attn_grads = (
        lax.psum_scatter(
            attn_part[0].astype(jnp.bfloat16), "dp", scatter_dimension=0, tiled=True
        ).astype(jnp.float32),
        lax.psum_scatter(
            attn_part[1].astype(jnp.bfloat16), "dp", scatter_dimension=0, tiled=True
        ).astype(jnp.float32),
        lax.psum_scatter(
            attn_part[2].astype(jnp.bfloat16), "dp", scatter_dimension=0, tiled=True
        ).astype(jnp.float32),
        lax.psum_scatter(
            attn_part[3].astype(jnp.bfloat16), "dp", scatter_dimension=0, tiled=True
        ).astype(jnp.float32),
        lax.psum_scatter(
            attn_part[4].astype(jnp.bfloat16), "dp", scatter_dimension=0, tiled=True
        ).astype(jnp.float32),
        lax.psum_scatter(
            attn_part[5].astype(jnp.bfloat16), "dp", scatter_dimension=0, tiled=True
        ).astype(jnp.float32),
        lax.psum_scatter(
            attn_part[6].astype(jnp.bfloat16), "dp", scatter_dimension=0, tiled=True
        ).astype(jnp.float32),
        lax.psum_scatter(
            attn_part[7].astype(jnp.bfloat16), "dp", scatter_dimension=0, tiled=True
        ).astype(jnp.float32),
    )
    return (
        layer_out,
        grad_in,
        attn_grads[0],
        attn_grads[1],
        attn_grads[2],
        attn_grads[3],
        attn_grads[4],
        attn_grads[5],
        attn_grads[6],
        attn_grads[7],
        ffn_grads[0],
        ffn_grads[1],
        ffn_grads[2],
    )


def solution(mesh):
    placed = (
        P(("dp", "fsdp"), None),
        P(("dp", "fsdp")),
        P("dp", None),
        P(("dp", "fsdp")),
        P(("dp", "fsdp"), None),
        P(("dp", "fsdp")),
        P(("dp", "fsdp"), None),
        P(("dp", "fsdp"), None),
        P(("dp", "fsdp"), None),
        P(("dp", "fsdp"), None),
        P(("dp", "fsdp")),
        P(("dp", "fsdp"), None),
        P(("dp", "fsdp"), None),
        P(("dp", "fsdp"), None),
        P(("dp", "fsdp"), None),
    )
    return jax.shard_map(
        body,
        mesh=mesh,
        in_specs=placed,
        out_specs=(
            P(("dp", "fsdp"), None),
            P(("dp", "fsdp"), None),
            P(("dp", "fsdp")),
            P(("dp", "fsdp"), None),
            P(("dp", "fsdp")),
            P(("dp", "fsdp"), None),
            P(("dp", "fsdp"), None),
            P(("dp", "fsdp"), None),
            P(("dp", "fsdp"), None),
            P(("dp", "fsdp")),
            P(("dp", "fsdp"), None),
            P(("dp", "fsdp"), None),
            P(("dp", "fsdp"), None),
        ),
        check_vma=False,
    )
```

profile of v0, /device:TPU:0, one launch (start us, length us, event | category | flops | bytes accessed | tf_op | source)
XLA Modules:
  0.0 2177.5 jit_solution(16174511164807984141)
XLA Ops:
  13.6 42.2 %all-reduce.10 = (bf16[2048]{0:T(1024)(128)(2,1)S(1)}, bf16[1024]{0:T(1024)(128)(2,1)S(1)}, bf16[2048]{0:T(1024)(128)(2,1)S(1)}) all-reduce(bf16[2048]{0:T(1024)(128)(2,1)S(1)} %dynamic-update-slice.1, bf16[1024]{0:T(1024)(128)(2,1)S(1)} %dynamic-update-slice.2, ...), channel_id=1, replica_groups=mesh['dp'=4,'fsdp'=8] {'dp','fsdp'}, use_global_device_ids=true, to_apply=%add.1 | all-reduce | flops 5120 | bytes 20480
  57.4 14.6 all-reduce
  72.0 15.1 while.52
  93.4 30.1 %all-gather.18.cloned.1.call-done = bf16[2048,256]{1,0:T(8,128)(2,1)} async-done(((bf16[64,256]{1,0:T(8,128)(2,1)}), bf16[2048,256]{1,0:T(8,128)(2,1)}) %all-gather.18.cloned.1.call-update) | async-done | bytes 1048592 | tf_op jit(solution)/shard_map/all_gather | solution.py:129
  125.2 16.9 all_gather.65
  142.1 18.3 all_gather.70
  160.4 27.7 %all-gather.14.cloned.1.call-done = bf16[2048,1024]{1,0:T(8,128)(2,1)} async-done(((bf16[64,1024]{1,0:T(8,128)(2,1)}), bf16[2048,1024]{1,0:T(8,128)(2,1)}) %all-gather.14.cloned.1.call-update) | async-done | bytes 4194320 | tf_op jit(solution)/shard_map/all_gather | solution.py:125
  192.4 74.5 %all-gather.16.cloned.1.call-done = bf16[1024,4096]{1,0:T(8,128)(2,1)} async-done(((bf16[32,4096]{1,0:T(8,128)(2,1)}), bf16[1024,4096]{1,0:T(8,128)(2,1)}) %all-gather.16.cloned.1.call-update) | async-done | bytes 8388624 | tf_op jit(solution)/shard_map/all_gather | solution.py:127
  275.9 44.4 %while.53 = (s32[]{:T(128)}, f32[200,16]{0,1:T(8,128)S(1)}, f32[200,16]{0,1:T(8,128)S(1)}, pred[4,200,400]{1,2,0:T(8,128)(4,1)}, bf16[4,400,256]{2,1,0:T(8,128)(...) while((s32[]{:T(128)}, f32[200,16]{0,1:T(8,128)S(1)}, f32[200,16]{0,1:T(8,128)S(1)}, ...), condition=%wide.region_8.9_spmd.clone, body=%wide.region_5.8_spmd.clone.sunk | while | flops 665616000 | bytes 12570212 | solution.py:185
  320.3 67.0 %while.54 = (s32[]{:T(128)}, f32[200,16,256]{2,1,0:T(8,128)}, pred[4,200,400]{1,2,0:T(8,128)(4,1)}, bf16[4,400,256]{2,1,0:T(8,128)(2,1)}, bf16[200,16,256]{2,0,1...) while((s32[]{:T(128)}, f32[200,16,256]{2,1,0:T(8,128)}, ...), condition=%wide.region_10.11_spmd.clone, body=%wide.region_9.10_spmd.clone.sunk | while | flops 1317478400 | bytes 19095532 | solution.py:205
  326.3 6.3 copy.105
  342.4 6.0 copy.105
  359.4 6.1 copy.105
  376.3 6.0 copy.105
  392.5 8.6 multiply_reduce_fusion.3
  401.3 127.6 %all-gather.22.cloned.1.call-done = bf16[2048,5632]{1,0:T(8,128)(2,1)} async-done(((bf16[64,5632]{1,0:T(8,128)(2,1)}), bf16[2048,5632]{1,0:T(8,128)(2,1)}) %all-gather.22.cloned.1.call-update) | async-done | bytes 23068688 | tf_op jit(solution)/shard_map/all_gather | solution.py:210
  528.9 12.2 fusion.91
  541.1 133.4 %all-gather.24.cloned.1.call-done = bf16[2048,5632]{1,0:T(8,128)(2,1)} async-done(((bf16[64,5632]{1,0:T(8,128)(2,1)}), bf16[2048,5632]{1,0:T(8,128)(2,1)}) %all-gather.24.cloned.1.call-update) | async-done | bytes 23068688 | tf_op jit(solution)/shard_map/all_gather | solution.py:211
  674.6 22.2 %fusion.92 = f32[200,5632]{1,0:T(8,128)} fusion(bf16[200,2048]{1,0:T(8,128)(2,1)S(1)} %multiply_convert_fusion.3, bf16[2048,5632]{1,0:T(8,128)(2,1)} %all-gather.24.cloned.1.call-done), kind=kOutput, calls=%fused_computation.166 | convolution fusion | flops 4613734400 | bytes 28393472 | tf_op jit(solution)/shard_map/dot_general | solution.py:218
  696.7 123.5 %all-gather.26.cloned.1.call-done = bf16[5632,2048]{1,0:T(8,128)(2,1)} async-done(((bf16[176,2048]{1,0:T(8,128)(2,1)}), bf16[5632,2048]{1,0:T(8,128)(2,1)}) %all-gather.26.cloned.1.call-update) | async-done | bytes 23068688 | tf_op jit(solution)/shard_map/all_gather | solution.py:212
  820.2 16.9 multiply_convert_fusion
  837.2 12.3 fusion.93
  849.5 14.0 multiply_reduce_fusion.1
  865.6 11.8 convolution_convert_fusion.4
  880.1 118.7 %while.55 = (s32[]{:T(128)}, f32[200,16,256]{2,1,0:T(8,128)}, bf16[4,400,256]{2,1,0:T(8,128)(2,1)}, bf16[4,400,256]{2,1,0:T(8,128)(2,1)}, pred[4,200,400]{1,2,0:...) while((s32[]{:T(128)}, f32[200,16,256]{2,1,0:T(8,128)}, ...), condition=%wide.region_15.16_spmd.clone, body=%wide.region_14.15_spmd.clone.sunk | while | flops 3292160000 | bytes 122651928 | solution.py:307
  1001.9 26.9 %reduce-scatter.16.cloned.1.call-done = bf16[200,256]{1,0:T(8,128)(2,1)} async-done(((bf16[1600,256]{1,0:T(8,128)(2,1)}), bf16[200,256]{1,0:T(8,128)(2,1)}) %reduce-scatter.16.cloned.1.call-update) | async-done | bytes 102416 | tf_op jit(solution)/shard_map/reduce_scatter | solution.py:311
  1033.7 27.9 %reduce-scatter.18.cloned.1.call-done = bf16[200,256]{1,0:T(8,128)(2,1)} async-done(((bf16[1600,256]{1,0:T(8,128)(2,1)}), bf16[200,256]{1,0:T(8,128)(2,1)}) %reduce-scatter.18.cloned.1.call-update) | async-done | bytes 102416 | tf_op jit(solution)/shard_map/reduce_scatter | solution.py:317
  1066.3 6.4 multiply_reduce_fusion.4
  1091.4 8.5 convolution_convert_fusion
  1099.9 8.0 reshape.222
  1128.4 87.0 %reduce-scatter.20.cloned.1.call-done = bf16[256,1024]{1,0:T(8,128)(2,1)} async-done(((bf16[2048,1024]{1,0:T(8,128)(2,1)}), bf16[256,1024]{1,0:T(8,128)(2,1)}) %reduce-scatter.20.cloned.1.call-update) | async-done | bytes 524304 | tf_op jit(solution)/shard_map/reduce_scatter | solution.py:354
  1215.4 72.3 %all-gather.32.cloned.1.call-done = bf16[1600,2048]{1,0:T(8,128)(2,1)} async-done(((bf16[200,2048]{1,0:T(8,128)(2,1)}), bf16[1600,2048]{1,0:T(8,128)(2,1)}) %all-gather.32.cloned.1.call-update) | async-done | bytes 6553616 | tf_op jit(solution)/shard_map/all_gather | solution.py:239
  1287.7 9.5 convolution_convert_fusion.6
  1305.7 85.5 %reduce-scatter.24.cloned.1.call-done = bf16[128,4096]{1,0:T(8,128)(2,1)} async-done(((bf16[1024,4096]{1,0:T(8,128)(2,1)}), bf16[128,4096]{1,0:T(8,128)(2,1)}) %reduce-scatter.24.cloned.1.call-update) | async-done | bytes 1048592 | tf_op jit(solution)/shard_map/reduce_scatter | solution.py:360
  1391.4 164.6 %all-gather.28.cloned.1.call-done = bf16[1600,5632]{1,0:T(8,128)(2,1)} async-done(((bf16[200,5632]{1,0:T(8,128)(2,1)}), bf16[1600,5632]{1,0:T(8,128)(2,1)}) %all-gather.28.cloned.1.call-update) | async-done | bytes 18022416 | tf_op jit(solution)/shard_map/all_gather | solution.py:237
  1556.0 13.1 convolution_convert_fusion.2
  1569.3 147.7 %all-gather.30.cloned.1.call-done = bf16[1600,5632]{1,0:T(8,128)(2,1)} async-done(((bf16[200,5632]{1,0:T(8,128)(2,1)}), bf16[1600,5632]{1,0:T(8,128)(2,1)}) %all-gather.30.cloned.1.call-update) | async-done | bytes 18022416 | tf_op jit(solution)/shard_map/all_gather | solution.py:238
  1717.0 12.9 convolution_convert_fusion.1
  1733.6 152.1 %reduce-scatter.36.cloned.1.call-done = bf16[512,2048]{1,0:T(8,128)(2,1)} async-done(((bf16[4096,2048]{1,0:T(8,128)(2,1)}), bf16[512,2048]{1,0:T(8,128)(2,1)}) %reduce-scatter.36.cloned.1.call-update) | async-done | bytes 2097168 | tf_op jit(solution)/shard_map/reduce_scatter | solution.py:369
  1889.6 11.4 fusion.41
  1904.6 25.9 %all-reduce.11 = (bf16[2048]{0:T(1024)(128)(2,1)S(1)}, bf16[1024]{0:T(1024)(128)(2,1)S(1)}, bf16[2048]{0:T(1024)(128)(2,1)S(1)}) all-reduce(bf16[2048]{0:T(1024)(128)(2,1)S(1)} %convert_element_type.269, bf16[1024]{0:T(1024)(128)(2,1)S(1)} %convert_element_type.276, ...), channel_id=4, replica_groups=mesh['dp'=4,'fsdp'=8] {'fsdp'}, use_global_device_ids=true, to_apply=%region_21.22.clone | all-reduce | flops 5120 | bytes 20480
  1930.7 9.8 all-reduce.12
  1947.3 17.7 reduce-scatter.22.cloned.1.call-done
  1966.6 43.5 %reduce-scatter.44.cloned.1.call-done = bf16[176,2048]{1,0:T(8,128)(2,1)} async-done(((bf16[704,2048]{1,0:T(8,128)(2,1)}), bf16[176,2048]{1,0:T(8,128)(2,1)}) %reduce-scatter.44.cloned.1.call-update) | async-done | bytes 720912 | tf_op jit(solution)/shard_map/reduce_scatter | solution.py:255
  2012.5 28.5 %reduce-scatter.26.cloned.1.call-done = bf16[32,4096]{1,0:T(8,128)(2,1)} async-done(((bf16[128,4096]{1,0:T(8,128)(2,1)}), bf16[32,4096]{1,0:T(8,128)(2,1)}) %reduce-scatter.26.cloned.1.call-update) | async-done | bytes 262160 | tf_op jit(solution)/shard_map/reduce_scatter | solution.py:386
  2042.8 42.9 %reduce-scatter.40.cloned.1.call-done = bf16[64,5632]{1,0:T(8,128)(2,1)} async-done(((bf16[256,5632]{1,0:T(8,128)(2,1)}), bf16[64,5632]{1,0:T(8,128)(2,1)}) %reduce-scatter.40.cloned.1.call-update) | async-done | bytes 720912 | tf_op jit(solution)/shard_map/reduce_scatter | solution.py:249
  2088.0 42.5 %reduce-scatter.42.cloned.1.call-done = bf16[64,5632]{1,0:T(8,128)(2,1)} async-done(((bf16[256,5632]{1,0:T(8,128)(2,1)}), bf16[64,5632]{1,0:T(8,128)(2,1)}) %reduce-scatter.42.cloned.1.call-update) | async-done | bytes 720912 | tf_op jit(solution)/shard_map/reduce_scatter | solution.py:252
  2132.8 35.8 %reduce-scatter.38.cloned.1.call-done = bf16[128,2048]{1,0:T(8,128)(2,1)} async-done(((bf16[512,2048]{1,0:T(8,128)(2,1)}), bf16[128,2048]{1,0:T(8,128)(2,1)}) %reduce-scatter.38.cloned.1.call-update) | async-done | bytes 524304 | tf_op jit(solution)/shard_map/reduce_scatter | solution.py:395
  (489 shorter events, 345.8 us)
Async XLA Ops:
  7.2 48.7 %copy-start.57 = (u32[32]{0:T(128)S(1)}, u32[32]{0:T(128)}, u32[]{:S(2)}) copy-start(u32[32]{0:T(128)} %constant.115) | copy-start | bytes 388
  7.2 48.6 %copy-start.58 = (s32[200]{0:T(256)S(1)}, s32[200]{0:T(256)}, u32[]{:S(2)}) copy-start(s32[200]{0:T(256)} %param.24) | copy-start | bytes 2404
  7.2 64.8 %copy-start = (s32[1,20]{1,0:T(1,128)S(1)}, s32[1,20]{1,0:T(1,128)}, u32[]{:S(2)}) copy-start(s32[1,20]{1,0:T(1,128)} %param.25) | copy-start | bytes 244
  7.2 83.8 %all-gather.12.cloned.1.call-start = ((), (), s32[]{:S(2)}) async-start(), calls=%async_computation.17 | async-start | bytes 1081344 | tf_op jit(solution)/shard_map/all_gather | solution.py:128
  8.0 115.6 %all-gather.18.cloned.1.call-start = ((), (), s32[]{:S(2)}) async-start(), calls=%async_computation.20 | async-start | bytes 1081344 | tf_op jit(solution)/shard_map/all_gather | solution.py:129
  8.7 179.4 %all-gather.14.cloned.1.call-start = ((), (), s32[]{:S(2)}) async-start(), calls=%async_computation.18 | async-start | bytes 4325376 | tf_op jit(solution)/shard_map/all_gather | solution.py:125
  9.5 257.5 %all-gather.16.cloned.1.call-start = ((), (), s32[]{:S(2)}) async-start(), calls=%async_computation.19 | async-start | bytes 8650752 | tf_op jit(solution)/shard_map/all_gather | solution.py:127
  10.0 382.4 %all-gather.20.cloned.1.call-start = ((), (), s32[]{:S(2)}) async-start(), calls=%async_computation.21 | async-start | bytes 17301504 | tf_op jit(solution)/shard_map/all_gather | solution.py:130
  10.6 518.2 %all-gather.22.cloned.1.call-start = ((), (), s32[]{:S(2)}) async-start(), calls=%async_computation.22 | async-start | bytes 23789568 | tf_op jit(solution)/shard_map/all_gather | solution.py:210
  11.2 663.3 %all-gather.24.cloned.1.call-start = ((), (), s32[]{:S(2)}) async-start(), calls=%async_computation.23 | async-start | bytes 23789568 | tf_op jit(solution)/shard_map/all_gather | solution.py:211
  12.0 808.3 %all-gather.26.cloned.1.call-start = ((), (), s32[]{:S(2)}) async-start(), calls=%async_computation.24 | async-start | bytes 23789568 | tf_op jit(solution)/shard_map/all_gather | solution.py:212
  12.7 1016.1 %reduce-scatter.16.cloned.1.call-start = ((), (), s32[]{:S(2)}) async-start(), calls=%async_computation.25 | async-start | bytes 921600 | tf_op jit(solution)/shard_map/reduce_scatter | solution.py:311
  55.8 34.9 %copy-start.44 = (f32[2048]{0:T(1024)}, f32[2048]{0:T(1024)S(1)}, u32[]{:S(2)}) copy-start(f32[2048]{0:T(1024)S(1)} %convert_element_type.239) | copy-start | bytes 24580
  55.8 135.6 %copy-start.46 = (f32[1024]{0:T(1024)}, f32[1024]{0:T(1024)S(1)}, u32[]{:S(2)}) copy-start(f32[1024]{0:T(1024)S(1)} %convert_element_type.242) | copy-start | bytes 12292
  90.1 35.0 %copy-start.55 = (f32[128]{0:T(128)}, f32[128]{0:T(128)S(1)}, u32[]{:S(2)}) copy-start(f32[128]{0:T(128)S(1)} %multiply_power_fusion) | copy-start | bytes 1540
  90.4 34.8 %copy-start.48 = (f32[200]{0:T(256)}, f32[200]{0:T(256)S(1)}, u32[]{:S(2)}) copy-start(f32[200]{0:T(256)S(1)} %add_rsqrt_fusion.2) | copy-start | bytes 2404
  90.7 34.5 %copy-start.50 = (f32[200]{0:T(256)}, f32[200]{0:T(256)S(1)}, u32[]{:S(2)}) copy-start(f32[200]{0:T(256)S(1)} %fusion.81) | copy-start | bytes 2404
  91.0 97.1 %copy-start.14 = (bf16[200,2048]{1,0:T(8,128)(2,1)}, bf16[200,2048]{1,0:T(8,128)(2,1)S(1)}, u32[]{:S(2)}) copy-start(bf16[200,2048]{1,0:T(8,128)(2,1)S(1)} %fusion.47) | copy-start | bytes 2457604
  93.4 180.1 %copy-start.31 = (f32[200,128]{1,0:T(8,128)}, f32[200,128]{1,0:T(8,128)S(1)}, u32[]{:S(2)}) copy-start(f32[200,128]{1,0:T(8,128)S(1)} %get-tuple-element.447) | copy-start | bytes 307204
  93.4 180.1 %copy-start.33 = (f32[200,128]{1,0:T(8,128)}, f32[200,128]{1,0:T(8,128)S(1)}, u32[]{:S(2)}) copy-start(f32[200,128]{1,0:T(8,128)S(1)} %get-tuple-element.448) | copy-start | bytes 307204
  191.4 80.8 %copy-start.52 = (f32[200]{0:T(256)}, f32[200]{0:T(256)S(1)}, u32[]{:S(2)}) copy-start(f32[200]{0:T(256)S(1)} %add_rsqrt_fusion.1) | copy-start | bytes 2404
  192.4 79.8 %copy-start.17 = (bf16[200,1024]{1,0:T(8,128)(2,1)}, bf16[200,1024]{1,0:T(8,128)(2,1)S(1)}, u32[]{:S(2)}) copy-start(bf16[200,1024]{1,0:T(8,128)(2,1)S(1)} %multiply_convert_fusion.5) | copy-start | bytes 1228804
  401.0 462.4 %copy-start.15 = (f32[200,2048]{1,0:T(8,128)}, f32[200,2048]{1,0:T(8,128)S(1)}, u32[]{:S(2)}) copy-start(f32[200,2048]{1,0:T(8,128)S(1)} %get-tuple-element.456) | copy-start | bytes 4915204
  401.3 273.3 %copy-start.21 = (bf16[200,2048]{1,0:T(8,128)(2,1)}, bf16[200,2048]{1,0:T(8,128)(2,1)S(1)}, u32[]{:S(2)}) copy-start(bf16[200,2048]{1,0:T(8,128)(2,1)S(1)} %multiply_convert_fusion.3) | copy-start | bytes 2457604
  541.1 279.1 %copy-start.25 = (bf16[200,2048]{1,0:T(8,128)(2,1)S(1)}, bf16[200,2048]{1,0:T(8,128)(2,1)}, u32[]{:S(2)}) copy-start(bf16[200,2048]{1,0:T(8,128)(2,1)} %param.37) | copy-start | bytes 2457604
  998.8 62.8 %reduce-scatter.18.cloned.1.call-start = ((), (), s32[]{:S(2)}) async-start(), calls=%async_computation.26 | async-start | bytes 921600 | tf_op jit(solution)/shard_map/reduce_scatter | solution.py:317
  999.4 122.8 %reduce-scatter.28.cloned.1.call-start = ((), (), s32[]{:S(2)}) async-start(), calls=%async_computation.31 | async-start | bytes 1179648 | tf_op jit(solution)/shard_map/reduce_scatter | solution.py:363
  1030.8 33.8 %copy-start.4 = (f32[200,16,256]{2,1,0:T(8,128)S(1)}, f32[200,16,256]{2,1,0:T(8,128)}, u32[]{:S(2)}) copy-start(f32[200,16,256]{2,1,0:T(8,128)} %get-tuple-element.173) | copy-start | bytes 9830404
  1030.8 33.8 %copy-start.32 = (f32[200,128]{1,0:T(8,128)S(1)}, f32[200,128]{1,0:T(8,128)}, u32[]{:S(2)}) copy-start(f32[200,128]{1,0:T(8,128)} %copy-done.31) | copy-start | bytes 307204
  1030.9 33.8 %copy-start.34 = (f32[200,128]{1,0:T(8,128)S(1)}, f32[200,128]{1,0:T(8,128)}, u32[]{:S(2)}) copy-start(f32[200,128]{1,0:T(8,128)} %copy-done.33) | copy-start | bytes 307204
  1033.6 94.7 %reduce-scatter.32.cloned.1.call-start = ((), (), s32[]{:S(2)}) async-start(), calls=%async_computation.33 | async-start | bytes 1179648 | tf_op jit(solution)/shard_map/reduce_scatter | solution.py:366
  1064.2 151.1 %reduce-scatter.20.cloned.1.call-start = ((), (), s32[]{:S(2)}) async-start(), calls=%async_computation.27 | async-start | bytes 4718592 | tf_op jit(solution)/shard_map/reduce_scatter | solution.py:354
  1077.3 210.4 %all-gather.32.cloned.1.call-start = ((), (), s32[]{:S(2)}) async-start(), calls=%async_computation.41 | async-start | bytes 7372800 | tf_op jit(solution)/shard_map/all_gather | solution.py:239
  1077.9 313.4 %reduce-scatter.24.cloned.1.call-start = ((), (), s32[]{:S(2)}) async-start(), calls=%async_computation.29 | async-start | bytes 9437184 | tf_op jit(solution)/shard_map/reduce_scatter | solution.py:360
  1084.3 471.6 %all-gather.28.cloned.1.call-start = ((), (), s32[]{:S(2)}) async-start(), calls=%async_computation.37 | async-start | bytes 20275200 | tf_op jit(solution)/shard_map/all_gather | solution.py:237
  1084.9 632.1 %all-gather.30.cloned.1.call-start = ((), (), s32[]{:S(2)}) async-start(), calls=%async_computation.39 | async-start | bytes 20275200 | tf_op jit(solution)/shard_map/all_gather | solution.py:238
  1085.5 800.2 %reduce-scatter.36.cloned.1.call-start = ((), (), s32[]{:S(2)}) async-start(), calls=%async_computation.35 | async-start | bytes 18874368 | tf_op jit(solution)/shard_map/reduce_scatter | solution.py:369
  1117.7 170.0 %all-to-all-start.1 = ((bf16[200,8,704]{2,0,1:T(8,128)(2,1)}), bf16[200,8,704]{2,0,1:T(8,128)(2,1)}, u32[]{:S(2)}, u32[]{:S(2)}) async-start(bf16[200,8,704]{2,0,1:T(8,128)(2,1)} %copy.92), calls=%async_computation.15 | async-start | bytes 4915200 | tf_op jit(solution)/shard_map/all_to_all | solution.py:243
  1122.1 822.4 %reduce-scatter.30.cloned.1.call-start = ((), (), s32[]{:S(2)}) async-start(), calls=%async_computation.32 | async-start | bytes 163840 | tf_op jit(solution)/shard_map/reduce_scatter | solution.py:389
  1122.9 823.0 %reduce-scatter.34.cloned.1.call-start = ((), (), s32[]{:S(2)}) async-start(), calls=%async_computation.34 | async-start | bytes 163840 | tf_op jit(solution)/shard_map/reduce_scatter | solution.py:392
  1128.3 836.6 %reduce-scatter.22.cloned.1.call-start = ((), (), s32[]{:S(2)}) async-start(), calls=%async_computation.28 | async-start | bytes 655360 | tf_op jit(solution)/shard_map/reduce_scatter | solution.py:380
  1215.4 794.8 %reduce-scatter.44.cloned.1.call-start = ((), (), s32[]{:S(2)}) async-start(), calls=%async_computation.42 | async-start | bytes 3604480 | tf_op jit(solution)/shard_map/reduce_scatter | solution.py:255
  1302.1 89.2 %all-to-all-start = ((bf16[200,8,256]{2,0,1:T(8,128)(2,1)}), bf16[200,8,256]{2,0,1:T(8,128)(2,1)S(1)}, u32[]{:S(2)}, u32[]{:S(2)}) async-start(bf16[200,8,256]{2,0,1:T(8,128)(2,1)} %copy.90), calls=%async_computation.12 | async-start | bytes 1638400 | tf_op jit(solution)/shard_map/all_to_all | solution.py:242
  1305.7 735.3 %reduce-scatter.26.cloned.1.call-start = ((), (), s32[]{:S(2)}) async-start(), calls=%async_computation.30 | async-start | bytes 1310720 | tf_op jit(solution)/shard_map/reduce_scatter | solution.py:386
  1391.3 694.4 %reduce-scatter.40.cloned.1.call-start = ((), (), s32[]{:S(2)}) async-start(), calls=%async_computation.38 | async-start | bytes 3604480 | tf_op jit(solution)/shard_map/reduce_scatter | solution.py:249
  1569.1 561.5 %reduce-scatter.42.cloned.1.call-start = ((), (), s32[]{:S(2)}) async-start(), calls=%async_computation.40 | async-start | bytes 3604480 | tf_op jit(solution)/shard_map/reduce_scatter | solution.py:252
  1729.9 155.8 %copy-start.30 = (bf16[200,1024]{1,0:T(8,128)(2,1)S(1)}, bf16[200,1024]{1,0:T(8,128)(2,1)}, u32[]{:S(2)}) copy-start(bf16[200,1024]{1,0:T(8,128)(2,1)} %copy-done.29) | copy-start | bytes 1228804
  1730.0 438.6 %reduce-scatter.38.cloned.1.call-start = ((), (), s32[]{:S(2)}) async-start(), calls=%async_computation.36 | async-start | bytes 2621440 | tf_op jit(solution)/shard_map/reduce_scatter | solution.py:395
  (70 other events, 291.3 us)
Sparse Core Ops, SparseCore 0:
  11.1 56.6 all-gather.11
  70.8 52.7 all-gather.17
  126.6 61.4 all-gather.13
  190.9 75.9 all-gather.15
  269.8 113.4 all-gather.19
  386.0 142.7 all-gather.21
  531.7 142.7 all-gather.23
  677.4 142.7 all-gather.25
  998.9 29.8 reduce-scatter.15
  1031.6 29.8 reduce-scatter.17
  1064.4 30.3 reduce-scatter.27
  1097.5 30.7 reduce-scatter.31
  1130.6 84.6 reduce-scatter.19
  1216.8 70.8 all-gather.31
  1289.9 101.3 reduce-scatter.23
  1392.8 163.1 all-gather.27
  1557.4 159.4 all-gather.29
  1719.2 166.4 reduce-scatter.35
  1888.4 22.1 reduce-scatter.29
  1913.4 23.8 reduce-scatter.33
  1940.2 24.7 reduce-scatter.21
  1968.3 41.7 reduce-scatter.43
  2013.3 27.7 reduce-scatter.25
  2043.9 41.7 reduce-scatter.39
  2088.7 41.7 reduce-scatter.41
  2133.3 35.1 reduce-scatter.37
where the time goes:
time: 2190 us; the launch traced here: 2180 us
  waiting for transfers between devices  1510 us (69%)
  matrix products  331 us (15%)
  local copies, waits for them, and re-layouts  136 us (6%)
  blocking collectives  128 us (6%)
  other arithmetic  48.5 us (2%)
    all_gather x1, waiting for transfers between devices, body(): lax.all_gather(gate_grad, 'fsdp', axis=0, tiled=True)  165 us
    reduce_scatter x1, waiting for transfers between devices, body(): lax.psum_scatter(out_w_grad.astype(jnp.bfloat16), 'fsdp', scatter_dimensi...  152 us
    all_gather x1, waiting for transfers between devices, body(): lax.all_gather(up_grad, 'fsdp', axis=0, tiled=True)  148 us
    all_gather x1, waiting for transfers between devices, body(): lax.all_gather(w_up, ('dp', 'fsdp'), axis=0, tiled=True)  133 us
    all_gather x1, waiting for transfers between devices, body(): lax.all_gather(w_gate, ('dp', 'fsdp'), axis=0, tiled=True)  128 us
    all_gather x1, waiting for transfers between devices, body(): lax.all_gather(w_down, ('dp', 'fsdp'), axis=0, tiled=True)  124 us
    unnamed x4, blocking collectives  92.5 us
    reduce_scatter x1, waiting for transfers between devices, body(): lax.psum_scatter(qdown_w_grad.astype(jnp.bfloat16), 'fsdp', scatter_dimen...  87 us
  transfers between devices with their start and end apart: 28, of which 21 were waited for; matrix products, arithmetic and copies ran while one was open for 15% of the time, Pallas kernels for 0%

commit v1 on v0

v1 whole, which is shorter than its diff:
```python
import functools

import jax
import jax.numpy as jnp
from jax import lax
from jax.experimental import pallas as pl
from jax.experimental.pallas import tpu as pltpu
from jax.sharding import PartitionSpec as P

H = 16
HD = 256
NSEG = 20

EPSILON = 1e-06
ROPE_BASE = 10000.0
HIGHEST = lax.Precision.HIGHEST
NEGATIVE = -1e30
BF = jnp.bfloat16
F32 = jnp.float32
CHUNK = 160
TREE = ("q", "r", "c")
LINE = ("q", "r")
SHARE = ("r", "c")
VMEM_LIMIT = 48 * 1024 * 1024


def dot32(a, b):
    return jnp.dot(a, b, preferred_element_type=F32)


def dot_nt(a, b):
    return lax.dot_general(a, b, (((1,), (1,)), ((), ())), preferred_element_type=F32)


def dot_tn(a, b):
    return lax.dot_general(a, b, (((0,), (0,)), ((), ())), preferred_element_type=F32)


def rms_scale(values):
    return lax.rsqrt(jnp.mean(values * values, axis=-1, keepdims=True) + EPSILON)


def norm_back(upstream, normed, row_scale, gain_vec):
    scaled = upstream * gain_vec
    inner_mean = jnp.mean(scaled * normed, axis=-1, keepdims=True)
    return (row_scale * (scaled - normed * inner_mean), jnp.sum(upstream * normed, axis=0))


def rotate(values, cosines, sines):
    half = values.shape[-1] // 2
    a, b = values[..., :half], values[..., half:]
    return jnp.concatenate([a * cosines - b * sines, b * cosines + a * sines], axis=-1)


def tile_plan(tile, chunks_per_tile):
    count = jnp.where(tile == 4, 4, tile + 1) * chunks_per_tile
    return count


def chunk_start(tile, j, chunks_per_tile):
    jump = jnp.where((tile == 4) & (j >= 3 * chunks_per_tile), chunks_per_tile, 0)
    return (j + jump) * CHUNK


def seen(k0, bits_row, tile_rows, q0, heads, seg_len):
    shape = (CHUNK, heads * tile_rows)
    key_pos = lax.broadcasted_iota(jnp.int32, (CHUNK, 1), 0) + k0
    key_bit = jnp.left_shift(jnp.int32(1), key_pos // seg_len)
    lane = lax.broadcasted_iota(jnp.int32, (1, heads * tile_rows), 1)
    q_pos = q0 + lax.rem(lane, tile_rows)
    reach = jnp.broadcast_to(key_bit, shape) & jnp.broadcast_to(bits_row, shape)
    return (reach != 0) & (jnp.broadcast_to(key_pos, shape) <= jnp.broadcast_to(q_pos, shape))


def attn_fwd_kernel(heads, seg_len, bits_ref, q_ref, k_ref, v_ref, att_ref, lse_ref, qs, st):
    tile_rows = 4 * seg_len
    width = heads * tile_rows
    per_tile = tile_rows // CHUNK
    scale = HD ** (-0.5)

    def one_tile(tile, carry):
        q0 = pl.multiple_of(tile * tile_rows, tile_rows)
        for h in range(heads):
            qs[h * tile_rows : (h + 1) * tile_rows, :] = q_ref[pl.ds(q0, tile_rows), h * HD : (h + 1) * HD]
        bits_row = bits_ref[tile]
        n_chunks = tile_plan(tile, per_tile)

        def score(j, top):
            k0 = pl.multiple_of(chunk_start(tile, j, per_tile), CHUNK)
            s = dot_nt(k_ref[pl.ds(k0, CHUNK), :], qs[...]) * scale
            s = jnp.where(seen(k0, bits_row, tile_rows, q0, heads, seg_len), s, NEGATIVE)
            st[pl.ds(pl.multiple_of(j * CHUNK, CHUNK), CHUNK), :] = s
            return jnp.maximum(top, jnp.max(s, axis=0, keepdims=True))

        top = lax.fori_loop(0, n_chunks, score, jnp.full((1, width), NEGATIVE, F32))

        def expo(j, total):
            at = pl.ds(pl.multiple_of(j * CHUNK, CHUNK), CHUNK)
            p = jnp.exp(st[at, :] - top)
            st[at, :] = p
            return total + jnp.sum(p, axis=0, keepdims=True)

        total = lax.fori_loop(0, n_chunks, expo, jnp.zeros((1, width), F32))
        inv = 1.0 / total
        lse_ref[tile] = top + jnp.log(total)

        def gather(j, acc):
            k0 = pl.multiple_of(chunk_start(tile, j, per_tile), CHUNK)
            at = pl.ds(pl.multiple_of(j * CHUNK, CHUNK), CHUNK)
            probs = (st[at, :] * inv).astype(BF)
            return acc + dot_tn(v_ref[pl.ds(k0, CHUNK), :], probs)

        out = lax.fori_loop(0, n_chunks, gather, jnp.zeros((HD, width), F32))
        out = out.T.astype(BF)
        for h in range(heads):
            att_ref[pl.ds(q0, tile_rows), h * HD : (h + 1) * HD] = out[h * tile_rows : (h + 1) * tile_rows, :]
        return carry

    lax.fori_loop(0, 5, one_tile, 0)


def attn_bwd_kernel(
    heads, seg_len, bits_ref, lse_ref, cos_ref, sin_ref, q_ref, k_ref, v_ref, da_ref, dq_ref, dk_ref, dv_ref, qs, das, pt, dpt, dk, dv
):
    tile_rows = 4 * seg_len
    width = heads * tile_rows
    per_tile = tile_rows // CHUNK
    scale = HD ** (-0.5)
    dk[...] = jnp.zeros_like(dk)
    dv[...] = jnp.zeros_like(dv)

    def one_tile(tile, carry):
        q0 = pl.multiple_of(tile * tile_rows, tile_rows)
        for h in range(heads):
            rows = slice(h * tile_rows, (h + 1) * tile_rows)
            cols = slice(h * HD, (h + 1) * HD)
            qs[rows, :] = q_ref[pl.ds(q0, tile_rows), cols]
            das[rows, :] = da_ref[pl.ds(q0, tile_rows), cols]
        bits_row = bits_ref[tile]
        lse_row = lse_ref[tile]
        n_chunks = tile_plan(tile, per_tile)

        def first(j, delta):
            k0 = pl.multiple_of(chunk_start(tile, j, per_tile), CHUNK)
            at = pl.ds(pl.multiple_of(j * CHUNK, CHUNK), CHUNK)
            s = dot_nt(k_ref[pl.ds(k0, CHUNK), :], qs[...]) * scale
            p = jnp.where(seen(k0, bits_row, tile_rows, q0, heads, seg_len), jnp.exp(s - lse_row), 0.0)
            low = p.astype(BF)
            dp = dot_nt(v_ref[pl.ds(k0, CHUNK), :], das[...])
            pt[at, :] = p
            dpt[at, :] = dp
            dv[pl.ds(k0, CHUNK), :] += dot32(low, das[...])
            return delta + jnp.sum(low.astype(F32) * dp, axis=0, keepdims=True)

        delta = lax.fori_loop(0, n_chunks, first, jnp.zeros((1, width), F32))

        def second(j, acc):
            k0 = pl.multiple_of(chunk_start(tile, j, per_tile), CHUNK)
            at = pl.ds(pl.multiple_of(j * CHUNK, CHUNK), CHUNK)
            ds = (pt[at, :] * (dpt[at, :] - delta)).astype(BF)
            dk[pl.ds(k0, CHUNK), :] += dot32(ds, qs[...])
            return acc + dot_tn(k_ref[pl.ds(k0, CHUNK), :], ds)

        acc = lax.fori_loop(0, n_chunks, second, jnp.zeros((HD, width), F32))
        out = (acc * scale).T
        at = pl.ds(q0, tile_rows)
        for h in range(heads):
            grad = out[h * tile_rows : (h + 1) * tile_rows, :]
            dq_ref[at, h * HD : (h + 1) * HD] = rotate(grad, cos_ref[at, :], -sin_ref[at, :]).astype(BF)
        return carry

    lax.fori_loop(0, 5, one_tile, 0)
    dk_ref[...] = (dk[...] * scale).astype(BF)
    dv_ref[...] = dv[...].astype(BF)


def attention(bits, q, k, v, heads, seg_len):
    tree_len = q.shape[0]
    width = heads * 4 * seg_len
    work = heads * tree_len * tree_len // 2
    return pl.pallas_call(
        functools.partial(attn_fwd_kernel, heads, seg_len),
        out_shape=(
            jax.ShapeDtypeStruct((tree_len, heads * HD), BF),
            jax.ShapeDtypeStruct((5, 1, width), F32),
        ),
        in_specs=[pl.BlockSpec(memory_space=pltpu.VMEM)] * 4,
        out_specs=(pl.BlockSpec(memory_space=pltpu.VMEM),) * 2,
        scratch_shapes=[pltpu.VMEM((width, HD), BF), pltpu.VMEM((16 * seg_len, width), F32)],
        compiler_params=pltpu.CompilerParams(vmem_limit_bytes=VMEM_LIMIT),
        cost_estimate=pl.CostEstimate(flops=4 * HD * work, bytes_accessed=6 * tree_len * HD * 2, transcendentals=work),
        name="attn_fwd",
    )(bits, q, k, v)


def attention_back(bits, lse, cosines, sines, q, k, v, da, heads, seg_len):
    tree_len = q.shape[0]
    width = heads * 4 * seg_len
    work = heads * tree_len * tree_len // 2
    return pl.pallas_call(
        functools.partial(attn_bwd_kernel, heads, seg_len),
        out_shape=(
            jax.ShapeDtypeStruct((tree_len, heads * HD), BF),
            jax.ShapeDtypeStruct((tree_len, HD), BF),
            jax.ShapeDtypeStruct((tree_len, HD), BF),
        ),
        in_specs=[pl.BlockSpec(memory_space=pltpu.VMEM)] * 8,
        out_specs=(pl.BlockSpec(memory_space=pltpu.VMEM),) * 3,
        scratch_shapes=[
            pltpu.VMEM((width, HD), BF),
            pltpu.VMEM((width, HD), BF),
            pltpu.VMEM((16 * seg_len, width), F32),
            pltpu.VMEM((16 * seg_len, width), F32),
            pltpu.VMEM((tree_len, HD), F32),
            pltpu.VMEM((tree_len, HD), F32),
        ],
        compiler_params=pltpu.CompilerParams(vmem_limit_bytes=VMEM_LIMIT),
        cost_estimate=pl.CostEstimate(flops=10 * HD * work, bytes_accessed=12 * tree_len * HD * 2, transcendentals=work),
        name="attn_bwd",
    )(bits, lse, cosines, sines, q, k, v, da)


def body(
    hidden_in,
    segment_ids,
    parents,
    norm_gain,
    w_qdown,
    q_gain,
    w_qup,
    w_key,
    w_value,
    w_out,
    ffn_gain,
    w_gate,
    w_up,
    w_down,
    cotangent,
):
    rows, model = hidden_in.shape
    dn, cn = lax.axis_size("dp"), lax.axis_size("c")
    zn, sn = lax.axis_size(LINE), lax.axis_size(SHARE)
    fn = lax.axis_size(TREE)
    heads = H // fn
    latent_width = w_qdown.shape[1]
    in_width = latent_width + 2 * HD
    per_row, per_latent = norm_gain.shape[0], q_gain.shape[0]
    d_at, c_at, f_at = lax.axis_index("dp"), lax.axis_index("c"), lax.axis_index(TREE)
    tree_len = rows * fn
    seg_len = tree_len // NSEG

    def exchange(parts, axes):
        return lax.all_to_all(parts, axes, split_axis=0, concat_axis=0, tiled=True)

    def spread(block, axes):
        return exchange(jnp.broadcast_to(block[None], (lax.axis_size(axes),) + block.shape), axes)

    def total(parts, axes):
        return jnp.sum(exchange(parts.astype(BF), axes).astype(F32), axis=0)

    def other_core(a):
        return lax.ppermute(a, "c", [(c, (c + 1) % cn) for c in range(cn)])

    def by_core(mine, axis):
        came = other_core(mine)
        return jnp.stack([jnp.where(c_at == 0, mine, came), jnp.where(c_at == 0, came, mine)], axis=axis)

    def at_index(a, index, axis=0):
        return lax.dynamic_index_in_dim(a, index, axis, keepdims=False)

    def after(a, *before):
        return lax.optimization_barrier((a,) + before)[0]

    def own_rows(a):
        return lax.dynamic_slice_in_dim(a, f_at * rows, rows, 0)

    def tree_gather(block):
        return lax.all_gather(block, TREE, axis=0, tiled=True)

    def tree_scatter(parts):
        return lax.psum_scatter(parts, TREE, scatter_dimension=0, tiled=True).astype(F32)

    def over_dp(a, m):
        return lax.ppermute(a, "dp", [(d, d ^ m) for d in range(dn)])

    def spread_dp(block):
        out = jnp.zeros((dn,) + block.shape, block.dtype)
        for m in range(dn):
            got = over_dp(block, m) if m else block
            out = lax.dynamic_update_index_in_dim(out, got, d_at ^ m, 0)
        return out

    tags = -(-rows // per_row)
    extra = jnp.concatenate(
        [
            norm_gain[:, None],
            ffn_gain[:, None],
            jnp.pad(q_gain, (0, per_row - per_latent))[:, None],
            jnp.pad(segment_ids.astype(BF), (0, tags * per_row - rows)).reshape(tags, per_row).T,
            jnp.zeros((per_row, 125 - tags), BF),
        ],
        axis=1,
    )
    x_all = tree_gather(hidden_in)
    in_block = jnp.concatenate([w_qdown, w_key, w_value, extra], axis=1)
    in_mine = spread(spread(in_block, LINE), "dp")
    in_full = by_core(in_mine, 2).reshape(model, in_width + 128)
    w_in = in_full[:, :in_width]
    extra = in_full[:, in_width:].T.astype(F32)
    gain_one, gain_two = extra[0], extra[1]
    gain_latent = extra[2].reshape(dn * fn, per_row)[:, :per_latent].reshape(latent_width)
    run_labels = lax.dynamic_slice_in_dim(extra[3 : 3 + tags].reshape(tags, dn, fn, per_row), d_at, 1, 1)[:, 0]
    run_labels = jnp.swapaxes(run_labels, 0, 1).reshape(fn, tags * per_row)[:, :rows]
    run_labels = run_labels.reshape(tree_len)[::seg_len].astype(jnp.int32)

    qup_rows, out_rows = w_qup.shape[0], w_out.shape[0]
    qn = fn // sn
    qup_cols = jnp.transpose(w_qup.reshape(qup_rows, sn, heads, qn, HD), (3, 1, 0, 2, 4))
    qup_cols = exchange(after(qup_cols.reshape(fn, qup_rows, heads * HD), in_mine), TREE)
    qup_cols = spread_dp(qup_cols).reshape(latent_width, heads * HD)
    out_cols = exchange(spread_dp(after(w_out, in_mine)).reshape(sn, heads, out_rows, model), SHARE)
    out_cols = jnp.swapaxes(out_cols, 0, 1).reshape(heads * HD, model)
    cot = tree_gather(after(cotangent, x_all))

    labels = jnp.arange(NSEG, dtype=jnp.int32)
    reach = jnp.maximum(
        (labels[:, None] == labels[None, :]).astype(F32), (parents[0][:, None] == labels[None, :]).astype(F32)
    )
    for _ in range(5):
        reach = jnp.minimum(jnp.dot(reach, reach, precision=HIGHEST), 1.0)
    pick_run = (run_labels[:, None] == labels[None, :]).astype(F32)
    run_reach = jnp.dot(jnp.dot(pick_run, reach, precision=HIGHEST), pick_run.T, precision=HIGHEST)
    run_depth = jnp.sum(run_reach, axis=1) - 1.0
    run_bits = jnp.sum(jnp.where(run_reach > 0.5, jnp.left_shift(1, labels)[None, :], 0), axis=1).astype(jnp.int32)
    bits = jnp.broadcast_to(run_bits.reshape(5, 1, 4, 1), (5, heads, 4, seg_len)).reshape(5, 1, heads * 4 * seg_len)
    inverse = ROPE_BASE ** (-(jnp.arange(HD // 2, dtype=F32) * 2.0) / HD)
    coarse = (run_depth * seg_len)[:, None] * inverse[None, :]
    fine = jnp.arange(seg_len, dtype=F32)[:, None] * inverse[None, :]
    cos_a, sin_a = jnp.cos(coarse)[:, None, :], jnp.sin(coarse)[:, None, :]
    cos_b, sin_b = jnp.cos(fine)[None, :, :], jnp.sin(fine)[None, :, :]
    cosines = (cos_a * cos_b - sin_a * sin_b).reshape(tree_len, HD // 2)
    sines = (sin_a * cos_b + cos_a * sin_b).reshape(tree_len, HD // 2)

    unit_rows = w_down.shape[0]
    units = dn * unit_rows

    def unit_columns(weight):
        return jnp.transpose(weight.reshape(per_row, dn, fn, unit_rows), (2, 0, 1, 3)).reshape(fn, 1, per_row, units)

    unit_cols = jnp.concatenate([unit_columns(w_gate), unit_columns(w_up)], axis=1)
    unit_cols = exchange(after(unit_cols, x_all, qup_cols), TREE)

    x_wide = x_all.astype(F32)
    normed_all = (x_wide * rms_scale(x_wide) * gain_one).astype(BF)
    mixed_in = dot32(normed_all, w_in)
    latent_all = mixed_in[:, :latent_width]
    latent_in = (latent_all * rms_scale(latent_all) * gain_latent).astype(BF)
    key_all = rotate(mixed_in[:, latent_width : latent_width + HD], cosines, sines).astype(BF)
    value_all = mixed_in[:, latent_width + HD :].astype(BF)
    query_wide = dot32(latent_in, qup_cols)
    query_all = jnp.concatenate(
        [rotate(query_wide[:, h * HD : (h + 1) * HD], cosines, sines).astype(BF) for h in range(heads)], axis=1
    )
    attended, lse = attention(bits, query_all, key_all, value_all, heads, seg_len)
    x = hidden_in.astype(F32)
    out_part = dot32(after(attended, unit_cols, cot), out_cols).astype(BF)
    unit_cols = spread(after(unit_cols, out_part), "dp")
    mixed = x + after(tree_scatter(out_part), unit_cols)
    gate_cols = unit_cols[:, :, 0].reshape(model, units)
    up_cols = unit_cols[:, :, 1].reshape(model, units)

    scale_two = rms_scale(mixed)
    normed_two = mixed * scale_two
    normed_mid = (normed_two * gain_two).astype(BF)
    down_rows = spread(after(w_down, normed_mid), "dp").reshape(units, model)
    mid = after(tree_gather(normed_mid), down_rows, gate_cols, up_cols)
    gate = dot32(mid, gate_cols)
    up = dot32(mid, up_cols)
    sig = jax.nn.sigmoid(gate)
    activated = (gate * sig * up).astype(BF)
    act_grad = dot_nt(cot, down_rows)
    gate_grad = (act_grad * up * sig * (1.0 + gate * (1.0 - sig))).astype(BF)
    up_grad = (act_grad * gate * sig).astype(BF)
    mid_part = (dot_nt(gate_grad, gate_cols) + dot_nt(up_grad, up_cols)).astype(BF)
    down_parts = dot_tn(after(activated, mid_part), cot).astype(BF).reshape(dn, unit_rows, model)
    grad_down = total(down_parts, "dp")
    mid_late = after(mid, mid_part)
    unit_parts = jnp.stack(
        [dot_tn(mid_late, gate_grad).astype(BF).reshape(dn, fn * per_row, units),
         dot_tn(mid_late, up_grad).astype(BF).reshape(dn, fn * per_row, units)], axis=1
    )
    mid_grad = after(tree_scatter(mid_part), unit_parts, grad_down)
    mixed_back, gain_two_part = norm_back(mid_grad, normed_two, scale_two, gain_two)
    mixed_grad = cotangent.astype(F32) + mixed_back
    branch_grad = mixed_grad.astype(BF)

    unit_own = total(after(unit_parts, branch_grad), "dp").astype(BF).reshape(2, fn, per_row, units)
    branch = after(tree_gather(branch_grad), unit_own)
    unit_own = exchange(after(jnp.swapaxes(unit_own, 0, 1), branch), TREE).reshape(fn, 2, per_row, dn, unit_rows)
    attended_grad = dot_nt(branch, out_cols).astype(BF)
    query_grad, key_part, value_part = attention_back(
        bits, lse, cosines, sines, query_all, key_all, value_all, attended_grad, heads, seg_len
    )
    latent_part = dot_nt(query_grad, qup_cols).astype(BF)
    back_part = after(jnp.concatenate([latent_part, key_part, value_part], axis=1), unit_own)
    out_grads = jnp.swapaxes(
        dot_tn(attended, after(branch, back_part)).astype(BF).reshape(heads, sn, out_rows, model), 0, 1
    )
    grad_out = total(exchange(out_grads, SHARE).reshape(dn, out_rows, model), "dp")
    grad_qup = dot_tn(latent_in, after(query_grad, back_part))
    grad_qup = total(grad_qup.reshape(dn, fn * qup_rows, heads * HD), "dp").astype(BF)
    back = after(tree_scatter(back_part), grad_qup, grad_out)
    layer_part = dot32(after(activated, back_part), down_rows).astype(BF)
    layer_out = (mixed + tree_scatter(after(layer_part, back))).astype(BF)
    grad_qup = exchange(grad_qup.reshape(fn, qup_rows, heads * HD), TREE).reshape(qn, sn, qup_rows, heads, HD)
    grad_qup = jnp.transpose(grad_qup, (2, 1, 3, 0, 4)).reshape(qup_rows, H * HD).astype(F32)
    unit_own = jnp.transpose(unit_own, (1, 2, 3, 0, 4)).reshape(2, per_row, dn * fn * unit_rows).astype(F32)

    scale_one = rms_scale(x)
    normed_one = x * scale_one
    normed_in = (normed_one * gain_one).astype(BF)
    latent = own_rows(latent_all)
    scale_latent = rms_scale(latent)
    latent_back, gain_latent_part = norm_back(
        back[:, :latent_width], latent * scale_latent, scale_latent, gain_latent
    )
    key_grad = rotate(back[:, latent_width : latent_width + HD], own_rows(cosines), -own_rows(sines))
    in_grad = jnp.concatenate([latent_back, key_grad, back[:, latent_width + HD :]], axis=1).astype(BF)
    normed_grad = dot_nt(in_grad, w_in)
    input_back, gain_one_part = norm_back(normed_grad, normed_one, scale_one, gain_one)
    grad_in = (mixed_grad + input_back).astype(BF)

    def per_core(a, core):
        return at_index(a.reshape(a.shape[0], dn * zn, cn, per_row), core, 2).reshape(a.shape[0], dn * zn * per_row)

    def over_cores(sent, kept):
        return other_core(sent.astype(BF)).astype(F32) + kept

    in_own = over_cores(dot_tn(per_core(normed_in, 1 - c_at), in_grad), dot_tn(per_core(normed_in, c_at), in_grad))

    def per_device(a):
        return jnp.pad(a.reshape(dn * fn, -1), ((0, 0), (0, per_row - a.shape[0] // (dn * fn)))).reshape(1, model)

    gain_parts = jnp.concatenate([per_device(a) for a in (gain_one_part, gain_two_part, gain_latent_part)], axis=0)
    gain_parts = jnp.pad(gain_parts, ((0, 125), (0, 0)))
    gain_own = over_cores(per_core(gain_parts, 1 - c_at), per_core(gain_parts, c_at)).T
    in_own = jnp.concatenate([in_own, gain_own], axis=1).reshape(dn, zn, per_row, in_width + 128)
    in_sum = total(total(in_own, "dp"), LINE)
    return (
        layer_out,
        grad_in,
        in_sum[:, in_width],
        in_sum[:, :latent_width],
        in_sum[:per_latent, in_width + 2],
        grad_qup,
        in_sum[:, latent_width : latent_width + HD],
        in_sum[:, latent_width + HD : in_width],
        grad_out,
        in_sum[:, in_width + 1],
        unit_own[0],
        unit_own[1],
        grad_down,
    )


def solution(mesh):
    dn, fn = mesh.shape["dp"], mesh.shape["fsdp"]
    share = dn * fn // H
    fine = jax.sharding.Mesh(mesh.devices.reshape(dn, fn // share, share // 2, 2), ("dp",) + TREE)
    split = P(("dp",) + TREE, None)
    line = P(("dp",) + TREE)
    placed = (
        split, line, P("dp", None), line, split, line, split, split, split, split, line, split, split, split, split,
    )
    given = (split, split, line, split, line, split, split, split, split, line, split, split, split)
    return jax.shard_map(body, mesh=fine, in_specs=placed, out_specs=given, check_vma=False)
```

time: 2190 us -> 860 us (0.39)
  waiting for transfers between devices: 1510 us -> 171 us
  matrix products: 331 us -> 154 us
  blocking collectives: 128 us -> 187 us
  Pallas kernels: 0 us -> 54.2 us
  starting transfers between devices: 9.75 us -> 63.6 us
    all_gather x11 -> x4, waiting for transfers between devices: 901 us -> 26.8 us  [tree_gather(): return lax.all_gather(block, TREE, axis=0, tiled=True)]
    reduce_scatter x15 -> x4, waiting for transfers between devices: 596 us -> 73.9 us  [tree_scatter(): lax.psum_scatter(parts, TREE, scatter_dimension=0, tiled=True).astype(F32)]
    all_to_all x0 -> x5, blocking collectives: none -> 187 us  [exchange(): return lax.all_to_all(parts, axes, split_axis=0, concat_axis=0, tiled=True)]
    dot_general x59 -> x26, matrix products: 331 us -> 154 us  [the longest x6 55.4 us: dot32(): return jnp.dot(a, b, preferred_element_type=F32)]
    unnamed x4 -> x0, blocking collectives: 92.5 us -> none
    all_to_all x2 -> x11, waiting for transfers between devices: 0.01 us -> 68.3 us  [exchange(): return lax.all_to_all(parts, axes, split_axis=0, concat_axis=0, tiled=True)]
    pallas_call x0 -> x2, Pallas kernels: none -> 54.2 us  [the longest x1 31.9 us: attention_back(): pl.pallas_call(functools.partial(attn_bwd_kernel, heads, seg_len), out_sh...]
    convert_element_type x22 -> x5, local copies, waits for them, and re-layouts: 54 us -> 7.04 us  [the longest x3 6.49 us: body(): jnp.transpose(grad_qup, (2, 1, 3, 0, 4)).reshape(qup_rows, H * HD)]
  transfers between devices with their start and end apart: 28 -> 28, of which waited for: 21 -> 13; matrix products, arithmetic and copies ran while one was open for 15% -> 32% of each run, Pallas kernels for 0% -> 6%
where the time goes in v1:
time: 860 us; the launch traced here: 849 us
  blocking collectives  187 us (22%)
  waiting for transfers between devices  171 us (20%)
  matrix products  154 us (18%)
  local copies, waits for them, and re-layouts  136 us (16%)
  other arithmetic  67.3 us (8%)
  starting transfers between devices  63.6 us (7%)
  Pallas kernels  54.2 us (6%)
  between operations  15.4 us (2%)
    all_to_all x5, blocking collectives, exchange(): return lax.all_to_all(parts, axes, split_axis=0, concat_axis=0, tiled=True)  187 us
    reduce_scatter x4, waiting for transfers between devices, tree_scatter(): lax.psum_scatter(parts, TREE, scatter_dimension=0, tiled=True).astype(F32)  73.9 us
    all_to_all x11, waiting for transfers between devices, exchange(): return lax.all_to_all(parts, axes, split_axis=0, concat_axis=0, tiled=True)  68.3 us
    dot_general x6, matrix products, dot32(): return jnp.dot(a, b, preferred_element_type=F32)  55.4 us
    all_to_all x11, starting transfers between devices, exchange(): return lax.all_to_all(parts, axes, split_axis=0, concat_axis=0, tiled=True)  54.8 us
    dot_general x6, matrix products, dot_nt(): lax.dot_general(a, b, (((1,), (1,)), ((), ())), preferred_element_type=F32)  50.1 us
    dot_general x7, matrix products, dot_tn(): lax.dot_general(a, b, (((0,), (0,)), ((), ())), preferred_element_type=F32)  47.8 us
    pallas_call x1, Pallas kernels, attention_back(): pl.pallas_call(functools.partial(attn_bwd_kernel, heads, seg_len), out_sh...  31.9 us
  transfers between devices with their start and end apart: 28, of which 13 were waited for; matrix products, arithmetic and copies ran while one was open for 32% of the time, Pallas kernels for 6%

profile of v1, /device:TPU:0, one launch (start us, length us, event | category | flops | bytes accessed | tf_op | source)
XLA Modules:
  0.0 848.7 jit_solution(5461771296876736914)
XLA Ops:
  12.2 49.5 %all_to_all.80 = bf16[4,64,1664]{2,1,0:T(8,128)(2,1)S(1)} all-to-all(bf16[4,64,1664]{2,1,0:T(8,128)(2,1)S(1)} %broadcast_in_dim.113), channel_id=1, replica_groups=mesh['dp'=4,'q'=4,'r'=1,'c'=2] {'q','r'}, dimensions={0} | all-to-all | bytes 1703936 | tf_op jit(solution)/shard_map/all_to_all | solution.py:253
  95.3 6.2 all-to-all-done.1
  105.4 6.6 all-to-all-start.2
  115.5 6.3 all-to-all-done.2
  134.3 6.8 all_to_all.81
  160.6 14.7 %fusion.3 = f32[1600,1536]{1,0:T(8,128)S(1)} fusion(bf16[1600,2048]{1,0:T(8,128)(2,1)} %all-gather.5.cloned.1.call-done, f32[2048]{0:T(1024)S(1)} %get-tuple-element.73, f32[1600]{0:T(1024)S(1)} %add_rsqrt_fusion.1, bf16[2048,1664]{1,0:T(8,128)(2,1)} %bitcast.152), kind=kOutput, calls=%fused_computation.9 | convolution fusion | flops 10079436800 | bytes 22690048 | tf_op jit(solution)/shard_map/dot_general | solution.py:28
  181.4 7.0 all-to-all-start.3
  188.8 7.0 fusion.38
  202.2 22.3 %attn_fwd.1 = (bf16[1600,512]{1,0:T(8,128)(2,1)S(1)}, f32[5,1,640]{2,1,0:T(1,128)S(1)}) custom-call(s32[5,1,640]{2,1,0:T(1,128)S(1)} %reshape.331.bits_ref, bf16[1600,512]{1,0:T(8,128)(2,1)S(1)} %pad_maximum_fusion.3.q_ref, bf16[1600,256]{1,0:T(8,128)(2,1)S(1)} %pad_maximum_fusion.5.k_ref, bf16[1600,256]{1,0:T(8,128)(2,1)S(1)} %copy-done.1), custom_call_target="tpu_custom_call" | custom-call | flops 2621440000 | bytes 4915200 | tf_op jit(solution)/shard_map/attn_fwd/pallas_call | solution.py:181
  226.3 8.3 convolution_convert_fusion.1
  234.6 4.8 broadcast_in_dim.129
  239.4 5.3 all-to-all-start.5
  244.8 61.9 %reduce-scatter.5.cloned.1.call-done = bf16[200,2048]{1,0:T(8,128)(2,1)} async-done(((bf16[1600,2048]{1,0:T(8,128)(2,1)}), bf16[200,2048]{1,0:T(8,128)(2,1)}) %reduce-scatter.5.cloned.1.call-update) | async-done | bytes 819216 | tf_op jit(solution)/shard_map/reduce_scatter | solution.py:281
  309.2 5.7 all-to-all-done.5
  321.8 4.6 all-to-all-start.6
  326.6 6.8 fusion.39
  333.5 25.8 %all-to-all-done.6 = bf16[4,176,2048]{2,1,0:T(8,128)(2,1)} async-done(((bf16[4,176,2048]{2,1,0:T(8,128)(2,1)}), bf16[4,176,2048]{2,1,0:T(8,128)(2,1)}, u32[]{:S(2)}, u32[]{:S(2)}) %all-to-all-start.6) | async-done | bytes 2883616 | tf_op jit(solution)/shard_map/all_to_all | solution.py:253
  359.3 26.7 %all-gather.9.cloned.1.call-done = bf16[1600,2048]{1,0:T(8,128)(2,1)} async-done(((bf16[200,2048]{1,0:T(8,128)(2,1)}), bf16[1600,2048]{1,0:T(8,128)(2,1)}) %all-gather.9.cloned.1.call-update) | async-done | bytes 6553616 | tf_op jit(solution)/shard_map/all_gather | solution.py:278
  386.0 11.5 %fusion.42 = f32[1600,704]{0,1:T(8,128)} fusion(bf16[1600,2048]{1,0:T(8,128)(2,1)} %all-gather.9.cloned.1.call-done, bf16[2048,704]{1,0:T(8,128)(2,1)} %bitcast.164), kind=kOutput, calls=%fused_computation.153 | convolution fusion | flops 4613734400 | bytes 13942784 | tf_op jit(solution)/shard_map/dot_general | solution.py:28
  397.5 8.0 fusion.43
  405.5 13.6 %multiply_convert_fusion.1 = (bf16[1600,704]{0,1:T(8,128)(2,1)}, bf16[1600,704]{0,1:T(8,128)(2,1)}, bf16[1600,704]{0,1:T(8,128)(2,1)}) fusion(f32[1600,704]{0,1:T(8,128)} %fusion.42, f32[1600,704]{0,1:T(8,128)} %fusion.43, bf16[1600,2048]{1,0:T(8,128)(2,1)S(1)} %bitcast.186, bf16[704,2048]{1,0:T(8,128)(2,1)} %bitcast.30), kind=kOutput, calls=%fused_computation.20 | convolution fusion | flops 4631756800 | bytes 25206784 | tf_op jit(solution)/shard_map/dot_general | solution.py:32
  419.2 7.3 fusion.44
  426.5 9.8 %add_convert_fusion = bf16[1600,2048]{1,0:T(8,128)(2,1)} fusion(f32[1600,2048]{1,0:T(8,128)S(1)} %fusion.44, bf16[1600,704]{0,1:T(8,128)(2,1)} %get-tuple-element.82, bf16[2048,704]{1,0:T(8,128)(2,1)S(1)} %bitcast.163), kind=kOutput, calls=%fused_computation.5 | convolution fusion | flops 4620288000 | bytes 24797184 | tf_op jit(solution)/shard_map/dot_general | solution.py:32
  436.3 10.4 %convolution_convert_fusion.6 = bf16[704,2048]{1,0:T(8,128)(2,1)} fusion(bf16[1600,704]{0,1:T(8,128)(2,1)} %get-tuple-element.60, bf16[1600,2048]{1,0:T(8,128)(2,1)} %all-gather.7.cloned.1.call-done), kind=kOutput, calls=%fused_computation.33 | convolution fusion | flops 4615176192 | bytes 11689984 | tf_op jit(solution)/shard_map/dot_general | solution.py:36
  446.7 4.6 all-to-all-start.7
  451.3 10.0 %convolution_convert_fusion.5 = bf16[2048,704]{0,1:T(8,128)(2,1)} fusion(bf16[1600,704]{0,1:T(8,128)(2,1)} %get-tuple-element.83, bf16[1600,2048]{1,0:T(8,128)(2,1)} %all-gather.9.cloned.1.call-done), kind=kOutput, calls=%fused_computation.32 | convolution fusion | flops 4615176192 | bytes 11689984 | tf_op jit(solution)/shard_map/dot_general | solution.py:36
  461.4 7.1 stack_reshape.6
  468.4 10.0 %convolution_convert_fusion.4 = bf16[2048,704]{0,1:T(8,128)(2,1)} fusion(bf16[1600,704]{0,1:T(8,128)(2,1)} %get-tuple-element.82, bf16[1600,2048]{1,0:T(8,128)(2,1)} %all-gather.9.cloned.1.call-done), kind=kOutput, calls=%fused_computation.31 | convolution fusion | flops 4615176192 | bytes 11689984 | tf_op jit(solution)/shard_map/dot_general | solution.py:36
  478.5 7.1 stack_reshape.7
  495.4 11.9 %reduce-scatter.7.cloned.1.call-done = bf16[200,2048]{1,0:T(8,128)(2,1)} async-done(((bf16[1600,2048]{1,0:T(8,128)(2,1)}), bf16[200,2048]{1,0:T(8,128)(2,1)}) %reduce-scatter.7.cloned.1.call-update) | async-done | bytes 819216 | tf_op jit(solution)/shard_map/reduce_scatter | solution.py:281
  512.0 69.5 %all_to_all.82 = bf16[4,2,512,704]{2,3,1,0:T(8,128)(2,1)} all-to-all(bf16[4,2,512,704]{2,3,1,0:T(8,128)(2,1)} %copy_dynamic-update-slice_fusion), channel_id=1, replica_groups=mesh['dp'=4,'q'=4,'r'=1,'c'=2] {'dp'}, dimensions={0} | all-to-all | bytes 11534336 | tf_op jit(solution)/shard_map/all_to_all | solution.py:253
  581.5 5.1 reduce_sum.187
  589.5 4.3 all-to-all-start.9
  593.9 8.4 convolution_convert_fusion.8.da_ref
  602.2 31.9 %attn_bwd.1 = (bf16[1600,512]{1,0:T(8,128)(2,1)}, bf16[1600,256]{1,0:T(8,128)(2,1)S(1)}, bf16[1600,256]{1,0:T(8,128)(2,1)S(1)}) custom-call(s32[5,1,640]{2,1,0:T(1,128)S(1)} %reshape.331.bits_ref, f32[5,1,640]{2,1,0:T(1,128)S(1)} %get-tuple-element.49.lse_ref, f32[1600,128]{1,0:T(8,128)S(1)} %bitcast.144, f32[1600,128]{1,0:T(8,128)S(1)} %bitcast.146, ...), custom_call_target="tpu_custom_call" | custom-call | flops 6553600000 | bytes 9830400 | tf_op jit(solution)/shard_map/attn_bwd/pallas_call | solution.py:200
  641.8 5.8 reshape.344
  648.9 7.1 convolution_convert_fusion.7
  657.5 4.9 all-to-all-start.11
  662.5 6.6 convolution_convert_fusion.9
  669.0 18.5 %all_to_all.83 = bf16[4,256,512]{2,1,0:T(8,128)(2,1)S(1)} all-to-all(bf16[4,256,512]{2,1,0:T(8,128)(2,1)} %bitcast.173), channel_id=1, replica_groups=mesh['dp'=4,'q'=4,'r'=1,'c'=2] {'dp'}, dimensions={0} | all-to-all | bytes 2097152 | tf_op jit(solution)/shard_map/all_to_all | solution.py:253
  687.5 4.5 all-to-all-start.12
  692.1 9.6 %convolution_convert_fusion = bf16[1600,2048]{1,0:T(8,128)(2,1)} fusion(bf16[1600,704]{0,1:T(8,128)(2,1)} %get-tuple-element.60, bf16[704,2048]{1,0:T(8,128)(2,1)} %bitcast.30), kind=kOutput, calls=%fused_computation.6 | convolution fusion | flops 4617011200 | bytes 11689984 | tf_op jit(solution)/shard_map/dot_general | solution.py:28
  702.6 14.2 %all-to-all-done.12 = bf16[4,128,2048]{2,1,0:T(8,128)(2,1)} async-done(((bf16[4,128,2048]{2,1,0:T(8,128)(2,1)}), bf16[4,128,2048]{2,1,0:T(8,128)(2,1)}, u32[]{:S(2)}, u32[]{:S(2)}) %all-to-all-start.12) | async-done | bytes 2097184 | tf_op jit(solution)/shard_map/all_to_all | solution.py:253
  726.1 7.4 fusion.20
  749.7 42.8 %all_to_all.84 = bf16[4,4,64,1664]{3,2,1,0:T(8,128)(2,1)S(1)} all-to-all(bf16[4,4,64,1664]{3,2,1,0:T(8,128)(2,1)S(1)} %bitcast.148), channel_id=1, replica_groups=mesh['dp'=4,'q'=4,'r'=1,'c'=2] {'dp'}, dimensions={0} | all-to-all | bytes 6815744 | tf_op jit(solution)/shard_map/all_to_all | solution.py:253
  792.5 4.9 all-to-all-start.15
  799.0 8.2 all-to-all-done.15
  807.2 4.5 all-to-all-start.14
  (271 shorter events, 187.7 us)
Async XLA Ops:
  7.2 118.9 %all-gather.5.cloned.1.call-start = ((), (), s32[]{:S(2)}) async-start(), calls=%async_computation.20 | async-start | bytes 7372800 | tf_op jit(solution)/shard_map/all_gather | solution.py:278
  63.8 37.7 %all-to-all-start.1 = ((bf16[4,4,64,1664]{3,2,1,0:T(8,128)(2,1)}), bf16[4,4,64,1664]{3,2,1,0:T(8,128)(2,1)S(1)}, u32[]{:S(2)}, u32[]{:S(2)}) async-start(bf16[4,4,64,1664]{3,2,1,0:T(8,128)(2,1)} %broadcast_in_dim.114), calls=%async_computation.1 | async-start | bytes 6815744 | tf_op jit(solution)/shard_map/all_to_all | solution.py:253
  101.5 44.2 %collective-permute-start = (bf16[4,4,64,1664]{3,2,1,0:T(8,128)(2,1)S(1)}, bf16[4,4,64,1664]{3,2,1,0:T(8,128)(2,1)}, u32[]{:S(2)}, u32[]{:S(2)}) collective-permute-start(bf16[4,4,64,1664]{3,2,1,0:T(8,128)(2,1)S(1)} %all-to-all-done.1), channel_id=1, source_target_pairs={{0,1},{1,0},{2,3},{3,2},{4,5},{5,4},{6,7},{7,6},{8,9},{9,8},{10,11... | collective-permute-start | bytes 10223624 | tf_op jit(solution)/shard_map/ppermute | solution.py:262
  101.8 24.3 %collective-permute-start.4 = (bf16[128,2048]{1,0:T(8,128)(2,1)}, bf16[128,2048]{1,0:T(8,128)(2,1)}, u32[]{:S(2)}, u32[]{:S(2)}) collective-permute-start(bf16[128,2048]{1,0:T(8,128)(2,1)} %param.24), channel_id=1, source_target_pairs={{0,8},{8,0},{16,24},{24,16},{1,9},{9,1},{17,25},{25,17},{2,10},{10... | collective-permute-start | bytes 1572872 | tf_op jit(solution)/shard_map/ppermute | solution.py:284
  103.3 25.5 %collective-permute-start.5 = (bf16[128,2048]{1,0:T(8,128)(2,1)}, bf16[128,2048]{1,0:T(8,128)(2,1)}, u32[]{:S(2)}, u32[]{:S(2)}) collective-permute-start(bf16[128,2048]{1,0:T(8,128)(2,1)} %param.24), channel_id=1, source_target_pairs={{0,16},{8,24},{16,0},{24,8},{1,17},{9,25},{17,1},{25,9},{2,18},{10... | collective-permute-start | bytes 1572872 | tf_op jit(solution)/shard_map/ppermute | solution.py:284
  103.9 28.5 %collective-permute-start.6 = (bf16[128,2048]{1,0:T(8,128)(2,1)}, bf16[128,2048]{1,0:T(8,128)(2,1)}, u32[]{:S(2)}, u32[]{:S(2)}) collective-permute-start(bf16[128,2048]{1,0:T(8,128)(2,1)} %param.24), channel_id=1, source_target_pairs={{0,24},{8,16},{16,8},{24,0},{1,25},{9,17},{17,9},{25,1},{2,26},{10... | collective-permute-start | bytes 1572872 | tf_op jit(solution)/shard_map/ppermute | solution.py:284
  105.4 16.5 %all-to-all-start.2 = ((bf16[8,32,512]{2,1,0:T(8,128)(2,1)}), bf16[8,32,512]{2,1,0:T(8,128)(2,1)}, u32[]{:S(2)}, u32[]{:S(2)}) async-start(bf16[8,32,512]{2,1,0:T(8,128)(2,1)} %reshape.333), calls=%async_computation.2 | async-start | bytes 524288 | tf_op jit(solution)/shard_map/all_to_all | solution.py:253
  112.0 114.3 %all-gather.7.cloned.1.call-start = ((), (), s32[]{:S(2)}) async-start(), calls=%async_computation.21 | async-start | bytes 7372800 | tf_op jit(solution)/shard_map/all_gather | solution.py:278
  121.8 20.7 %collective-permute-start.1 = (bf16[8,32,512]{2,1,0:T(8,128)(2,1)}, bf16[8,32,512]{2,1,0:T(8,128)(2,1)}, u32[]{:S(2)}, u32[]{:S(2)}) collective-permute-start(bf16[8,32,512]{2,1,0:T(8,128)(2,1)} %all-to-all-done.2), channel_id=1, source_target_pairs={{0,8},{8,0},{16,24},{24,16},{1,9},{9,1},{17,25},{25,17},{2,10},{10... | collective-permute-start | bytes 786440 | tf_op jit(solution)/shard_map/ppermute | solution.py:284
  126.1 18.1 %collective-permute-start.2 = (bf16[8,32,512]{2,1,0:T(8,128)(2,1)}, bf16[8,32,512]{2,1,0:T(8,128)(2,1)S(1)}, u32[]{:S(2)}, u32[]{:S(2)}) collective-permute-start(bf16[8,32,512]{2,1,0:T(8,128)(2,1)} %all-to-all-done.2), channel_id=1, source_target_pairs={{0,16},{8,24},{16,0},{24,8},{1,17},{9,25},{17,1},{25,9},{2,18},{10... | collective-permute-start | bytes 786440 | tf_op jit(solution)/shard_map/ppermute | solution.py:284
  128.7 16.2 %collective-permute-start.3 = (bf16[8,32,512]{2,1,0:T(8,128)(2,1)}, bf16[8,32,512]{2,1,0:T(8,128)(2,1)S(1)}, u32[]{:S(2)}, u32[]{:S(2)}) collective-permute-start(bf16[8,32,512]{2,1,0:T(8,128)(2,1)} %all-to-all-done.2), channel_id=1, source_target_pairs={{0,24},{8,16},{16,8},{24,0},{1,25},{9,17},{17,9},{25,1},{2,26},{10... | collective-permute-start | bytes 786440 | tf_op jit(solution)/shard_map/ppermute | solution.py:284
  155.8 354.1 %copy-start.26 = (f32[2048]{0:T(1024)}, f32[2048]{0:T(1024)S(1)}, u32[]{:S(2)}) copy-start(f32[2048]{0:T(1024)S(1)} %get-tuple-element.71) | copy-start | bytes 24580
  156.0 39.8 %copy-start.28 = (f32[1024]{0:T(1024)}, f32[1024]{0:T(1024)S(1)}, u32[]{:S(2)}) copy-start(f32[1024]{0:T(1024)S(1)} %mul.402) | copy-start | bytes 12292
  160.6 19.5 %copy-start.16 = (bf16[8,2,64,704]{3,2,0,1:T(8,128)(2,1)S(1)}, bf16[8,2,64,704]{3,2,0,1:T(8,128)(2,1)}, u32[]{:S(2)}) copy-start(bf16[8,2,64,704]{3,2,0,1:T(8,128)(2,1)} %pad_maximum_fusion.4) | copy-start | bytes 4325380
  181.4 44.9 %all-to-all-start.3 = ((bf16[8,2,64,704]{3,2,1,0:T(8,128)(2,1)}), bf16[8,2,64,704]{3,2,1,0:T(8,128)(2,1)}, u32[]{:S(2)}, u32[]{:S(2)}) async-start(bf16[8,2,64,704]{3,2,1,0:T(8,128)(2,1)} %copy.92), calls=%async_computation.3 | async-start | bytes 3145728 | tf_op jit(solution)/shard_map/all_to_all | solution.py:253
  188.3 118.3 %reduce-scatter.5.cloned.1.call-start = ((), (), s32[]{:S(2)}) async-start(), calls=%async_computation.22 | async-start | bytes 7372800 | tf_op jit(solution)/shard_map/reduce_scatter | solution.py:281
  202.2 22.3 %copy-start = (bf16[1600,512]{1,0:T(8,128)(2,1)}, bf16[1600,512]{1,0:T(8,128)(2,1)S(1)}, u32[]{:S(2)}) copy-start(bf16[1600,512]{1,0:T(8,128)(2,1)S(1)} %pad_maximum_fusion.3.q_ref) | copy-start | bytes 4915204
  239.4 75.5 %all-to-all-start.5 = ((bf16[4,8,2,64,704]{4,3,2,1,0:T(8,128)(2,1)}), bf16[4,8,2,64,704]{4,3,2,1,0:T(8,128)(2,1)}, u32[]{:S(2)}, u32[]{:S(2)}) async-start(bf16[4,8,2,64,704]{4,3,2,1,0:T(8,128)(2,1)} %broadcast_in_dim.129), calls=%async_computation.6 | async-start | bytes 12582912 | tf_op jit(solution)/shard_map/all_to_all | solution.py:253
  244.7 141.3 %all-gather.9.cloned.1.call-start = ((), (), s32[]{:S(2)}) async-start(), calls=%async_computation.23 | async-start | bytes 7372800 | tf_op jit(solution)/shard_map/all_gather | solution.py:278
  317.5 192.4 %copy-start.7 = (f32[200,2048]{1,0:T(8,128)}, f32[200,2048]{1,0:T(8,128)S(1)}, u32[]{:S(2)}) copy-start(f32[200,2048]{1,0:T(8,128)S(1)} %get-tuple-element.77) | copy-start | bytes 4915204
  317.5 192.4 %copy-start.33 = (f32[200]{0:T(256)}, f32[200]{0:T(256)S(1)}, u32[]{:S(2)}) copy-start(f32[200]{0:T(256)S(1)} %add_rsqrt_fusion.4) | copy-start | bytes 2404
  321.8 37.5 %all-to-all-start.6 = ((bf16[4,176,2048]{2,1,0:T(8,128)(2,1)}), bf16[4,176,2048]{2,1,0:T(8,128)(2,1)}, u32[]{:S(2)}, u32[]{:S(2)}) async-start(bf16[4,176,2048]{2,1,0:T(8,128)(2,1)} %broadcast_in_dim.130), calls=%async_computation.7 | async-start | bytes 5767168 | tf_op jit(solution)/shard_map/all_to_all | solution.py:253
  326.4 181.0 %reduce-scatter.7.cloned.1.call-start = ((), (), s32[]{:S(2)}) async-start(), calls=%async_computation.24 | async-start | bytes 7372800 | tf_op jit(solution)/shard_map/reduce_scatter | solution.py:281
  386.0 11.5 %copy-start.18 = (bf16[4,8,1,64,704]{4,3,2,1,0:T(8,128)(2,1)S(1)}, bf16[4,8,1,64,704]{4,3,2,1,0:T(8,128)(2,1)}, u32[]{:S(2)}) copy-start(bf16[4,8,1,64,704]{4,3,2,1,0:T(8,128)(2,1)} %get-tuple-element.87) | copy-start | bytes 8650756
  386.0 11.5 %copy-start.43 = (bf16[1600,2048]{1,0:T(8,128)(2,1)S(1)}, bf16[1600,2048]{1,0:T(8,128)(2,1)}, u32[]{:S(2)}) copy-start(bf16[1600,2048]{1,0:T(8,128)(2,1)} %all-gather.9.cloned.1.call-done) | copy-start | bytes 19660804
  386.0 19.5 %slice-start = ((s8[6553600]{0:T(1024)(128)(4,1)}), s8[4194304]{0:T(1024)(128)(4,1)S(1)}, s32[]{:S(2)}) async-start(s8[6553600]{0:T(1024)(128)(4,1)} %bitcast.185), calls=%async_computation.28 | async-start | bytes 8388608
  405.5 13.6 %copy-start.19 = (bf16[4,8,1,64,704]{4,3,2,1,0:T(8,128)(2,1)S(1)}, bf16[4,8,1,64,704]{4,3,2,1,0:T(8,128)(2,1)}, u32[]{:S(2)}) copy-start(bf16[4,8,1,64,704]{4,3,2,1,0:T(8,128)(2,1)} %get-tuple-element.88) | copy-start | bytes 8650756
  446.7 45.2 %all-to-all-start.7 = ((bf16[4,176,2048]{2,1,0:T(8,128)(2,1)}), bf16[4,176,2048]{2,1,0:T(8,128)(2,1)}, u32[]{:S(2)}, u32[]{:S(2)}) async-start(bf16[4,176,2048]{2,1,0:T(8,128)(2,1)} %bitcast.166), calls=%async_computation.9 | async-start | bytes 5767168 | tf_op jit(solution)/shard_map/all_to_all | solution.py:253
  451.3 137.0 %all-gather.11.cloned.1.call-start = ((), (), s32[]{:S(2)}) async-start(), calls=%async_computation.25 | async-start | bytes 7372800 | tf_op jit(solution)/shard_map/all_gather | solution.py:278
  589.5 52.3 %all-to-all-start.9 = ((bf16[8,2,64,704]{3,2,1,0:T(8,128)(2,1)}), bf16[8,2,64,704]{3,2,1,0:T(8,128)(2,1)}, u32[]{:S(2)}, u32[]{:S(2)}) async-start(bf16[8,2,64,704]{3,2,1,0:T(8,128)(2,1)} %copy.98), calls=%async_computation.11 | async-start | bytes 3145728 | tf_op jit(solution)/shard_map/all_to_all | solution.py:253
  593.8 126.0 %reduce-scatter.9.cloned.1.call-start = ((), (), s32[]{:S(2)}) async-start(), calls=%async_computation.26 | async-start | bytes 5529600 | tf_op jit(solution)/shard_map/reduce_scatter | solution.py:281
  657.5 11.6 %all-to-all-start.11 = ((bf16[2,2,128,2048]{3,2,1,0:T(8,128)(2,1)}), bf16[2,2,128,2048]{3,2,1,0:T(8,128)(2,1)}, u32[]{:S(2)}, u32[]{:S(2)}) async-start(bf16[2,2,128,2048]{3,2,1,0:T(8,128)(2,1)} %bitcast.149), calls=%async_computation.14 | async-start | bytes 4194304 | tf_op jit(solution)/shard_map/all_to_all | solution.py:253
  687.5 29.2 %all-to-all-start.12 = ((bf16[4,128,2048]{2,1,0:T(8,128)(2,1)}), bf16[4,128,2048]{2,1,0:T(8,128)(2,1)}, u32[]{:S(2)}, u32[]{:S(2)}) async-start(bf16[4,128,2048]{2,1,0:T(8,128)(2,1)} %bitcast.39), calls=%async_computation.15 | async-start | bytes 4194304 | tf_op jit(solution)/shard_map/all_to_all | solution.py:253
  692.0 145.2 %reduce-scatter.11.cloned.1.call-start = ((), (), s32[]{:S(2)}) async-start(), calls=%async_computation.27 | async-start | bytes 7372800 | tf_op jit(solution)/shard_map/reduce_scatter | solution.py:281
  722.5 11.0 %copy-start.40 = (f32[200]{0:T(256)}, f32[200]{0:T(256)S(1)}, u32[]{:S(2)}) copy-start(f32[200]{0:T(256)S(1)} %add_rsqrt_fusion.3) | copy-start | bytes 2404
  722.5 12.4 %copy-start.20 = (bf16[200,256]{1,0:T(8,128)(2,1)}, bf16[200,256]{1,0:T(8,128)(2,1)S(1)}, u32[]{:S(2)}) copy-start(bf16[200,256]{1,0:T(8,128)(2,1)S(1)} %slice.209) | copy-start | bytes 307204
  724.7 10.2 %copy-start.22 = (bf16[200,128]{1,0:T(8,128)(2,1)}, bf16[200,128]{1,0:T(8,128)(2,1)S(1)}, u32[]{:S(2)}) copy-start(bf16[200,128]{1,0:T(8,128)(2,1)S(1)} %get-tuple-element.95) | copy-start | bytes 153604
  737.6 10.8 %collective-permute-start.7 = (bf16[1024,1536]{1,0:T(8,128)(2,1)}, bf16[1024,1536]{1,0:T(8,128)(2,1)S(1)}, u32[]{:S(2)}, u32[]{:S(2)}) collective-permute-start(bf16[1024,1536]{1,0:T(8,128)(2,1)} %convolution_convert_fusion.2), channel_id=1, source_target_pairs={{0,1},{1,0},{2,3},{3,2},{4,5},{5,4},{6,7},{7,6},{8,9},{9,8},{10,11... | collective-permute-start | bytes 9437192 | tf_op jit(solution)/shard_map/ppermute | solution.py:262
  746.6 1.7 collective-permute-start.8
  792.5 14.7 %all-to-all-start.15 = ((bf16[8,32,512]{2,1,0:T(8,128)(2,1)}), bf16[8,32,512]{2,1,0:T(8,128)(2,1)}, u32[]{:S(2)}, u32[]{:S(2)}) async-start(bf16[8,32,512]{2,1,0:T(8,128)(2,1)} %bitcast.172), calls=%async_computation.19 | async-start | bytes 524288 | tf_op jit(solution)/shard_map/all_to_all | solution.py:253
  807.2 25.9 %all-to-all-start.14 = ((bf16[4,64,1664]{2,1,0:T(8,128)(2,1)}), bf16[4,64,1664]{2,1,0:T(8,128)(2,1)}, u32[]{:S(2)}, u32[]{:S(2)}) async-start(bf16[4,64,1664]{2,1,0:T(8,128)(2,1)} %reduce_sum.197), calls=%async_computation.18 | async-start | bytes 1703936 | tf_op jit(solution)/shard_map/all_to_all | solution.py:253
  825.3 11.9 %copy-start.8 = (f32[200,2048]{1,0:T(8,128)S(1)}, f32[200,2048]{1,0:T(8,128)}, u32[]{:S(2)}) copy-start(f32[200,2048]{1,0:T(8,128)} %copy-done.7) | copy-start | bytes 4915204
  825.3 11.9 %copy-start.10 = (f32[200,2048]{1,0:T(8,128)S(1)}, f32[200,2048]{1,0:T(8,128)}, u32[]{:S(2)}) copy-start(f32[200,2048]{1,0:T(8,128)} %copy-done.9) | copy-start | bytes 4915204
  825.3 11.9 %copy-start.27 = (f32[2048]{0:T(1024)S(1)}, f32[2048]{0:T(1024)}, u32[]{:S(2)}) copy-start(f32[2048]{0:T(1024)} %copy-done.26) | copy-start | bytes 24580
  825.3 11.9 %copy-start.32 = (f32[2048]{0:T(1024)S(1)}, f32[2048]{0:T(1024)}, u32[]{:S(2)}) copy-start(f32[2048]{0:T(1024)} %copy-done.30) | copy-start | bytes 24580
  825.3 11.9 %copy-start.34 = (f32[200]{0:T(256)S(1)}, f32[200]{0:T(256)}, u32[]{:S(2)}) copy-start(f32[200]{0:T(256)} %copy-done.33) | copy-start | bytes 2404
  825.3 11.9 %copy-start.36 = (f32[200]{0:T(256)S(1)}, f32[200]{0:T(256)}, u32[]{:S(2)}) copy-start(f32[200]{0:T(256)} %copy-done.35) | copy-start | bytes 2404
  825.3 11.9 %copy-start.41 = (f32[200]{0:T(256)S(1)}, f32[200]{0:T(256)}, u32[]{:S(2)}) copy-start(f32[200]{0:T(256)} %copy-done.40) | copy-start | bytes 2404
  (27 other events, 118.4 us)
Sparse Core Ops, SparseCore 0:
  9.7 84.5 all-gather.4
  126.2 64.8 all-gather.6
  234.7 71.8 reduce-scatter.4
  318.9 67.0 all-gather.8
  436.4 70.9 reduce-scatter.6
  512.1 65.2 all-gather.10
  647.7 56.6 reduce-scatter.8
  721.2 72.5 reduce-scatter.10

commit v2 on v1

v2 whole, which is shorter than its diff:
```python
import functools

import jax
import jax.numpy as jnp
from jax import lax
from jax.experimental import pallas as pl
from jax.experimental.layout import Layout, with_layout_constraint
from jax.experimental.pallas import tpu as pltpu
from jax.sharding import PartitionSpec as P

H = 16
HD = 256
NSEG = 20

EPSILON = 1e-06
ROPE_BASE = 10000.0
HIGHEST = lax.Precision.HIGHEST
NEGATIVE = -1e30
BF = jnp.bfloat16
F32 = jnp.float32
CHUNK = 160
TREE = ("q", "r", "c")
LINE = ("q", "r")
SHARE = ("r", "c")
VMEM_LIMIT = 48 * 1024 * 1024


def dot32(a, b):
    return jnp.dot(a, b, preferred_element_type=F32)


def dot_nt(a, b):
    return lax.dot_general(a, b, (((1,), (1,)), ((), ())), preferred_element_type=F32)


def dot_tn(a, b):
    return lax.dot_general(a, b, (((0,), (0,)), ((), ())), preferred_element_type=F32)


def rms_scale(values):
    return lax.rsqrt(jnp.mean(values * values, axis=-1, keepdims=True) + EPSILON)


def norm_back(upstream, normed, row_scale, gain_vec):
    scaled = upstream * gain_vec
    inner_mean = jnp.mean(scaled * normed, axis=-1, keepdims=True)
    return row_scale * (scaled - normed * inner_mean)


def gain_column(upstream, normed, column):
    picked = (lax.broadcasted_iota(jnp.int32, (upstream.shape[0], 128), 1) == column).astype(F32)
    return lax.dot_general(
        upstream * normed, picked, (((0,), (0,)), ((), ())), precision=HIGHEST, preferred_element_type=F32
    )


def rotate(values, cosines, sines):
    half = values.shape[-1] // 2
    a, b = values[..., :half], values[..., half:]
    return jnp.concatenate([a * cosines - b * sines, b * cosines + a * sines], axis=-1)


def tile_plan(tile, per_tile):
    free = jnp.minimum(tile, 2) * per_tile
    count = jnp.where(tile == 4, 4, tile + 1) * per_tile
    return free, count


def chunk_start(tile, j, per_tile):
    jump = jnp.where((tile == 4) & (j >= 3 * per_tile), per_tile, 0)
    return pl.multiple_of((j + jump) * CHUNK, CHUNK)


def seen(k0, bits_row, q_pos, seg_len):
    shape = (CHUNK, q_pos.shape[1])
    key_pos = lax.broadcasted_iota(jnp.int32, (CHUNK, 1), 0) + k0
    key_bit = jnp.left_shift(jnp.int32(1), key_pos // seg_len)
    reach = jnp.broadcast_to(key_bit, shape) & jnp.broadcast_to(bits_row, shape)
    return (reach != 0) & (jnp.broadcast_to(key_pos, shape) <= jnp.broadcast_to(q_pos, shape))


def query_places(tile, tile_rows, heads):
    lane = lax.broadcasted_iota(jnp.int32, (1, heads * tile_rows), 1)
    return tile * tile_rows + lax.rem(lane, tile_rows)


def attn_fwd_kernel(heads, seg_len, bits_ref, q_ref, k_ref, v_ref, att_ref, lse_ref, qs, st):
    tile_rows = 4 * seg_len
    width = heads * tile_rows
    per_tile = tile_rows // CHUNK
    scale = HD ** (-0.5)

    def one_tile(tile, carry):
        q0 = pl.multiple_of(tile * tile_rows, tile_rows)
        for h in range(heads):
            rows = q_ref[pl.ds(q0, tile_rows), h * HD : (h + 1) * HD]
            qs[h * tile_rows : (h + 1) * tile_rows, :] = (rows.astype(F32) * scale).astype(BF)
        bits_row = bits_ref[tile]
        q_pos = query_places(tile, tile_rows, heads)
        free, count = tile_plan(tile, per_tile)

        def score(masked, j, top):
            k0 = chunk_start(tile, j, per_tile)
            s = dot_nt(k_ref[pl.ds(k0, CHUNK), :], qs[...])
            if masked:
                s = jnp.where(seen(k0, bits_row, q_pos, seg_len), s, NEGATIVE)
            st[pl.ds(pl.multiple_of(j * CHUNK, CHUNK), CHUNK), :] = s
            return jnp.maximum(top, jnp.max(s, axis=0, keepdims=True))

        top = lax.fori_loop(0, free, functools.partial(score, False), jnp.full((1, width), NEGATIVE, F32))
        top = lax.fori_loop(free, count, functools.partial(score, True), top)

        def gather(j, carry):
            total, acc = carry
            k0 = chunk_start(tile, j, per_tile)
            p = jnp.exp(st[pl.ds(pl.multiple_of(j * CHUNK, CHUNK), CHUNK), :] - top)
            acc = acc + dot_tn(v_ref[pl.ds(k0, CHUNK), :], p.astype(BF))
            return total + jnp.sum(p, axis=0, keepdims=True), acc

        total, out = lax.fori_loop(0, count, gather, (jnp.zeros((1, width), F32), jnp.zeros((HD, width), F32)))
        lse_ref[tile] = top + jnp.log(total)
        out = (out * (1.0 / total)).T.astype(BF)
        for h in range(heads):
            att_ref[pl.ds(q0, tile_rows), h * HD : (h + 1) * HD] = out[h * tile_rows : (h + 1) * tile_rows, :]
        return carry

    lax.fori_loop(0, 5, one_tile, 0)


def attn_bwd_kernel(
    heads, seg_len, bits_ref, lse_ref, cos_ref, sin_ref, q_ref, k_ref, v_ref, att_ref, da_ref,
    dq_ref, dk_ref, dv_ref, qs, das, dk, dv,
):
    tile_rows = 4 * seg_len
    width = heads * tile_rows
    per_tile = tile_rows // CHUNK
    scale = HD ** (-0.5)
    dk[...] = jnp.zeros_like(dk)
    dv[...] = jnp.zeros_like(dv)

    def one_tile(tile, carry):
        q0 = pl.multiple_of(tile * tile_rows, tile_rows)
        deltas = []
        for h in range(heads):
            rows = slice(h * tile_rows, (h + 1) * tile_rows)
            cols = slice(h * HD, (h + 1) * HD)
            here = pl.ds(q0, tile_rows)
            qs[rows, :] = (q_ref[here, cols].astype(F32) * scale).astype(BF)
            grad = da_ref[here, cols]
            das[rows, :] = grad
            both = grad.astype(F32) * att_ref[here, cols].astype(F32)
            deltas.append(jnp.sum(both.T, axis=0, keepdims=True))
        delta = jnp.concatenate(deltas, axis=1)
        bits_row = bits_ref[tile]
        lse_row = lse_ref[tile]
        q_pos = query_places(tile, tile_rows, heads)
        free, count = tile_plan(tile, per_tile)

        def step(masked, j, acc):
            k0 = chunk_start(tile, j, per_tile)
            at = pl.ds(k0, CHUNK)
            keys = k_ref[at, :]
            p = jnp.exp(dot_nt(keys, qs[...]) - lse_row)
            if masked:
                p = jnp.where(seen(k0, bits_row, q_pos, seg_len), p, 0.0)
            dp = dot_nt(v_ref[at, :], das[...])
            ds = (p * (dp - delta)).astype(BF)
            dv[at, :] += dot32(p.astype(BF), das[...])
            dk[at, :] += dot32(ds, qs[...])
            return acc + dot_tn(keys, ds)

        acc = lax.fori_loop(0, free, functools.partial(step, False), jnp.zeros((HD, width), F32))
        acc = lax.fori_loop(free, count, functools.partial(step, True), acc)
        out = (acc * scale).T
        at = pl.ds(q0, tile_rows)
        for h in range(heads):
            grad = out[h * tile_rows : (h + 1) * tile_rows, :]
            dq_ref[at, h * HD : (h + 1) * HD] = rotate(grad, cos_ref[at, :], -sin_ref[at, :]).astype(BF)
        return carry

    lax.fori_loop(0, 5, one_tile, 0)
    dk_ref[...] = dk[...].astype(BF)
    dv_ref[...] = dv[...].astype(BF)


def attention(bits, q, k, v, heads, seg_len):
    tree_len = q.shape[0]
    width = heads * 4 * seg_len
    work = heads * tree_len * tree_len // 2
    return pl.pallas_call(
        functools.partial(attn_fwd_kernel, heads, seg_len),
        out_shape=(
            jax.ShapeDtypeStruct((tree_len, heads * HD), BF),
            jax.ShapeDtypeStruct((5, 1, width), F32),
        ),
        in_specs=[pl.BlockSpec(memory_space=pltpu.VMEM)] * 4,
        out_specs=(pl.BlockSpec(memory_space=pltpu.VMEM),) * 2,
        scratch_shapes=[pltpu.VMEM((width, HD), BF), pltpu.VMEM((16 * seg_len, width), F32)],
        compiler_params=pltpu.CompilerParams(vmem_limit_bytes=VMEM_LIMIT),
        cost_estimate=pl.CostEstimate(flops=4 * HD * work, bytes_accessed=6 * tree_len * HD * 2, transcendentals=work),
        name="attn_fwd",
    )(bits, q, k, v)


def attention_back(bits, lse, cosines, sines, q, k, v, attended, da, heads, seg_len):
    tree_len = q.shape[0]
    width = heads * 4 * seg_len
    work = heads * tree_len * tree_len // 2
    return pl.pallas_call(
        functools.partial(attn_bwd_kernel, heads, seg_len),
        out_shape=(
            jax.ShapeDtypeStruct((tree_len, heads * HD), BF),
            jax.ShapeDtypeStruct((tree_len, HD), BF),
            jax.ShapeDtypeStruct((tree_len, HD), BF),
        ),
        in_specs=[pl.BlockSpec(memory_space=pltpu.VMEM)] * 9,
        out_specs=(pl.BlockSpec(memory_space=pltpu.VMEM),) * 3,
        scratch_shapes=[
            pltpu.VMEM((width, HD), BF),
            pltpu.VMEM((width, HD), BF),
            pltpu.VMEM((tree_len, HD), F32),
            pltpu.VMEM((tree_len, HD), F32),
        ],
        compiler_params=pltpu.CompilerParams(vmem_limit_bytes=VMEM_LIMIT),
        cost_estimate=pl.CostEstimate(flops=10 * HD * work, bytes_accessed=12 * tree_len * HD * 2, transcendentals=work),
        name="attn_bwd",
    )(bits, lse, cosines, sines, q, k, v, attended, da)


def whole(shape):
    return pl.BlockSpec(shape, lambda i: (0,) * len(shape), pipeline_mode=pl.Buffered(1))


def by_rows(rows, width):
    return pl.BlockSpec((rows, width), lambda i: (i, 0))


def project_kernel(heads, latent_width, x_ref, w_ref, qup_ref, g1_ref, gl_ref, cos_ref, sin_ref, q_ref, k_ref, v_ref, l_ref):
    x = x_ref[...].astype(F32)
    normed = (x * rms_scale(x) * g1_ref[...]).astype(BF)
    latent = dot32(normed, w_ref[:, :latent_width])
    latent_in = (latent * rms_scale(latent) * gl_ref[...]).astype(BF)
    l_ref[...] = latent_in
    cosines, sines = cos_ref[...], sin_ref[...]
    both = dot32(normed, w_ref[:, latent_width : latent_width + 2 * HD])
    k_ref[...] = rotate(both[:, :HD], cosines, sines).astype(BF)
    v_ref[...] = both[:, HD:].astype(BF)
    query = dot32(latent_in, qup_ref[...])
    for h in range(heads):
        at = slice(h * HD, (h + 1) * HD)
        q_ref[:, at] = rotate(query[:, at], cosines, sines).astype(BF)


def project(x, w_in, qup_cols, gain_one, gain_latent, cosines, sines, heads, rows):
    tree_len, model = x.shape
    latent_width = qup_cols.shape[0]
    outs = [(heads * HD, BF), (HD, BF), (HD, BF), (latent_width, BF)]
    flops = 2 * tree_len * (model * (latent_width + 2 * HD) + latent_width * heads * HD)
    return pl.pallas_call(
        functools.partial(project_kernel, heads, latent_width),
        grid=(tree_len // rows,),
        out_shape=[jax.ShapeDtypeStruct((tree_len, w), t) for w, t in outs],
        in_specs=[
            by_rows(rows, model),
            whole(w_in.shape),
            whole(qup_cols.shape),
            whole((1, model)),
            whole((1, latent_width)),
            by_rows(rows, HD // 2),
            by_rows(rows, HD // 2),
        ],
        out_specs=[by_rows(rows, w) for w, _ in outs],
        compiler_params=pltpu.CompilerParams(vmem_limit_bytes=VMEM_LIMIT),
        cost_estimate=pl.CostEstimate(flops=flops, bytes_accessed=tree_len * 10000 + w_in.size * 2, transcendentals=0),
        name="project",
    )(x, w_in, qup_cols, gain_one[None], gain_latent[None], cosines, sines)


def ffn_kernel(mid_ref, cot_ref, wg_ref, wu_ref, wd_ref, act_ref, gg_ref, ug_ref, part_ref):
    mid = mid_ref[...]
    gate = dot32(mid, wg_ref[...])
    up = dot32(mid, wu_ref[...])
    grad = dot_nt(cot_ref[...], wd_ref[...])
    sig = jax.nn.sigmoid(gate)
    silu = gate * sig
    act_ref[...] = (silu * up).astype(BF)
    gate_grad = (grad * up * sig * (1.0 + gate * (1.0 - sig))).astype(BF)
    up_grad = (grad * silu).astype(BF)
    gg_ref[...] = gate_grad
    ug_ref[...] = up_grad
    part_ref[...] = (dot_nt(gate_grad, wg_ref[...]) + dot_nt(up_grad, wu_ref[...])).astype(BF)


def ffn(mid, cot, gate_cols, up_cols, down_rows, rows):
    count, model = mid.shape
    units = gate_cols.shape[1]
    outs = [(units, BF)] * 3 + [(model, BF)]
    return pl.pallas_call(
        ffn_kernel,
        grid=(count // rows,),
        out_shape=[jax.ShapeDtypeStruct((count, w), t) for w, t in outs],
        in_specs=[by_rows(rows, model)] * 2 + [whole(gate_cols.shape)] * 2 + [whole(down_rows.shape)],
        out_specs=[by_rows(rows, w) for w, _ in outs],
        compiler_params=pltpu.CompilerParams(vmem_limit_bytes=VMEM_LIMIT),
        cost_estimate=pl.CostEstimate(
            flops=10 * count * model * units, bytes_accessed=6 * (count + units) * model, transcendentals=count * units
        ),
        name="ffn",
    )(mid, cot, gate_cols, up_cols, down_rows)


def unit_grad_kernel(mid_ref, grad_ref, out_ref, turned):
    @pl.when(pl.program_id(0) == 0)
    def _():
        turned[...] = grad_ref[...].T

    out_ref[0] = dot32(turned[...], mid_ref[...]).astype(BF)


def unit_grads(mid, grad, parts):
    count, model = mid.shape
    units = grad.shape[1]
    wide = model // parts
    return pl.pallas_call(
        unit_grad_kernel,
        grid=(parts,),
        out_shape=jax.ShapeDtypeStruct((parts, units, wide), BF),
        in_specs=[pl.BlockSpec((count, wide), lambda i: (0, i)), whole(grad.shape)],
        out_specs=pl.BlockSpec((1, units, wide), lambda i: (i, 0, 0)),
        scratch_shapes=[pltpu.VMEM((units, count), BF)],
        compiler_params=pltpu.CompilerParams(vmem_limit_bytes=VMEM_LIMIT),
        cost_estimate=pl.CostEstimate(
            flops=2 * count * model * units, bytes_accessed=2 * (count + units) * model, transcendentals=0
        ),
        name="unit_grads",
    )(mid, grad)


def body(
    hidden_in,
    segment_ids,
    parents,
    norm_gain,
    w_qdown,
    q_gain,
    w_qup,
    w_key,
    w_value,
    w_out,
    ffn_gain,
    w_gate,
    w_up,
    w_down,
    cotangent,
):
    rows, model = hidden_in.shape
    dn, cn = lax.axis_size("dp"), lax.axis_size("c")
    zn, sn = lax.axis_size(LINE), lax.axis_size(SHARE)
    fn = lax.axis_size(TREE)
    heads = H // fn
    latent_width = w_qdown.shape[1]
    in_width = latent_width + 2 * HD
    per_row, per_latent = norm_gain.shape[0], q_gain.shape[0]
    d_at, c_at, f_at = lax.axis_index("dp"), lax.axis_index("c"), lax.axis_index(TREE)
    tree_len = rows * fn
    seg_len = tree_len // NSEG
    block_rows = 2 * rows

    def exchange(parts, axes):
        return lax.all_to_all(parts, axes, split_axis=0, concat_axis=0, tiled=True)

    def spread(block, axes):
        return exchange(jnp.broadcast_to(block[None], (lax.axis_size(axes),) + block.shape), axes)

    def total(parts, axes):
        return jnp.sum(exchange(parts.astype(BF), axes).astype(F32), axis=0)

    def other_core(a):
        return lax.ppermute(a, "c", [(c, (c + 1) % cn) for c in range(cn)])

    def by_core(mine, axis):
        came = other_core(mine)
        return jnp.stack([jnp.where(c_at == 0, mine, came), jnp.where(c_at == 0, came, mine)], axis=axis)

    def exchange_share(parts):
        if sn != cn:
            return exchange(parts, SHARE)
        came = other_core(at_index(parts, 1 - c_at))
        return jnp.stack([jnp.where(c_at == 0, parts[0], came), jnp.where(c_at == 0, came, parts[1])])

    def at_index(a, index, axis=0):
        return lax.dynamic_index_in_dim(a, index, axis, keepdims=False)

    def plain(a):
        return with_layout_constraint(a, Layout(major_to_minor=tuple(range(a.ndim))))

    def after(a, *before):
        return lax.optimization_barrier((a,) + before)[0]

    def own_rows(a):
        return lax.dynamic_slice_in_dim(a, f_at * rows, rows, 0)

    def tree_gather(block):
        return lax.all_gather(block, TREE, axis=0, tiled=True)

    def tree_scatter(parts):
        return lax.psum_scatter(parts, TREE, scatter_dimension=0, tiled=True).astype(F32)

    def over_dp(a, m):
        return lax.ppermute(a, "dp", [(d, d ^ m) for d in range(dn)])

    def spread_dp(block):
        out = jnp.zeros((dn,) + block.shape, block.dtype)
        for m in range(dn):
            got = over_dp(block, m) if m else block
            out = lax.dynamic_update_index_in_dim(out, got, d_at ^ m, 0)
        return out

    def spread_line(block):
        out = jnp.zeros((zn,) + block.shape, block.dtype)
        z_at = lax.axis_index(LINE)
        for m in range(zn):
            got = lax.ppermute(block, LINE, [(z, (z + m) % zn) for z in range(zn)]) if m else block
            out = lax.dynamic_update_index_in_dim(out, got, (z_at + zn - m) % zn, 0)
        return out

    tags = -(-rows // per_row)
    extra = jnp.concatenate(
        [
            norm_gain[:, None],
            ffn_gain[:, None],
            jnp.pad(q_gain, (0, per_row - per_latent))[:, None],
            jnp.pad(segment_ids.astype(BF), (0, tags * per_row - rows)).reshape(tags, per_row).T,
            jnp.zeros((per_row, 125 - tags), BF),
        ],
        axis=1,
    )
    x_all = tree_gather(hidden_in)
    in_block = jnp.concatenate([w_qdown, w_key, w_value, extra], axis=1)
    qup_rows, out_rows, unit_rows = w_qup.shape[0], w_out.shape[0], w_down.shape[0]
    qn, units = fn // sn, dn * unit_rows

    def unit_columns(weight):
        return jnp.transpose(weight.reshape(per_row, dn, fn, unit_rows), (2, 0, 1, 3)).reshape(fn, per_row, units)

    unit_sent = jnp.stack([unit_columns(w_gate), unit_columns(w_up)], axis=1)
    qup_cols = jnp.transpose(w_qup.reshape(qup_rows, sn, heads, qn, HD), (3, 1, 0, 2, 4))
    qup_cols = exchange(qup_cols.reshape(fn, qup_rows, heads * HD), TREE)
    out_cols = spread_dp(w_out).reshape(sn, heads, out_rows, model)
    in_line = after(spread_line(in_block), qup_cols, unit_sent)
    qup_cols = spread_dp(qup_cols).reshape(latent_width, heads * HD)
    out_cols = jnp.swapaxes(exchange_share(out_cols), 0, 1).reshape(heads * HD, model)
    in_full = by_core(after(spread(in_line, "dp"), qup_cols, out_cols), 2).reshape(model, in_width + 128)
    w_in = in_full[:, :in_width]
    extra = in_full[:, in_width:].T.astype(F32)
    gain_one, gain_two = extra[0], extra[1]
    gain_latent = extra[2].reshape(dn * fn, per_row)[:, :per_latent].reshape(latent_width)
    run_labels = lax.dynamic_slice_in_dim(extra[3 : 3 + tags].reshape(tags, dn, fn, per_row), d_at, 1, 1)[:, 0]
    run_labels = jnp.swapaxes(run_labels, 0, 1).reshape(fn, tags * per_row)[:, :rows]
    run_labels = run_labels.reshape(tree_len)[::seg_len].astype(jnp.int32)

    cot = tree_gather(after(cotangent, x_all))

    labels = jnp.arange(NSEG, dtype=jnp.int32)
    reach = jnp.maximum(
        (labels[:, None] == labels[None, :]).astype(F32), (parents[0][:, None] == labels[None, :]).astype(F32)
    )
    for _ in range(5):
        reach = jnp.minimum(jnp.dot(reach, reach, precision=HIGHEST), 1.0)
    pick_run = (run_labels[:, None] == labels[None, :]).astype(F32)
    run_reach = jnp.dot(jnp.dot(pick_run, reach, precision=HIGHEST), pick_run.T, precision=HIGHEST)
    run_depth = jnp.sum(run_reach, axis=1) - 1.0
    run_bits = jnp.sum(jnp.where(run_reach > 0.5, jnp.left_shift(1, labels)[None, :], 0), axis=1).astype(jnp.int32)
    bits = jnp.broadcast_to(run_bits.reshape(5, 1, 4, 1), (5, heads, 4, seg_len)).reshape(5, 1, heads * 4 * seg_len)
    inverse = ROPE_BASE ** (-(jnp.arange(HD // 2, dtype=F32) * 2.0) / HD)
    coarse = (run_depth * seg_len)[:, None] * inverse[None, :]
    fine = jnp.arange(seg_len, dtype=F32)[:, None] * inverse[None, :]
    cos_a, sin_a = jnp.cos(coarse)[:, None, :], jnp.sin(coarse)[:, None, :]
    cos_b, sin_b = jnp.cos(fine)[None, :, :], jnp.sin(fine)[None, :, :]
    cosines = (cos_a * cos_b - sin_a * sin_b).reshape(tree_len, HD // 2)
    sines = (sin_a * cos_b + cos_a * sin_b).reshape(tree_len, HD // 2)

    query_all, key_all, value_all, latent_in = project(
        x_all, in_full, qup_cols, gain_one, gain_latent, cosines, sines, heads, block_rows
    )
    unit_cols = exchange(after(unit_sent, x_all), TREE)
    attended, lse = attention(bits, query_all, key_all, value_all, heads, seg_len)
    x = hidden_in.astype(F32)
    out_part = dot32(after(attended, cot, unit_cols), out_cols).astype(BF)
    gate_cols = spread(unit_cols[:, 0], "dp").reshape(model, units)
    up_cols = spread(after(unit_cols[:, 1], gate_cols), "dp").reshape(model, units)
    scale_one = rms_scale(x)
    normed_one = x * scale_one
    normed_in = (normed_one * gain_one).astype(BF)
    latent = dot32(after(normed_in, out_part), w_in[:, :latent_width])
    scale_latent = rms_scale(latent)

    def per_core(a, core):
        return at_index(a.reshape(a.shape[0], dn * zn, cn, per_row), core, 2).reshape(a.shape[0], dn * zn * per_row)

    normed_kept, normed_sent = per_core(normed_in, c_at), per_core(normed_in, 1 - c_at)
    mixed = x + after(tree_scatter(out_part), gate_cols, scale_latent, normed_kept, normed_sent)
    mixed = lax.optimization_barrier(mixed)
    down_rows = spread_dp(after(w_down, out_part)).reshape(units, model)

    scale_two = rms_scale(mixed)
    normed_two = mixed * scale_two
    normed_mid = (normed_two * gain_two).astype(BF)
    mid = after(tree_gather(normed_mid), down_rows, gate_cols, up_cols)
    activated, gate_grad, up_grad, mid_part = ffn(mid, cot, gate_cols, up_cols, down_rows, block_rows)
    gate_parts = unit_grads(after(mid, mid_part), gate_grad, dn)
    down_parts = dot_tn(after(activated, gate_parts), cot).astype(BF).reshape(dn, unit_rows, model)
    up_parts = unit_grads(after(mid, down_parts), up_grad, dn)
    gate_parts = exchange(gate_parts, "dp")
    down_parts = exchange(after(down_parts, gate_parts), "dp")
    mid_grad = after(tree_scatter(mid_part), down_parts, up_parts)
    up_parts = exchange(after(up_parts, down_parts), "dp")
    layer_part = dot32(after(activated, up_grad), down_rows).astype(BF)
    mixed_back = norm_back(mid_grad, normed_two, scale_two, gain_two)
    gain_two_cols = gain_column(mid_grad, normed_two, 1)
    mixed_grad = lax.optimization_barrier(cotangent.astype(F32) + mixed_back)
    branch_grad = mixed_grad.astype(BF)

    grad_down = jnp.sum(down_parts.astype(F32), axis=0)

    def unit_sum(parts):
        return jnp.sum(parts.astype(F32), axis=0).astype(BF).reshape(units, fn, per_row)

    unit_own = jnp.stack([unit_sum(gate_parts), unit_sum(up_parts)])
    unit_own = plain(jnp.transpose(unit_own, (2, 0, 3, 1)))
    branch, layer_part, gain_two_cols, unit_own, grad_down = lax.optimization_barrier(
        (tree_gather(branch_grad), layer_part, gain_two_cols, unit_own, grad_down)
    )
    unit_own = exchange(unit_own, TREE).reshape(fn, 2, per_row, dn, unit_rows)
    attended_grad = dot_nt(branch, out_cols).astype(BF)
    query_grad, key_part, value_part = attention_back(
        bits, lse, cosines, sines, query_all, key_all, value_all, attended, attended_grad, heads, seg_len
    )
    latent_part = dot_nt(query_grad, qup_cols).astype(BF)
    back_part = after(jnp.concatenate([latent_part, key_part, value_part], axis=1), unit_own)
    out_grads = jnp.swapaxes(
        dot_tn(attended, after(branch, back_part)).astype(BF).reshape(heads, sn, out_rows, model), 0, 1
    )
    out_grads = exchange_share(out_grads).reshape(dn, out_rows, model)
    grad_out = at_index(out_grads, d_at).astype(F32)
    for m in range(1, dn):
        grad_out = grad_out + over_dp(at_index(out_grads, d_at ^ m), m).astype(F32)
    grad_qup = dot_tn(latent_in, after(query_grad, back_part, out_grads))
    grad_qup = total(grad_qup.reshape(dn, fn * qup_rows, heads * HD), "dp").astype(BF)
    grad_qup = exchange(grad_qup.reshape(fn, qup_rows, heads * HD), TREE).reshape(qn, sn, qup_rows, heads, HD)
    unit_own = jnp.transpose(unit_own, (1, 2, 3, 0, 4)).reshape(2, per_row, dn * fn * unit_rows).astype(F32)
    back, grad_qup, grad_out, grad_gate, grad_up = lax.optimization_barrier(
        (tree_scatter(back_part), grad_qup, grad_out, plain(unit_own[0]), plain(unit_own[1]))
    )
    layer_out = (mixed + tree_scatter(after(layer_part, back))).astype(BF)
    grad_qup = jnp.transpose(grad_qup, (2, 1, 3, 0, 4)).reshape(qup_rows, H * HD).astype(F32)

    normed_latent = latent * scale_latent
    latent_back = norm_back(back[:, :latent_width], normed_latent, scale_latent, gain_latent)
    key_grad = rotate(back[:, latent_width : latent_width + HD], own_rows(cosines), -own_rows(sines))
    in_grad = jnp.concatenate([latent_back, key_grad, back[:, latent_width + HD :]], axis=1).astype(BF)

    in_own = other_core(dot_tn(normed_sent, in_grad).astype(BF)).astype(F32) + dot_tn(normed_kept, in_grad)
    in_own = in_own.astype(BF).reshape(dn, zn, per_row, in_width)
    in_parts = exchange(in_own, "dp")
    in_late, back_late, _ = lax.optimization_barrier((in_grad, back, in_own))
    normed_grad = dot_nt(in_late, w_in)
    input_back = norm_back(normed_grad, normed_one, scale_one, gain_one)
    grad_in = (mixed_grad + input_back).astype(BF)
    in_sum = total(jnp.sum(in_parts.astype(F32), axis=0), LINE)

    gain_cols = gain_column(back_late[:, :latent_width], normed_latent, 2).reshape(dn * fn, per_latent, 128)
    gain_cols = jnp.pad(gain_cols, ((0, 0), (0, per_row - per_latent), (0, 0))).reshape(model, 128)
    gain_cols = gain_cols + gain_two_cols + gain_column(normed_grad, normed_one, 0)
    gain_cols = gain_cols.reshape(dn, zn, cn, per_row, 128)
    gain_own = other_core(at_index(gain_cols, 1 - c_at, 2).astype(BF)).astype(F32) + at_index(gain_cols, c_at, 2)
    gain_own = after(gain_own, in_parts)
    gain_sum = at_index(gain_own, d_at)
    for m in range(1, dn):
        gain_sum = gain_sum + over_dp(at_index(gain_own, d_at ^ m).astype(BF), m).astype(F32)
    gain_line, z_at = gain_sum, lax.axis_index(LINE)
    gain_sum = at_index(gain_line, z_at)
    for m in range(1, zn):
        sent = at_index(gain_line, (z_at + m) % zn).astype(BF)
        gain_sum = gain_sum + lax.ppermute(sent, LINE, [(z, (z + m) % zn) for z in range(zn)]).astype(F32)
    return (
        layer_out,
        grad_in,
        gain_sum[:, 0],
        in_sum[:, :latent_width],
        gain_sum[:per_latent, 2],
        grad_qup,
        in_sum[:, latent_width : latent_width + HD],
        in_sum[:, latent_width + HD : in_width],
        grad_out,
        gain_sum[:, 1],
        grad_gate,
        grad_up,
        grad_down,
    )


def solution(mesh):
    dn, fn = mesh.shape["dp"], mesh.shape["fsdp"]
    share = dn * fn // H
    fine = jax.sharding.Mesh(mesh.devices.reshape(dn, fn // share, share // 2, 2), ("dp",) + TREE)
    split = P(("dp",) + TREE, None)
    line = P(("dp",) + TREE)
    placed = (
        split, line, P("dp", None), line, split, line, split, split, split, split, line, split, split, split, split,
    )
    given = (split, split, line, split, line, split, split, split, split, line, split, split, split)
    return jax.shard_map(body, mesh=fine, in_specs=placed, out_specs=given, check_vma=False)
```

time: 860 us -> 794 us (0.923)
  blocking collectives: 187 us -> 0 us
  waiting for transfers between devices: 171 us -> 305 us
  matrix products: 154 us -> 73 us
  Pallas kernels: 54.2 us -> 121 us
  starting transfers between devices: 63.6 us -> 104 us
  local copies, waits for them, and re-layouts: 136 us -> 101 us
    all_to_all x5 -> x0, blocking collectives: 187 us -> none  [exchange(): return lax.all_to_all(parts, axes, split_axis=0, concat_axis=0, tiled=True)]
    ppermute x6 -> x15, waiting for transfers between devices: 0.18 us -> 82.9 us  [over_dp(): return lax.ppermute(a, 'dp', [(d, d ^ m) for d in range(dn)])]
    pallas_call x0 -> x4, Pallas kernels: none -> 73.2 us  [the longest x1 36.7 us: ffn(): pl.pallas_call(ffn_kernel, grid=(count // rows,), out_shape=[jax.ShapeDty...]
    dot_general x6 -> x3, matrix products: 55.4 us -> 21.4 us  [dot32(): return jnp.dot(a, b, preferred_element_type=F32)]
    dot_general x6 -> x3, matrix products: 50.1 us -> 16.7 us  [dot_nt(): lax.dot_general(a, b, (((1,), (1,)), ((), ())), preferred_element_type=F32)]
    ppermute x0 -> x6, waiting for transfers between devices: none -> 23.4 us  [the longest x3 12.5 us: body(): lax.ppermute(sent, LINE, [(z, (z + m) % zn) for z in range(zn)]).astype(F32)]
    dot_general x7 -> x5, matrix products: 47.8 us -> 26.9 us  [dot_tn(): lax.dot_general(a, b, (((0,), (0,)), ((), ())), preferred_element_type=F32)]
    all_gather x4, waiting for transfers between devices: 26.8 us -> 47.1 us  [tree_gather(): return lax.all_gather(block, TREE, axis=0, tiled=True)]
  transfers between devices with their start and end apart: 28 -> 47, of which waited for: 13 -> 25; matrix products, arithmetic and copies ran while one was open for 32% -> 24% of each run, Pallas kernels for 6% -> 11%
where the time goes in v2:
time: 794 us; the launch traced here: 784 us
  waiting for transfers between devices  305 us (38%)
  Pallas kernels  121 us (15%)
  starting transfers between devices  104 us (13%)
  local copies, waits for them, and re-layouts  101 us (13%)
  matrix products  73 us (9%)
  other arithmetic  64.4 us (8%)
  between operations  15.6 us (2%)
    ppermute x15, waiting for transfers between devices, over_dp(): return lax.ppermute(a, 'dp', [(d, d ^ m) for d in range(dn)])  82.9 us
    all_to_all x13, waiting for transfers between devices, exchange(): return lax.all_to_all(parts, axes, split_axis=0, concat_axis=0, tiled=True)  74.4 us
    all_to_all x13, starting transfers between devices, exchange(): return lax.all_to_all(parts, axes, split_axis=0, concat_axis=0, tiled=True)  71 us
    reduce_scatter x4, waiting for transfers between devices, tree_scatter(): lax.psum_scatter(parts, TREE, scatter_dimension=0, tiled=True).astype(F32)  63.7 us
    all_gather x4, waiting for transfers between devices, tree_gather(): return lax.all_gather(block, TREE, axis=0, tiled=True)  47.1 us
    pallas_call x1, Pallas kernels, ffn(): pl.pallas_call(ffn_kernel, grid=(count // rows,), out_shape=[jax.ShapeDty...  36.7 us
    pallas_call x1, Pallas kernels, attention_back(): pl.pallas_call(functools.partial(attn_bwd_kernel, heads, seg_len), out_sh...  28.3 us
    dot_general x5, matrix products, dot_tn(): lax.dot_general(a, b, (((0,), (0,)), ((), ())), preferred_element_type=F32)  26.9 us
  transfers between devices with their start and end apart: 47, of which 25 were waited for; matrix products, arithmetic and copies ran while one was open for 24% of the time, Pallas kernels for 11%

profile of v2, /device:TPU:0, one launch (start us, length us, event | category | flops | bytes accessed | tf_op | source)
XLA Modules:
  0.0 784.3 jit_solution(2150154368540970144)
XLA Ops:
  12.2 5.1 collective-permute-start.2
  23.5 4.1 all-to-all-start
  45.4 7.3 collective-permute-done.1
  54.6 6.9 all-to-all-done
  63.6 4.8 all-to-all-start.1
  68.6 26.9 %all-gather.5.cloned.1.call-done.x_ref = bf16[1600,2048]{1,0:T(8,128)(2,1)} async-done(((bf16[200,2048]{1,0:T(8,128)(2,1)}), bf16[1600,2048]{1,0:T(8,128)(2,1)}) %all-gather.5.cloned.1.call-update) | async-done | bytes 6553616 | tf_op jit(solution)/shard_map/all_gather | solution.py:404
  103.8 7.8 collective-permute-done.3
  112.5 4.2 collective-permute-done.5
  120.7 5.2 collective-permute-done.10
  135.9 16.1 %all-to-all-start.2 = ((bf16[8,2,64,704]{3,2,1,0:T(8,128)(2,1)}), bf16[8,2,64,704]{3,2,1,0:T(8,128)(2,1)}, u32[]{:S(2)}, u32[]{:S(2)}) async-start(bf16[8,2,64,704]{3,2,1,0:T(8,128)(2,1)} %copy.108), calls=%async_computation.2 | async-start | bytes 3145728 | tf_op jit(solution)/shard_map/all_to_all | solution.py:370
  153.6 18.0 %project.1 = (bf16[1600,512]{1,0:T(8,128)(2,1)S(1)}, bf16[1600,256]{1,0:T(8,128)(2,1)S(1)}, bf16[1600,256]{1,0:T(8,128)(2,1)S(1)}, bf16[1600,1024]{1,0:T(8,128)(2,1)}) custom-call(bf16[1600,2048]{1,0:T(8,128)(2,1)} %all-gather.5.cloned.1.call-done.x_ref, bf16[2048,1664]{1,0:T(8,128)(2,1)} %bitcast.222, bf16[1024,512]{1,0:T(8,128)(2,1)S(1)} %bitcast.206, ...), custom_call_target="tpu_custom_call" | custom-call | flops 11744051200 | bytes 22815744 | tf_op jit(solution)/shard_map/project/pallas_call | solution.py:259
  171.6 19.8 %attn_fwd.1 = (bf16[1600,512]{1,0:T(8,128)(2,1)S(1)}, f32[5,1,640]{2,1,0:T(1,128)S(1)}) custom-call(s32[5,1,640]{2,1,0:T(1,128)S(1)} %reshape.315.bits_ref, bf16[1600,512]{1,0:T(8,128)(2,1)S(1)} %get-tuple-element.62.q_ref, bf16[1600,256]{1,0:T(8,128)(2,1)S(1)} %get-tuple-element.63.k_ref, bf16[1600,256]{1,0:T(8,128)(2,1)S(1)} %get-tuple-element.64.v_ref), custom_call_target="tpu_custom_call" | custom-call | flops 2621440000 | bytes 4915200 | tf_op jit(solution)/shard_map/attn_fwd/pallas_call | solution.py:190
  197.4 8.4 %convolution_convert_fusion.1 = bf16[1600,2048]{1,0:T(8,128)(2,1)} fusion(bf16[1600,512]{1,0:T(8,128)(2,1)} %copy-done, bf16[512,2048]{1,0:T(8,128)(2,1)} %bitcast.238), kind=kOutput, calls=%fused_computation.1 | convolution fusion | flops 3358720000 | bytes 10289152 | tf_op jit(solution)/shard_map/dot_general | solution.py:29
  210.2 4.7 all-to-all-start.3
  223.8 53.0 %reduce-scatter.5.cloned.1.call-done = bf16[200,2048]{1,0:T(8,128)(2,1)} async-done(((bf16[1600,2048]{1,0:T(8,128)(2,1)}), bf16[200,2048]{1,0:T(8,128)(2,1)}) %reduce-scatter.5.cloned.1.call-update) | async-done | bytes 819216 | tf_op jit(solution)/shard_map/reduce_scatter | solution.py:407
  288.2 4.7 all-to-all-start.4
  305.1 52.6 %collective-permute-done.12 = bf16[176,2048]{1,0:T(8,128)(2,1)S(1)} collective-permute-done((bf16[176,2048]{1,0:T(8,128)(2,1)}, bf16[176,2048]{1,0:T(8,128)(2,1)S(1)}, u32[]{:S(2)}, u32[]{:S(2)}) %collective-permute-start.12) | collective-permute-done | bytes 720928 | tf_op jit(solution)/shard_map/ppermute | solution.py:410
  359.5 36.7 %ffn.1 = (bf16[1600,704]{1,0:T(8,128)(2,1)S(1)}, bf16[1600,704]{1,0:T(8,128)(2,1)S(1)}, bf16[1600,704]{1,0:T(8,128)(2,1)}, bf16[1600,2048]{1,0:T(8,128)(2,1)}) custom-call(bf16[1600,2048]{1,0:T(8,128)(2,1)} %all-gather.9.cloned.1.call-done.mid_ref, bf16[1600,2048]{1,0:T(8,128)(2,1)} %all-gather.7.cloned.1.call-done.cot_ref, ...), custom_call_target="tpu_custom_call" | custom-call | flops 23068672000 | bytes 28311552 | tf_op jit(solution)/shard_map/ffn/pallas_call | solution.py:298
  400.8 9.3 %unit_grads.2 = bf16[4,704,512]{2,1,0:T(8,128)(2,1)} custom-call(bf16[1600,2048]{1,0:T(8,128)(2,1)} %all-gather.9.cloned.1.call-done.mid_ref, bf16[1600,704]{1,0:T(8,128)(2,1)S(1)} %copy-done.4), custom_call_target="tpu_custom_call" | custom-call | flops 4613734400 | bytes 9437184 | tf_op jit(solution)/shard_map/unit_grads/pallas_call | solution.py:324
  410.1 4.7 all-to-all-start.5
  414.8 9.6 %convolution_convert_fusion.4 = bf16[704,2048]{1,0:T(8,128)(2,1)} fusion(bf16[1600,704]{1,0:T(8,128)(2,1)} %copy-done.6, bf16[1600,2048]{1,0:T(8,128)(2,1)} %all-gather.7.cloned.1.call-done.cot_ref), kind=kOutput, calls=%fused_computation.15 | convolution fusion | flops 4615176192 | bytes 11689984 | tf_op jit(solution)/shard_map/dot_general | solution.py:37
  424.3 20.6 %all-to-all-done.5 = bf16[4,704,512]{2,1,0:T(8,128)(2,1)} async-done(((bf16[4,704,512]{2,1,0:T(8,128)(2,1)}), bf16[4,704,512]{2,1,0:T(8,128)(2,1)}, u32[]{:S(2)}, u32[]{:S(2)}) %all-to-all-start.5) | async-done | bytes 2883616 | tf_op jit(solution)/shard_map/all_to_all | solution.py:370
  444.9 4.7 all-to-all-start.6
  451.7 9.2 %unit_grads.3 = bf16[4,704,512]{2,1,0:T(8,128)(2,1)} custom-call(bf16[1600,2048]{1,0:T(8,128)(2,1)} %all-gather.9.cloned.1.call-done.mid_ref, bf16[1600,704]{1,0:T(8,128)(2,1)S(1)} %copy-done.2), custom_call_target="tpu_custom_call" | custom-call | flops 4613734400 | bytes 9437184 | tf_op jit(solution)/shard_map/unit_grads/pallas_call | solution.py:324
  461.0 10.3 %reduce-scatter.7.cloned.1.call-done = bf16[200,2048]{1,0:T(8,128)(2,1)} async-done(((bf16[1600,2048]{1,0:T(8,128)(2,1)}), bf16[200,2048]{1,0:T(8,128)(2,1)}) %reduce-scatter.7.cloned.1.call-update) | async-done | bytes 819216 | tf_op jit(solution)/shard_map/reduce_scatter | solution.py:407
  473.8 8.6 %all-to-all-done.6 = bf16[4,176,2048]{2,1,0:T(8,128)(2,1)} async-done(((bf16[4,176,2048]{2,1,0:T(8,128)(2,1)}), bf16[4,176,2048]{2,1,0:T(8,128)(2,1)}, u32[]{:S(2)}, u32[]{:S(2)}) %all-to-all-start.6) | async-done | bytes 2883616 | tf_op jit(solution)/shard_map/all_to_all | solution.py:370
  489.1 4.6 all-to-all-start.7
  493.7 9.4 %convolution_convert_fusion = bf16[1600,2048]{1,0:T(8,128)(2,1)} fusion(bf16[1600,704]{1,0:T(8,128)(2,1)} %copy-done.6, bf16[704,2048]{1,0:T(8,128)(2,1)} %bitcast.47.wd_ref), kind=kOutput, calls=%fused_computation | convolution fusion | flops 4617011200 | bytes 11689984 | tf_op jit(solution)/shard_map/dot_general | solution.py:29
  512.3 14.2 %all-to-all-done.7 = bf16[4,704,512]{2,1,0:T(8,128)(2,1)} async-done(((bf16[4,704,512]{2,1,0:T(8,128)(2,1)}), bf16[4,704,512]{2,1,0:T(8,128)(2,1)}, u32[]{:S(2)}, u32[]{:S(2)}) %all-to-all-start.7) | async-done | bytes 2883616 | tf_op jit(solution)/shard_map/all_to_all | solution.py:370
  534.9 4.3 fusion.16
  539.2 20.2 %all-gather.11.cloned.1.call-done = bf16[1600,2048]{1,0:T(8,128)(2,1)} async-done(((bf16[200,2048]{1,0:T(8,128)(2,1)}), bf16[1600,2048]{1,0:T(8,128)(2,1)}) %all-gather.11.cloned.1.call-update) | async-done | bytes 6553616 | tf_op jit(solution)/shard_map/all_gather | solution.py:404
  559.5 4.3 all-to-all-start.8
  564.0 8.3 %convolution_convert_fusion.6.da_ref = bf16[1600,512]{1,0:T(8,128)(2,1)} fusion(bf16[1600,2048]{1,0:T(8,128)(2,1)} %all-gather.11.cloned.1.call-done, bf16[512,2048]{1,0:T(8,128)(2,1)} %bitcast.239), kind=kOutput, calls=%fused_computation.17 | convolution fusion | flops 3356262400 | bytes 10289152 | tf_op jit(solution)/shard_map/dot_general | solution.py:33
  572.3 28.3 %attn_bwd.1 = (bf16[1600,512]{1,0:T(8,128)(2,1)}, bf16[1600,256]{1,0:T(8,128)(2,1)S(1)}, bf16[1600,256]{1,0:T(8,128)(2,1)S(1)}) custom-call(s32[5,1,640]{2,1,0:T(1,128)S(1)} %reshape.315.bits_ref, f32[5,1,640]{2,1,0:T(1,128)S(1)} %get-tuple-element.85.lse_ref, f32[1600,128]{1,0:T(8,128)S(1)} %bitcast.212, f32[1600,128]{1,0:T(8,128)S(1)} %bitcast.209, ...), custom_call_target="tpu_custom_call" | custom-call | flops 6553600000 | bytes 9830400 | tf_op jit(solution)/shard_map/attn_bwd/pallas_call | solution.py:209
  604.0 4.2 pad_maximum_fusion.1
  608.1 5.7 reshape.323
  615.3 7.1 convolution_convert_fusion.5
  631.5 3.9 all-to-all-start.9
  654.0 5.0 all-to-all-start.10
  661.7 11.4 %collective-permute-done.17 = bf16[128,2048]{1,0:T(8,128)(2,1)} collective-permute-done((bf16[128,2048]{1,0:T(8,128)(2,1)}, bf16[128,2048]{1,0:T(8,128)(2,1)}, u32[]{:S(2)}, u32[]{:S(2)}) %collective-permute-start.17) | collective-permute-done | bytes 524320 | tf_op jit(solution)/shard_map/ppermute | solution.py:410
  686.8 5.1 collective-permute-done.18
  691.9 4.6 add_convert_fusion
  696.5 5.1 all-to-all-start.11
  706.2 5.1 fusion.9
  716.9 21.4 %all-to-all-done.11 = bf16[4,4,64,1536]{3,2,1,0:T(8,128)(2,1)} async-done(((bf16[4,4,64,1536]{3,2,1,0:T(8,128)(2,1)}), bf16[4,4,64,1536]{3,2,1,0:T(8,128)(2,1)}, u32[]{:S(2)}, u32[]{:S(2)}) %all-to-all-start.11) | async-done | bytes 3145760 | tf_op jit(solution)/shard_map/all_to_all | solution.py:370
  746.1 4.6 all-to-all-start.12
  759.7 8.0 %collective-permute-done.23 = bf16[64,128]{0,1:T(8,128)(2,1)S(1)} collective-permute-done((bf16[64,128]{0,1:T(8,128)(2,1)S(1)}, bf16[64,128]{0,1:T(8,128)(2,1)S(1)}, u32[]{:S(2)}, u32[]{:S(2)}) %collective-permute-start.23) | collective-permute-done | bytes 16416 | tf_op jit(solution)/shard_map/ppermute | solution.py:585
  767.6 4.5 collective-permute-done.24
  (317 shorter events, 216.5 us)
Async XLA Ops:
  7.2 88.3 %all-gather.5.cloned.1.call-start = ((), (), s32[]{:S(2)}) async-start(), calls=%async_computation.17 | async-start | bytes 7372800 | tf_op jit(solution)/shard_map/all_gather | solution.py:404
  12.2 41.5 %collective-permute-start.2 = (bf16[64,1664]{1,0:T(8,128)(2,1)S(1)}, bf16[64,1664]{1,0:T(8,128)(2,1)}, u32[]{:S(2)}, u32[]{:S(2)}) collective-permute-start(bf16[64,1664]{1,0:T(8,128)(2,1)S(1)} %concatenate.10), channel_id=1, source_target_pairs={{0,6},{2,0},{4,2},{6,4},{1,7},{3,1},{5,3},{7,5},{8,14},{10,8},{12,... | collective-permute-start | bytes 638984 | tf_op jit(solution)/shard_map/ppermute | solution.py:423
  17.3 35.4 %collective-permute-start.1 = (bf16[64,1664]{1,0:T(8,128)(2,1)S(1)}, bf16[64,1664]{1,0:T(8,128)(2,1)}, u32[]{:S(2)}, u32[]{:S(2)}) collective-permute-start(bf16[64,1664]{1,0:T(8,128)(2,1)S(1)} %concatenate.10), channel_id=1, source_target_pairs={{0,4},{2,6},{4,0},{6,2},{1,5},{3,7},{5,1},{7,3},{8,12},{10,14},{12... | collective-permute-start | bytes 638984 | tf_op jit(solution)/shard_map/ppermute | solution.py:423
  17.3 25.8 %collective-permute-start = (bf16[64,1664]{1,0:T(8,128)(2,1)S(1)}, bf16[64,1664]{1,0:T(8,128)(2,1)}, u32[]{:S(2)}, u32[]{:S(2)}) collective-permute-start(bf16[64,1664]{1,0:T(8,128)(2,1)S(1)} %concatenate.10), channel_id=1, source_target_pairs={{0,2},{2,4},{4,6},{6,0},{1,3},{3,5},{5,7},{7,1},{8,10},{10,12},{12... | collective-permute-start | bytes 638984 | tf_op jit(solution)/shard_map/ppermute | solution.py:423
  18.3 77.2 %collective-permute-start.6 = (bf16[128,2048]{1,0:T(8,128)(2,1)}, bf16[128,2048]{1,0:T(8,128)(2,1)}, u32[]{:S(2)}, u32[]{:S(2)}) collective-permute-start(bf16[128,2048]{1,0:T(8,128)(2,1)} %param.24), channel_id=1, source_target_pairs={{0,8},{8,0},{16,24},{24,16},{1,9},{9,1},{17,25},{25,17},{2,10},{10... | collective-permute-start | bytes 1572872 | tf_op jit(solution)/shard_map/ppermute | solution.py:410
  19.8 77.9 %collective-permute-start.8 = (bf16[128,2048]{1,0:T(8,128)(2,1)}, bf16[128,2048]{1,0:T(8,128)(2,1)}, u32[]{:S(2)}, u32[]{:S(2)}) collective-permute-start(bf16[128,2048]{1,0:T(8,128)(2,1)} %param.24), channel_id=1, source_target_pairs={{0,24},{8,16},{16,8},{24,0},{1,25},{9,17},{17,9},{25,1},{2,26},{10... | collective-permute-start | bytes 1572872 | tf_op jit(solution)/shard_map/ppermute | solution.py:410
  23.5 38.0 %all-to-all-start = ((bf16[8,32,512]{2,1,0:T(8,128)(2,1)}), bf16[8,32,512]{2,1,0:T(8,128)(2,1)S(1)}, u32[]{:S(2)}, u32[]{:S(2)}) async-start(bf16[8,32,512]{2,1,0:T(8,128)(2,1)} %reshape.305), calls=%async_computation | async-start | bytes 524288 | tf_op jit(solution)/shard_map/all_to_all | solution.py:370
  43.1 53.5 %collective-permute-start.7 = (bf16[128,2048]{1,0:T(8,128)(2,1)}, bf16[128,2048]{1,0:T(8,128)(2,1)}, u32[]{:S(2)}, u32[]{:S(2)}) collective-permute-start(bf16[128,2048]{1,0:T(8,128)(2,1)} %param.24), channel_id=1, source_target_pairs={{0,16},{8,24},{16,0},{24,8},{1,17},{9,25},{17,1},{25,9},{2,18},{10... | collective-permute-start | bytes 1572872 | tf_op jit(solution)/shard_map/ppermute | solution.py:410
  63.6 56.1 %all-to-all-start.1 = ((bf16[4,4,64,1664]{3,2,1,0:T(8,128)(2,1)}), bf16[4,4,64,1664]{3,2,1,0:T(8,128)(2,1)}, u32[]{:S(2)}, u32[]{:S(2)}) async-start(bf16[4,4,64,1664]{3,2,1,0:T(8,128)(2,1)} %broadcast_in_dim.143), calls=%async_computation.1 | async-start | bytes 6815744 | tf_op jit(solution)/shard_map/all_to_all | solution.py:370
  68.4 129.1 %all-gather.7.cloned.1.call-start = ((), (), s32[]{:S(2)}) async-start(), calls=%async_computation.18 | async-start | bytes 7372800 | tf_op jit(solution)/shard_map/all_gather | solution.py:404
  99.9 16.8 %collective-permute-start.9 = (bf16[2,128,2048]{2,1,0:T(8,128)(2,1)}, bf16[2,128,2048]{2,1,0:T(8,128)(2,1)}, u32[]{:S(2)}, u32[]{:S(2)}) collective-permute-start(bf16[2,128,2048]{2,1,0:T(8,128)(2,1)} %dynamic-slice_bitcast_fusion.1), channel_id=1, source_target_pairs={{0,1},{1,0},{2,3},{3,2},{4,5},{5,4},{6,7},{7,6},{8,9},{9,8},{10,11... | collective-permute-start | bytes 3145736 | tf_op jit(solution)/shard_map/ppermute | solution.py:379
  100.2 11.4 %collective-permute-start.3 = (bf16[8,32,512]{2,1,0:T(8,128)(2,1)S(1)}, bf16[8,32,512]{2,1,0:T(8,128)(2,1)S(1)}, u32[]{:S(2)}, u32[]{:S(2)}) collective-permute-start(bf16[8,32,512]{2,1,0:T(8,128)(2,1)S(1)} %all-to-all-done), channel_id=1, source_target_pairs={{0,8},{8,0},{16,24},{24,16},{1,9},{9,1},{17,25},{25,17},{2,10},{10... | collective-permute-start | bytes 786440 | tf_op jit(solution)/shard_map/ppermute | solution.py:410
  101.6 15.0 %collective-permute-start.5 = (bf16[8,32,512]{2,1,0:T(8,128)(2,1)S(1)}, bf16[8,32,512]{2,1,0:T(8,128)(2,1)S(1)}, u32[]{:S(2)}, u32[]{:S(2)}) collective-permute-start(bf16[8,32,512]{2,1,0:T(8,128)(2,1)S(1)} %all-to-all-done), channel_id=1, source_target_pairs={{0,24},{8,16},{16,8},{24,0},{1,25},{9,17},{17,9},{25,1},{2,26},{10... | collective-permute-start | bytes 786440 | tf_op jit(solution)/shard_map/ppermute | solution.py:410
  103.1 9.3 %collective-permute-start.4 = (bf16[8,32,512]{2,1,0:T(8,128)(2,1)S(1)}, bf16[8,32,512]{2,1,0:T(8,128)(2,1)S(1)}, u32[]{:S(2)}, u32[]{:S(2)}) collective-permute-start(bf16[8,32,512]{2,1,0:T(8,128)(2,1)S(1)} %all-to-all-done), channel_id=1, source_target_pairs={{0,16},{8,24},{16,0},{24,8},{1,17},{9,25},{17,1},{25,9},{2,18},{10... | collective-permute-start | bytes 786440 | tf_op jit(solution)/shard_map/ppermute | solution.py:410
  119.7 6.2 collective-permute-start.10
  135.9 61.5 %all-to-all-start.2 = ((bf16[8,2,64,704]{3,2,1,0:T(8,128)(2,1)}), bf16[8,2,64,704]{3,2,1,0:T(8,128)(2,1)}, u32[]{:S(2)}, u32[]{:S(2)}) async-start(bf16[8,2,64,704]{3,2,1,0:T(8,128)(2,1)} %copy.108), calls=%async_computation.2 | async-start | bytes 3145728 | tf_op jit(solution)/shard_map/all_to_all | solution.py:370
  152.0 124.8 %reduce-scatter.5.cloned.1.call-start = ((), (), s32[]{:S(2)}) async-start(), calls=%async_computation.19 | async-start | bytes 7372800 | tf_op jit(solution)/shard_map/reduce_scatter | solution.py:407
  210.2 69.1 %all-to-all-start.3 = ((bf16[4,8,64,704]{3,2,1,0:T(8,128)(2,1)}), bf16[4,8,64,704]{3,2,1,0:T(8,128)(2,1)}, u32[]{:S(2)}, u32[]{:S(2)}) async-start(bf16[4,8,64,704]{3,2,1,0:T(8,128)(2,1)} %broadcast_in_dim.159), calls=%async_computation.4 | async-start | bytes 6291456 | tf_op jit(solution)/shard_map/all_to_all | solution.py:370
  214.9 144.7 %all-gather.9.cloned.1.call-start = ((), (), s32[]{:S(2)}) async-start(), calls=%async_computation.20 | async-start | bytes 7372800 | tf_op jit(solution)/shard_map/all_gather | solution.py:404
  283.5 19.5 %collective-permute-start.11 = (bf16[176,2048]{1,0:T(8,128)(2,1)}, bf16[176,2048]{1,0:T(8,128)(2,1)}, u32[]{:S(2)}, u32[]{:S(2)}) collective-permute-start(bf16[176,2048]{1,0:T(8,128)(2,1)} %param.28), channel_id=1, source_target_pairs={{0,8},{8,0},{16,24},{24,16},{1,9},{9,1},{17,25},{25,17},{2,10},{10... | collective-permute-start | bytes 2162696 | tf_op jit(solution)/shard_map/ppermute | solution.py:410
  288.2 71.3 %all-to-all-start.4 = ((bf16[4,8,64,704]{3,2,1,0:T(8,128)(2,1)}), bf16[4,8,64,704]{3,2,1,0:T(8,128)(2,1)}, u32[]{:S(2)}, u32[]{:S(2)}) async-start(bf16[4,8,64,704]{3,2,1,0:T(8,128)(2,1)} %broadcast_in_dim.165), calls=%async_computation.5 | async-start | bytes 6291456 | tf_op jit(solution)/shard_map/all_to_all | solution.py:370
  293.0 178.3 %reduce-scatter.7.cloned.1.call-start = ((), (), s32[]{:S(2)}) async-start(), calls=%async_computation.21 | async-start | bytes 7372800 | tf_op jit(solution)/shard_map/reduce_scatter | solution.py:407
  293.2 65.4 %collective-permute-start.13 = (bf16[176,2048]{1,0:T(8,128)(2,1)}, bf16[176,2048]{1,0:T(8,128)(2,1)S(1)}, u32[]{:S(2)}, u32[]{:S(2)}) collective-permute-start(bf16[176,2048]{1,0:T(8,128)(2,1)} %param.28), channel_id=1, source_target_pairs={{0,24},{8,16},{16,8},{24,0},{1,25},{9,17},{17,9},{25,1},{2,26},{10... | collective-permute-start | bytes 2162696 | tf_op jit(solution)/shard_map/ppermute | solution.py:410
  296.1 61.5 %collective-permute-start.12 = (bf16[176,2048]{1,0:T(8,128)(2,1)}, bf16[176,2048]{1,0:T(8,128)(2,1)S(1)}, u32[]{:S(2)}, u32[]{:S(2)}) collective-permute-start(bf16[176,2048]{1,0:T(8,128)(2,1)} %param.28), channel_id=1, source_target_pairs={{0,16},{8,24},{16,0},{24,8},{1,17},{9,25},{17,1},{25,9},{2,18},{10... | collective-permute-start | bytes 2162696 | tf_op jit(solution)/shard_map/ppermute | solution.py:410
  410.1 34.8 %all-to-all-start.5 = ((bf16[4,704,512]{2,1,0:T(8,128)(2,1)}), bf16[4,704,512]{2,1,0:T(8,128)(2,1)}, u32[]{:S(2)}, u32[]{:S(2)}) async-start(bf16[4,704,512]{2,1,0:T(8,128)(2,1)} %unit_grads.2), calls=%async_computation.7 | async-start | bytes 5767168 | tf_op jit(solution)/shard_map/all_to_all | solution.py:370
  444.9 37.5 %all-to-all-start.6 = ((bf16[4,176,2048]{2,1,0:T(8,128)(2,1)}), bf16[4,176,2048]{2,1,0:T(8,128)(2,1)}, u32[]{:S(2)}, u32[]{:S(2)}) async-start(bf16[4,176,2048]{2,1,0:T(8,128)(2,1)} %bitcast.237), calls=%async_computation.8 | async-start | bytes 5767168 | tf_op jit(solution)/shard_map/all_to_all | solution.py:370
  449.6 109.9 %all-gather.11.cloned.1.call-start = ((), (), s32[]{:S(2)}) async-start(), calls=%async_computation.22 | async-start | bytes 7372800 | tf_op jit(solution)/shard_map/all_gather | solution.py:404
  489.1 37.4 %all-to-all-start.7 = ((bf16[4,704,512]{2,1,0:T(8,128)(2,1)}), bf16[4,704,512]{2,1,0:T(8,128)(2,1)}, u32[]{:S(2)}, u32[]{:S(2)}) async-start(bf16[4,704,512]{2,1,0:T(8,128)(2,1)} %unit_grads.3), calls=%async_computation.9 | async-start | bytes 5767168 | tf_op jit(solution)/shard_map/all_to_all | solution.py:370
  559.5 48.7 %all-to-all-start.8 = ((bf16[8,2,64,704]{3,2,1,0:T(8,128)(2,1)}), bf16[8,2,64,704]{3,2,1,0:T(8,128)(2,1)}, u32[]{:S(2)}, u32[]{:S(2)}) async-start(bf16[8,2,64,704]{3,2,1,0:T(8,128)(2,1)} %maximum_bitcast_fusion), calls=%async_computation.10 | async-start | bytes 3145728 | tf_op jit(solution)/shard_map/all_to_all | solution.py:370
  563.7 112.6 %reduce-scatter.9.cloned.1.call-start = ((), (), s32[]{:S(2)}) async-start(), calls=%async_computation.23 | async-start | bytes 5529600 | tf_op jit(solution)/shard_map/reduce_scatter | solution.py:407
  622.5 2.7 collective-permute-start.14
  631.5 21.6 %all-to-all-start.9 = ((bf16[4,256,512]{2,1,0:T(8,128)(2,1)}), bf16[4,256,512]{2,1,0:T(8,128)(2,1)S(1)}, u32[]{:S(2)}, u32[]{:S(2)}) async-start(bf16[4,256,512]{2,1,0:T(8,128)(2,1)} %bitcast.240), calls=%async_computation.12 | async-start | bytes 2097152 | tf_op jit(solution)/shard_map/all_to_all | solution.py:370
  638.1 23.7 %collective-permute-start.15 = (bf16[128,2048]{1,0:T(8,128)(2,1)}, bf16[128,2048]{1,0:T(8,128)(2,1)}, u32[]{:S(2)}, u32[]{:S(2)}) collective-permute-start(bf16[128,2048]{1,0:T(8,128)(2,1)} %get-tuple-element.117), channel_id=1, source_target_pairs={{0,8},{8,0},{16,24},{24,16},{1,9},{9,1},{17,25},{25,17},{2,10},{10... | collective-permute-start | bytes 1572872 | tf_op jit(solution)/shard_map/ppermute | solution.py:410
  640.0 33.0 %collective-permute-start.17 = (bf16[128,2048]{1,0:T(8,128)(2,1)}, bf16[128,2048]{1,0:T(8,128)(2,1)}, u32[]{:S(2)}, u32[]{:S(2)}) collective-permute-start(bf16[128,2048]{1,0:T(8,128)(2,1)} %get-tuple-element.118), channel_id=1, source_target_pairs={{0,24},{8,16},{16,8},{24,0},{1,25},{9,17},{17,9},{25,1},{2,26},{10... | collective-permute-start | bytes 1572872 | tf_op jit(solution)/shard_map/ppermute | solution.py:410
  641.5 31.6 %collective-permute-start.16 = (bf16[128,2048]{1,0:T(8,128)(2,1)S(1)}, bf16[128,2048]{1,0:T(8,128)(2,1)}, u32[]{:S(2)}, u32[]{:S(2)}) collective-permute-start(bf16[128,2048]{1,0:T(8,128)(2,1)S(1)} %get-tuple-element.119), channel_id=1, source_target_pairs={{0,16},{8,24},{16,0},{24,8},{1,17},{9,25},{17,1},{25,9},{2,18},{10... | collective-permute-start | bytes 1572872 | tf_op jit(solution)/shard_map/ppermute | solution.py:410
  654.0 21.9 %all-to-all-start.10 = ((bf16[8,32,512]{2,1,0:T(8,128)(2,1)}), bf16[8,32,512]{2,1,0:T(8,128)(2,1)S(1)}, u32[]{:S(2)}, u32[]{:S(2)}) async-start(bf16[8,32,512]{2,1,0:T(8,128)(2,1)} %bitcast.64), calls=%async_computation.13 | async-start | bytes 524288 | tf_op jit(solution)/shard_map/all_to_all | solution.py:370
  659.0 115.8 %reduce-scatter.11.cloned.1.call-start = ((), (), s32[]{:S(2)}) async-start(), calls=%async_computation.24 | async-start | bytes 7372800 | tf_op jit(solution)/shard_map/reduce_scatter | solution.py:407
  685.9 6.0 collective-permute-start.18
  696.5 41.8 %all-to-all-start.11 = ((bf16[4,4,64,1536]{3,2,1,0:T(8,128)(2,1)}), bf16[4,4,64,1536]{3,2,1,0:T(8,128)(2,1)}, u32[]{:S(2)}, u32[]{:S(2)}) async-start(bf16[4,4,64,1536]{3,2,1,0:T(8,128)(2,1)} %bitcast.70), calls=%async_computation.15 | async-start | bytes 6291456 | tf_op jit(solution)/shard_map/all_to_all | solution.py:370
  713.6 2.1 collective-permute-start.19
  716.9 25.7 %copy-start.29 = (f32[4,4,64,128]{2,3,1,0:T(8,128)}, f32[4,4,64,128]{2,3,1,0:T(8,128)S(1)}, u32[]{:S(2)}) copy-start(f32[4,4,64,128]{2,3,1,0:T(8,128)S(1)} %bitcast_add_fusion) | copy-start | bytes 1572868
  739.1 11.6 %collective-permute-start.20 = (bf16[4,64,128]{1,2,0:T(8,128)(2,1)}, bf16[4,64,128]{1,2,0:T(8,128)(2,1)S(1)}, u32[]{:S(2)}, u32[]{:S(2)}) collective-permute-start(bf16[4,64,128]{1,2,0:T(8,128)(2,1)} %get-tuple-element.122), channel_id=1, source_target_pairs={{0,8},{8,0},{16,24},{24,16},{1,9},{9,1},{17,25},{25,17},{2,10},{10... | collective-permute-start | bytes 196616 | tf_op jit(solution)/shard_map/ppermute | solution.py:410
  740.5 10.2 %collective-permute-start.22 = (bf16[4,64,128]{1,2,0:T(8,128)(2,1)}, bf16[4,64,128]{1,2,0:T(8,128)(2,1)S(1)}, u32[]{:S(2)}, u32[]{:S(2)}) collective-permute-start(bf16[4,64,128]{1,2,0:T(8,128)(2,1)} %get-tuple-element.123), channel_id=1, source_target_pairs={{0,24},{8,16},{16,8},{24,0},{1,25},{9,17},{17,9},{25,1},{2,26},{10... | collective-permute-start | bytes 196616 | tf_op jit(solution)/shard_map/ppermute | solution.py:410
  742.0 8.7 %collective-permute-start.21 = (bf16[4,64,128]{1,2,0:T(8,128)(2,1)}, bf16[4,64,128]{1,2,0:T(8,128)(2,1)}, u32[]{:S(2)}, u32[]{:S(2)}) collective-permute-start(bf16[4,64,128]{1,2,0:T(8,128)(2,1)} %get-tuple-element.124), channel_id=1, source_target_pairs={{0,16},{8,24},{16,0},{24,8},{1,17},{9,25},{17,1},{25,9},{2,18},{10... | collective-permute-start | bytes 196616 | tf_op jit(solution)/shard_map/ppermute | solution.py:410
  746.1 27.2 %all-to-all-start.12 = ((bf16[4,64,1536]{2,1,0:T(8,128)(2,1)}), bf16[4,64,1536]{2,1,0:T(8,128)(2,1)S(1)}, u32[]{:S(2)}, u32[]{:S(2)}) async-start(bf16[4,64,1536]{2,1,0:T(8,128)(2,1)} %reduce_sum.150), calls=%async_computation.16 | async-start | bytes 1572864 | tf_op jit(solution)/shard_map/all_to_all | solution.py:370
  751.8 15.8 %collective-permute-start.23 = (bf16[64,128]{0,1:T(8,128)(2,1)S(1)}, bf16[64,128]{0,1:T(8,128)(2,1)S(1)}, u32[]{:S(2)}, u32[]{:S(2)}) collective-permute-start(bf16[64,128]{0,1:T(8,128)(2,1)S(1)} %get-tuple-element.132), channel_id=1, source_target_pairs={{0,2},{2,4},{4,6},{6,0},{1,3},{3,5},{5,7},{7,1},{8,10},{10,12},{12... | collective-permute-start | bytes 49160 | tf_op jit(solution)/shard_map/ppermute | solution.py:585
  753.9 13.7 %collective-permute-start.25 = (bf16[64,128]{0,1:T(8,128)(2,1)S(1)}, bf16[64,128]{0,1:T(8,128)(2,1)S(1)}, u32[]{:S(2)}, u32[]{:S(2)}) collective-permute-start(bf16[64,128]{0,1:T(8,128)(2,1)S(1)} %get-tuple-element.133), channel_id=1, source_target_pairs={{0,6},{2,0},{4,2},{6,4},{1,7},{3,1},{5,3},{7,5},{8,14},{10,8},{12,... | collective-permute-start | bytes 49160 | tf_op jit(solution)/shard_map/ppermute | solution.py:585
  755.8 16.4 %collective-permute-start.24 = (bf16[64,128]{0,1:T(8,128)(2,1)S(1)}, bf16[64,128]{0,1:T(8,128)(2,1)S(1)}, u32[]{:S(2)}, u32[]{:S(2)}) collective-permute-start(bf16[64,128]{0,1:T(8,128)(2,1)S(1)} %get-tuple-element.134), channel_id=1, source_target_pairs={{0,4},{2,6},{4,0},{6,2},{1,5},{3,7},{5,1},{7,3},{8,12},{10,14},{12... | collective-permute-start | bytes 49160 | tf_op jit(solution)/shard_map/ppermute | solution.py:585
  (43 other events, 155.8 us)
Sparse Core Ops, SparseCore 0:
  9.7 85.7 all-gather.4
  97.1 75.6 all-gather.6
  206.0 70.7 reduce-scatter.4
  283.7 65.2 all-gather.8
  399.3 71.9 reduce-scatter.6
  489.2 70.1 all-gather.10
  614.0 62.3 reduce-scatter.8
  678.7 71.0 reduce-scatter.10

commit v3 on v2

--- a/solution.py
+++ b/solution.py
@@ -18,11 +18,11 @@
 NEGATIVE = -1e30
 BF = jnp.bfloat16
 F32 = jnp.float32
-CHUNK = 160
+CHUNK = 320
 TREE = ("q", "r", "c")
 LINE = ("q", "r")
 SHARE = ("r", "c")
-VMEM_LIMIT = 48 * 1024 * 1024
+VMEM_LIMIT = 56 * 1024 * 1024
 
 
 def dot32(a, b):
@@ -84,7 +84,7 @@
     return tile * tile_rows + lax.rem(lane, tile_rows)
 
 
-def attn_fwd_kernel(heads, seg_len, bits_ref, q_ref, k_ref, v_ref, att_ref, lse_ref, qs, st):
+def attn_fwd_kernel(heads, seg_len, bits_ref, q_ref, k_ref, v_ref, wo_ref, att_ref, lse_ref, part_ref, qs, st):
     tile_rows = 4 * seg_len
     width = heads * tile_rows
     per_tile = tile_rows // CHUNK
@@ -120,16 +120,23 @@
         total, out = lax.fori_loop(0, count, gather, (jnp.zeros((1, width), F32), jnp.zeros((HD, width), F32)))
         lse_ref[tile] = top + jnp.log(total)
         out = (out * (1.0 / total)).T.astype(BF)
+        here = pl.ds(q0, tile_rows)
+        part = None
         for h in range(heads):
-            att_ref[pl.ds(q0, tile_rows), h * HD : (h + 1) * HD] = out[h * tile_rows : (h + 1) * tile_rows, :]
+            cols = slice(h * HD, (h + 1) * HD)
+            own = out[h * tile_rows : (h + 1) * tile_rows, :]
+            att_ref[here, cols] = own
+            more = dot32(own, wo_ref[cols, :])
+            part = more if part is None else part + more
+        part_ref[here, :] = part.astype(BF)
         return carry
 
     lax.fori_loop(0, 5, one_tile, 0)
 
 
 def attn_bwd_kernel(
-    heads, seg_len, bits_ref, lse_ref, cos_ref, sin_ref, q_ref, k_ref, v_ref, att_ref, da_ref,
-    dq_ref, dk_ref, dv_ref, qs, das, dk, dv,
+    heads, seg_len, bits_ref, lse_ref, cos_ref, sin_ref, q_ref, k_ref, v_ref, att_ref, branch_ref, wo_ref, wq_ref,
+    dq_ref, back_ref, qs, das, dk, dv,
 ):
     tile_rows = 4 * seg_len
     width = heads * tile_rows
@@ -146,7 +153,7 @@
             cols = slice(h * HD, (h + 1) * HD)
             here = pl.ds(q0, tile_rows)
             qs[rows, :] = (q_ref[here, cols].astype(F32) * scale).astype(BF)
-            grad = da_ref[here, cols]
+            grad = dot_nt(branch_ref[here, :], wo_ref[cols, :]).astype(BF)
             das[rows, :] = grad
             both = grad.astype(F32) * att_ref[here, cols].astype(F32)
             deltas.append(jnp.sum(both.T, axis=0, keepdims=True))
@@ -173,17 +180,24 @@
         acc = lax.fori_loop(free, count, functools.partial(step, True), acc)
         out = (acc * scale).T
         at = pl.ds(q0, tile_rows)
+        latent = None
         for h in range(heads):
+            cols = slice(h * HD, (h + 1) * HD)
             grad = out[h * tile_rows : (h + 1) * tile_rows, :]
-            dq_ref[at, h * HD : (h + 1) * HD] = rotate(grad, cos_ref[at, :], -sin_ref[at, :]).astype(BF)
+            grad = rotate(grad, cos_ref[at, :], -sin_ref[at, :]).astype(BF)
+            dq_ref[at, cols] = grad
+            more = dot_nt(grad, wq_ref[:, cols])
+            latent = more if latent is None else latent + more
+        back_ref[at, :latent_width] = latent.astype(BF)
         return carry
 
+    latent_width = wq_ref.shape[0]
     lax.fori_loop(0, 5, one_tile, 0)
-    dk_ref[...] = dk[...].astype(BF)
-    dv_ref[...] = dv[...].astype(BF)
-
-
-def attention(bits, q, k, v, heads, seg_len):
+    back_ref[:, latent_width : latent_width + HD] = dk[...].astype(BF)
+    back_ref[:, latent_width + HD :] = dv[...].astype(BF)
+
+
+def attention(bits, q, k, v, out_cols, heads, seg_len):
     tree_len = q.shape[0]
     width = heads * 4 * seg_len
     work = heads * tree_len * tree_len // 2
@@ -192,17 +206,18 @@
         out_shape=(
             jax.ShapeDtypeStruct((tree_len, heads * HD), BF),
             jax.ShapeDtypeStruct((5, 1, width), F32),
+            jax.ShapeDtypeStruct((tree_len, out_cols.shape[1]), BF),
         ),
-        in_specs=[pl.BlockSpec(memory_space=pltpu.VMEM)] * 4,
-        out_specs=(pl.BlockSpec(memory_space=pltpu.VMEM),) * 2,
+        in_specs=[pl.BlockSpec(memory_space=pltpu.VMEM)] * 5,
+        out_specs=(pl.BlockSpec(memory_space=pltpu.VMEM),) * 3,
         scratch_shapes=[pltpu.VMEM((width, HD), BF), pltpu.VMEM((16 * seg_len, width), F32)],
         compiler_params=pltpu.CompilerParams(vmem_limit_bytes=VMEM_LIMIT),
-        cost_estimate=pl.CostEstimate(flops=4 * HD * work, bytes_accessed=6 * tree_len * HD * 2, transcendentals=work),
+        cost_estimate=pl.CostEstimate(flops=6 * HD * work, bytes_accessed=6 * tree_len * HD * 2, transcendentals=work),
         name="attn_fwd",
-    )(bits, q, k, v)
-
-
-def attention_back(bits, lse, cosines, sines, q, k, v, attended, da, heads, seg_len):
+    )(bits, q, k, v, out_cols)
+
+
+def attention_back(bits, lse, cosines, sines, q, k, v, attended, branch, out_cols, qup_cols, heads, seg_len):
     tree_len = q.shape[0]
     width = heads * 4 * seg_len
     work = heads * tree_len * tree_len // 2
@@ -210,11 +225,10 @@
         functools.partial(attn_bwd_kernel, heads, seg_len),
         out_shape=(
             jax.ShapeDtypeStruct((tree_len, heads * HD), BF),
-            jax.ShapeDtypeStruct((tree_len, HD), BF),
-            jax.ShapeDtypeStruct((tree_len, HD), BF),
+            jax.ShapeDtypeStruct((tree_len, qup_cols.shape[0] + 2 * HD), BF),
         ),
-        in_specs=[pl.BlockSpec(memory_space=pltpu.VMEM)] * 9,
-        out_specs=(pl.BlockSpec(memory_space=pltpu.VMEM),) * 3,
+        in_specs=[pl.BlockSpec(memory_space=pltpu.VMEM)] * 11,
+        out_specs=(pl.BlockSpec(memory_space=pltpu.VMEM),) * 2,
         scratch_shapes=[
             pltpu.VMEM((width, HD), BF),
             pltpu.VMEM((width, HD), BF),
@@ -222,9 +236,9 @@
             pltpu.VMEM((tree_len, HD), F32),
         ],
         compiler_params=pltpu.CompilerParams(vmem_limit_bytes=VMEM_LIMIT),
-        cost_estimate=pl.CostEstimate(flops=10 * HD * work, bytes_accessed=12 * tree_len * HD * 2, transcendentals=work),
+        cost_estimate=pl.CostEstimate(flops=14 * HD * work, bytes_accessed=12 * tree_len * HD * 2, transcendentals=work),
         name="attn_bwd",
-    )(bits, lse, cosines, sines, q, k, v, attended, da)
+    )(bits, lse, cosines, sines, q, k, v, attended, branch, out_cols, qup_cols)
 
 
 def whole(shape):
@@ -447,10 +461,10 @@
     qup_cols = jnp.transpose(w_qup.reshape(qup_rows, sn, heads, qn, HD), (3, 1, 0, 2, 4))
     qup_cols = exchange(qup_cols.reshape(fn, qup_rows, heads * HD), TREE)
     out_cols = spread_dp(w_out).reshape(sn, heads, out_rows, model)
-    in_line = after(spread_line(in_block), qup_cols, unit_sent)
-    qup_cols = spread_dp(qup_cols).reshape(latent_width, heads * HD)
-    out_cols = jnp.swapaxes(exchange_share(out_cols), 0, 1).reshape(heads * HD, model)
-    in_full = by_core(after(spread(in_line, "dp"), qup_cols, out_cols), 2).reshape(model, in_width + 128)
+    in_line = after(spread_line(in_block), qup_cols, unit_sent, out_cols)
+    in_wide = spread(in_line, "dp")
+    qup_cols = spread(after(qup_cols, in_wide), "dp").reshape(latent_width, heads * HD)
+    in_full = by_core(in_wide, 2).reshape(model, in_width + 128)
     w_in = in_full[:, :in_width]
     extra = in_full[:, in_width:].T.astype(F32)
     gain_one, gain_two = extra[0], extra[1]
@@ -483,12 +497,13 @@
     query_all, key_all, value_all, latent_in = project(
         x_all, in_full, qup_cols, gain_one, gain_latent, cosines, sines, heads, block_rows
     )
-    unit_cols = exchange(after(unit_sent, x_all), TREE)
-    attended, lse = attention(bits, query_all, key_all, value_all, heads, seg_len)
+    unit_cols = exchange(after(unit_sent, x_all, qup_cols), TREE)
+    out_cols = jnp.swapaxes(exchange_share(after(out_cols, key_all)), 0, 1).reshape(heads * HD, model)
+    attended, lse, out_part = attention(bits, query_all, key_all, value_all, out_cols, heads, seg_len)
     x = hidden_in.astype(F32)
-    out_part = dot32(after(attended, cot, unit_cols), out_cols).astype(BF)
+    out_part = after(out_part, cot, unit_cols)
     gate_cols = spread(unit_cols[:, 0], "dp").reshape(model, units)
-    up_cols = spread(after(unit_cols[:, 1], gate_cols), "dp").reshape(model, units)
+    up_cols = spread(after(unit_cols[:, 1], out_part), "dp").reshape(model, units)
     scale_one = rms_scale(x)
     normed_one = x * scale_one
     normed_in = (normed_one * gain_one).astype(BF)
@@ -499,9 +514,9 @@
         return at_index(a.reshape(a.shape[0], dn * zn, cn, per_row), core, 2).reshape(a.shape[0], dn * zn * per_row)
 
     normed_kept, normed_sent = per_core(normed_in, c_at), per_core(normed_in, 1 - c_at)
-    mixed = x + after(tree_scatter(out_part), gate_cols, scale_latent, normed_kept, normed_sent)
+    down_rows = spread(after(w_down, gate_cols), "dp").reshape(units, model)
+    mixed = x + after(tree_scatter(out_part), gate_cols, down_rows, scale_latent, normed_kept, normed_sent)
     mixed = lax.optimization_barrier(mixed)
-    down_rows = spread_dp(after(w_down, out_part)).reshape(units, model)
 
     scale_two = rms_scale(mixed)
     normed_two = mixed * scale_two
@@ -512,9 +527,9 @@
     down_parts = dot_tn(after(activated, gate_parts), cot).astype(BF).reshape(dn, unit_rows, model)
     up_parts = unit_grads(after(mid, down_parts), up_grad, dn)
     gate_parts = exchange(gate_parts, "dp")
-    down_parts = exchange(after(down_parts, gate_parts), "dp")
-    mid_grad = after(tree_scatter(mid_part), down_parts, up_parts)
-    up_parts = exchange(after(up_parts, down_parts), "dp")
+    mid_grad = after(tree_scatter(mid_part), gate_parts, down_parts, up_parts)
+    up_parts = exchange(after(up_parts, gate_parts), "dp")
+    down_parts = exchange(after(down_parts, up_parts), "dp")
     layer_part = dot32(after(activated, up_grad), down_rows).astype(BF)
     mixed_back = norm_back(mid_grad, normed_two, scale_two, gain_two)
     gain_two_cols = gain_column(mid_grad, normed_two, 1)
@@ -532,12 +547,10 @@
         (tree_gather(branch_grad), layer_part, gain_two_cols, unit_own, grad_down)
     )
     unit_own = exchange(unit_own, TREE).reshape(fn, 2, per_row, dn, unit_rows)
-    attended_grad = dot_nt(branch, out_cols).astype(BF)
-    query_grad, key_part, value_part = attention_back(
-        bits, lse, cosines, sines, query_all, key_all, value_all, attended, attended_grad, heads, seg_len
-    )
-    latent_part = dot_nt(query_grad, qup_cols).astype(BF)
-    back_part = after(jnp.concatenate([latent_part, key_part, value_part], axis=1), unit_own)
+    query_grad, back_part = attention_back(
+        bits, lse, cosines, sines, query_all, key_all, value_all, attended, branch, out_cols, qup_cols, heads, seg_len
+    )
+    back_part = after(back_part, unit_own)
     out_grads = jnp.swapaxes(
         dot_tn(attended, after(branch, back_part)).astype(BF).reshape(heads, sn, out_rows, model), 0, 1
     )
@@ -567,14 +580,15 @@
     normed_grad = dot_nt(in_late, w_in)
     input_back = norm_back(normed_grad, normed_one, scale_one, gain_one)
     grad_in = (mixed_grad + input_back).astype(BF)
-    in_sum = total(jnp.sum(in_parts.astype(F32), axis=0), LINE)
+    in_line_parts = jnp.sum(in_parts.astype(F32), axis=0).astype(BF)
+    in_sum = total(in_line_parts, LINE)
 
     gain_cols = gain_column(back_late[:, :latent_width], normed_latent, 2).reshape(dn * fn, per_latent, 128)
     gain_cols = jnp.pad(gain_cols, ((0, 0), (0, per_row - per_latent), (0, 0))).reshape(model, 128)
     gain_cols = gain_cols + gain_two_cols + gain_column(normed_grad, normed_one, 0)
     gain_cols = gain_cols.reshape(dn, zn, cn, per_row, 128)
     gain_own = other_core(at_index(gain_cols, 1 - c_at, 2).astype(BF)).astype(F32) + at_index(gain_cols, c_at, 2)
-    gain_own = after(gain_own, in_parts)
+    gain_own = after(gain_own, in_line_parts)
     gain_sum = at_index(gain_own, d_at)
     for m in range(1, dn):
         gain_sum = gain_sum + over_dp(at_index(gain_own, d_at ^ m).astype(BF), m).astype(F32)

time: 794 us -> 771 us (0.971)
  blocking collectives: 0 us -> 118 us
  waiting for transfers between devices: 305 us -> 209 us
  matrix products: 73 us -> 52.2 us
  local copies, waits for them, and re-layouts: 101 us -> 80.8 us
  starting transfers between devices: 104 us -> 88.2 us
  Pallas kernels: 121 us -> 133 us
    all_to_all x0 -> x3, blocking collectives: none -> 118 us  [exchange(): return lax.all_to_all(parts, axes, split_axis=0, concat_axis=0, tiled=True)]
    ppermute x15 -> x9, waiting for transfers between devices: 82.9 us -> 18.9 us  [over_dp(): return lax.ppermute(a, 'dp', [(d, d ^ m) for d in range(dn)])]
    all_to_all x13 -> x12, waiting for transfers between devices: 74.4 us -> 49.8 us  [exchange(): return lax.all_to_all(parts, axes, split_axis=0, concat_axis=0, tiled=True)]
    unnamed x91 -> x61, local copies, waits for them, and re-layouts: 22.7 us -> 8.5 us
    dot_general x3 -> x1, matrix products: 16.7 us -> 5.03 us  [dot_nt(): lax.dot_general(a, b, (((1,), (1,)), ((), ())), preferred_element_type=F32)]
    ppermute x15 -> x9, starting transfers between devices: 19.8 us -> 11.3 us  [over_dp(): return lax.ppermute(a, 'dp', [(d, d ^ m) for d in range(dn)])]
    dot_general x3 -> x2, matrix products: 21.4 us -> 13 us  [dot32(): return jnp.dot(a, b, preferred_element_type=F32)]
    all_to_all x13 -> x12, starting transfers between devices: 71 us -> 65.7 us  [exchange(): return lax.all_to_all(parts, axes, split_axis=0, concat_axis=0, tiled=True)]
  transfers between devices with their start and end apart: 47 -> 40, of which waited for: 25 -> 22; matrix products, arithmetic and copies ran while one was open for 24% -> 23% of each run, Pallas kernels for 11% -> 13%
where the time goes in v3:
time: 771 us; the launch traced here: 762 us
  waiting for transfers between devices  209 us (27%)
  Pallas kernels  133 us (17%)
  blocking collectives  118 us (15%)
  starting transfers between devices  88.2 us (11%)
  local copies, waits for them, and re-layouts  80.8 us (10%)
  other arithmetic  66.4 us (9%)
  matrix products  52.2 us (7%)
  between operations  15.4 us (2%)
    all_to_all x3, blocking collectives, exchange(): return lax.all_to_all(parts, axes, split_axis=0, concat_axis=0, tiled=True)  118 us
    all_to_all x12, starting transfers between devices, exchange(): return lax.all_to_all(parts, axes, split_axis=0, concat_axis=0, tiled=True)  65.7 us
    reduce_scatter x4, waiting for transfers between devices, tree_scatter(): lax.psum_scatter(parts, TREE, scatter_dimension=0, tiled=True).astype(F32)  56.3 us
    all_gather x4, waiting for transfers between devices, tree_gather(): return lax.all_gather(block, TREE, axis=0, tiled=True)  52.2 us
    all_to_all x12, waiting for transfers between devices, exchange(): return lax.all_to_all(parts, axes, split_axis=0, concat_axis=0, tiled=True)  49.8 us
    pallas_call x1, Pallas kernels, ffn(): pl.pallas_call(ffn_kernel, grid=(count // rows,), out_shape=[jax.ShapeDty...  36.6 us
    pallas_call x1, Pallas kernels, attention_back(): pl.pallas_call(functools.partial(attn_bwd_kernel, heads, seg_len), out_sh...  33.4 us
    dot_general x5, matrix products, dot_tn(): lax.dot_general(a, b, (((0,), (0,)), ((), ())), preferred_element_type=F32)  27.5 us
  transfers between devices with their start and end apart: 40, of which 22 were waited for; matrix products, arithmetic and copies ran while one was open for 23% of the time, Pallas kernels for 13%

profile of v3, /device:TPU:0, one launch (start us, length us, event | category | flops | bytes accessed | tf_op | source)
XLA Modules:
  0.0 761.7 jit_solution(15128311759986535498)
XLA Ops:
  12.2 5.1 collective-permute-start.2
  23.5 4.1 all-to-all-start
  38.4 4.7 collective-permute-done
  45.4 7.3 collective-permute-done.1
  56.9 4.6 all-to-all-done
  63.6 3.9 all-to-all-start.1
  67.6 27.8 %all-gather.5.cloned.1.call-done.x_ref = bf16[1600,2048]{1,0:T(8,128)(2,1)} async-done(((bf16[200,2048]{1,0:T(8,128)(2,1)}), bf16[1600,2048]{1,0:T(8,128)(2,1)}) %all-gather.5.cloned.1.call-update) | async-done | bytes 6553616 | tf_op jit(solution)/shard_map/all_gather | solution.py:418
  95.5 8.2 %all-to-all-done.1 = bf16[4,4,64,1664]{3,2,1,0:T(8,128)(2,1)S(1)} async-done(((bf16[4,4,64,1664]{3,2,1,0:T(8,128)(2,1)}), bf16[4,4,64,1664]{3,2,1,0:T(8,128)(2,1)S(1)}, u32[]{:S(2)}, u32[]{:S(2)}) %all-to-all-start.1) | async-done | bytes 3407904 | tf_op jit(solution)/shard_map/all_to_all | solution.py:384
  106.8 4.4 all-to-all-start.2
  111.3 4.3 select_bitcast_fusion.1
  128.1 16.3 %all-to-all-start.3 = ((bf16[8,2,64,704]{3,2,1,0:T(8,128)(2,1)}), bf16[8,2,64,704]{3,2,1,0:T(8,128)(2,1)}, u32[]{:S(2)}, u32[]{:S(2)}) async-start(bf16[8,2,64,704]{3,2,1,0:T(8,128)(2,1)} %copy.108), calls=%async_computation.3 | async-start | bytes 3145728 | tf_op jit(solution)/shard_map/all_to_all | solution.py:384
  144.5 19.1 %project.1 = (bf16[1600,512]{1,0:T(8,128)(2,1)}, bf16[1600,256]{1,0:T(8,128)(2,1)}, bf16[1600,256]{1,0:T(8,128)(2,1)}, bf16[1600,1024]{1,0:T(8,128)(2,1)}) custom-call(bf16[1600,2048]{1,0:T(8,128)(2,1)} %all-gather.5.cloned.1.call-done.x_ref, bf16[2048,1664]{1,0:T(8,128)(2,1)} %bitcast.201, bf16[1024,512]{1,0:T(8,128)(2,1)} %bitcast.23.qup_ref.wq_ref, ...), custom_call_target="tpu_custom_call" | custom-call | flops 11744051200 | bytes 22815744 | tf_op jit(solution)/shard_map/project/pallas_call | solution.py:273
  169.7 23.3 %attn_fwd.1 = (bf16[1600,512]{1,0:T(8,128)(2,1)}, f32[5,1,640]{2,1,0:T(1,128)}, bf16[1600,2048]{1,0:T(8,128)(2,1)}) custom-call(s32[5,1,640]{2,1,0:T(1,128)} %reshape.311.bits_ref, bf16[1600,512]{1,0:T(8,128)(2,1)} %get-tuple-element.63.q_ref, bf16[1600,256]{1,0:T(8,128)(2,1)} %get-tuple-element.64.k_ref, bf16[1600,256]{1,0:T(8,128)(2,1)} %get-tuple-element.65.v_ref, ...), custom_call_target="tpu_custom_call" | custom-call | flops 3932160000 | bytes 4915200 | tf_op jit(solution)/shard_map/attn_fwd/pallas_call | solution.py:204
  193.0 4.4 all-to-all-done.3
  199.3 40.6 %all_to_all.75 = bf16[4,8,64,704]{3,2,1,0:T(8,128)(2,1)} all-to-all(bf16[4,8,64,704]{3,2,1,0:T(8,128)(2,1)S(1)} %broadcast_in_dim.135), channel_id=1, replica_groups=mesh['dp'=4,'q'=4,'r'=1,'c'=2] {'dp'}, dimensions={0} | all-to-all | bytes 5767168 | tf_op jit(solution)/shard_map/all_to_all | solution.py:384
  241.8 4.8 all-to-all-start.5
  248.7 19.7 %reduce-scatter.5.cloned.1.call-done = bf16[200,2048]{1,0:T(8,128)(2,1)} async-done(((bf16[1600,2048]{1,0:T(8,128)(2,1)}), bf16[200,2048]{1,0:T(8,128)(2,1)}) %reduce-scatter.5.cloned.1.call-update) | async-done | bytes 819216 | tf_op jit(solution)/shard_map/reduce_scatter | solution.py:421
  270.8 8.0 %all-to-all-done.5 = bf16[4,176,2048]{2,1,0:T(8,128)(2,1)} async-done(((bf16[4,176,2048]{2,1,0:T(8,128)(2,1)}), bf16[4,176,2048]{2,1,0:T(8,128)(2,1)}, u32[]{:S(2)}, u32[]{:S(2)}) %all-to-all-start.5) | async-done | bytes 2883616 | tf_op jit(solution)/shard_map/all_to_all | solution.py:384
  282.2 39.6 %all_to_all.76 = bf16[4,8,64,704]{3,2,1,0:T(8,128)(2,1)} all-to-all(bf16[4,8,64,704]{3,2,1,0:T(8,128)(2,1)S(1)} %broadcast_in_dim.137), channel_id=1, replica_groups=mesh['dp'=4,'q'=4,'r'=1,'c'=2] {'dp'}, dimensions={0} | all-to-all | bytes 5767168 | tf_op jit(solution)/shard_map/all_to_all | solution.py:384
  321.8 24.4 %all-gather.9.cloned.1.call-done.mid_ref = bf16[1600,2048]{1,0:T(8,128)(2,1)} async-done(((bf16[200,2048]{1,0:T(8,128)(2,1)}), bf16[1600,2048]{1,0:T(8,128)(2,1)}) %all-gather.9.cloned.1.call-update) | async-done | bytes 6553616 | tf_op jit(solution)/shard_map/all_gather | solution.py:418
  346.2 36.6 %ffn.1 = (bf16[1600,704]{1,0:T(8,128)(2,1)}, bf16[1600,704]{1,0:T(8,128)(2,1)}, bf16[1600,704]{1,0:T(8,128)(2,1)}, bf16[1600,2048]{1,0:T(8,128)(2,1)}) custom-call(bf16[1600,2048]{1,0:T(8,128)(2,1)} %all-gather.9.cloned.1.call-done.mid_ref, bf16[1600,2048]{1,0:T(8,128)(2,1)} %all-gather.7.cloned.1.call-done.cot_ref, bf16[2048,704]{1,0:T(8,128)(2,1)} %bitcast.214, ...), custom_call_target="tpu_custom_call" | custom-call | flops 23068672000 | bytes 28311552 | tf_op jit(solution)/shard_map/ffn/pallas_call | solution.py:312
  382.9 10.1 %unit_grads.2 = bf16[4,704,512]{2,1,0:T(8,128)(2,1)} custom-call(bf16[1600,2048]{1,0:T(8,128)(2,1)} %all-gather.9.cloned.1.call-done.mid_ref, bf16[1600,704]{1,0:T(8,128)(2,1)} %get-tuple-element.77.grad_ref), custom_call_target="tpu_custom_call" | custom-call | flops 4613734400 | bytes 9437184 | tf_op jit(solution)/shard_map/unit_grads/pallas_call | solution.py:338
  392.9 4.6 all-to-all-start.7
  397.6 9.6 %convolution_convert_fusion.2 = bf16[704,2048]{1,0:T(8,128)(2,1)} fusion(bf16[1600,704]{1,0:T(8,128)(2,1)} %get-tuple-element.83, bf16[1600,2048]{1,0:T(8,128)(2,1)} %all-gather.7.cloned.1.call-done.cot_ref), kind=kOutput, calls=%fused_computation.12 | convolution fusion | flops 4615176192 | bytes 11689984 | tf_op jit(solution)/shard_map/dot_general | solution.py:37
  407.2 10.1 %unit_grads.3 = bf16[4,704,512]{2,1,0:T(8,128)(2,1)} custom-call(bf16[1600,2048]{1,0:T(8,128)(2,1)} %all-gather.9.cloned.1.call-done.mid_ref, bf16[1600,704]{1,0:T(8,128)(2,1)} %get-tuple-element.81.grad_ref), custom_call_target="tpu_custom_call" | custom-call | flops 4613734400 | bytes 9437184 | tf_op jit(solution)/shard_map/unit_grads/pallas_call | solution.py:338
  417.3 36.7 %reduce-scatter.7.cloned.1.call-done = bf16[200,2048]{1,0:T(8,128)(2,1)} async-done(((bf16[1600,2048]{1,0:T(8,128)(2,1)}), bf16[200,2048]{1,0:T(8,128)(2,1)}) %reduce-scatter.7.cloned.1.call-update) | async-done | bytes 819216 | tf_op jit(solution)/shard_map/reduce_scatter | solution.py:421
  461.3 37.4 %all_to_all.77 = bf16[4,704,512]{2,1,0:T(8,128)(2,1)} all-to-all(bf16[4,704,512]{2,1,0:T(8,128)(2,1)} %unit_grads.3), channel_id=1, replica_groups=mesh['dp'=4,'q'=4,'r'=1,'c'=2] {'dp'}, dimensions={0} | all-to-all | bytes 5767168 | tf_op jit(solution)/shard_map/all_to_all | solution.py:384
  498.7 4.6 all-to-all-start.9
  503.4 9.4 %convolution_convert_fusion = bf16[1600,2048]{1,0:T(8,128)(2,1)} fusion(bf16[1600,704]{1,0:T(8,128)(2,1)} %get-tuple-element.83, bf16[704,2048]{1,0:T(8,128)(2,1)} %bitcast.36.wd_ref), kind=kOutput, calls=%fused_computation | convolution fusion | flops 4617011200 | bytes 11689984 | tf_op jit(solution)/shard_map/dot_general | solution.py:29
  525.6 8.0 %all-to-all-done.9 = bf16[4,176,2048]{2,1,0:T(8,128)(2,1)} async-done(((bf16[4,176,2048]{2,1,0:T(8,128)(2,1)}), bf16[4,176,2048]{2,1,0:T(8,128)(2,1)}, u32[]{:S(2)}, u32[]{:S(2)}) %all-to-all-start.9) | async-done | bytes 2883616 | tf_op jit(solution)/shard_map/all_to_all | solution.py:384
  533.6 3.7 convert_reduce_fusion
  540.2 7.3 all-to-all-start.10
  547.7 33.4 %attn_bwd.1 = (bf16[1600,512]{1,0:T(8,128)(2,1)}, bf16[1600,1536]{1,0:T(8,128)(2,1)}) custom-call(s32[5,1,640]{2,1,0:T(1,128)} %reshape.311.bits_ref, f32[5,1,640]{2,1,0:T(1,128)} %get-tuple-element.87.lse_ref, f32[1600,128]{1,0:T(8,128)} %bitcast.228, f32[1600,128]{1,0:T(8,128)} %bitcast.225, bf16[1600,512]{1,0:T(8,128)(2,1)} %get-tuple-element.63.q_ref, ...), custom_call_target="tpu_custom_call" | custom-call | flops 9175040000 | bytes 9830400 | tf_op jit(solution)/shard_map/attn_bwd/pallas_call | solution.py:224
  581.1 4.3 all-to-all-done.10
  585.5 5.7 reshape.321
  591.2 7.4 convolution_convert_fusion.3
  607.7 3.7 all-to-all-start.11
  633.5 4.4 collective-permute-done.9
  637.8 11.3 %collective-permute-done.11 = bf16[128,2048]{1,0:T(8,128)(2,1)} collective-permute-done((bf16[128,2048]{1,0:T(8,128)(2,1)}, bf16[128,2048]{1,0:T(8,128)(2,1)}, u32[]{:S(2)}, u32[]{:S(2)}) %collective-permute-start.11) | collective-permute-done | bytes 524320 | tf_op jit(solution)/shard_map/ppermute | solution.py:424
  655.1 3.6 multiply_reduce_fusion.3
  665.0 4.0 collective-permute-done.12
  669.0 4.8 add_convert_fusion
  673.8 4.9 all-to-all-start.13
  684.7 5.0 fusion.9
  703.3 12.2 %all-to-all-done.13 = bf16[4,4,64,1536]{3,2,1,0:T(8,128)(2,1)} async-done(((bf16[4,4,64,1536]{3,2,1,0:T(8,128)(2,1)}), bf16[4,4,64,1536]{3,2,1,0:T(8,128)(2,1)}, u32[]{:S(2)}, u32[]{:S(2)}) %all-to-all-start.13) | async-done | bytes 3145760 | tf_op jit(solution)/shard_map/all_to_all | solution.py:384
  732.2 3.8 collective-permute-start.19
  739.3 5.7 collective-permute-done.17
  745.0 4.7 collective-permute-done.18
  (264 shorter events, 174.5 us)
Async XLA Ops:
  7.2 20.4 %copy-start.20 = (bf16[64,5632]{1,0:T(8,128)(2,1)S(1)}, bf16[64,5632]{1,0:T(8,128)(2,1)}, u32[]{:S(2)}) copy-start(bf16[64,5632]{1,0:T(8,128)(2,1)} %param.26) | copy-start | bytes 2162692
  7.2 88.3 %all-gather.5.cloned.1.call-start = ((), (), s32[]{:S(2)}) async-start(), calls=%async_computation.19 | async-start | bytes 7372800 | tf_op jit(solution)/shard_map/all_gather | solution.py:418
  12.2 41.5 %collective-permute-start.2 = (bf16[64,1664]{1,0:T(8,128)(2,1)S(1)}, bf16[64,1664]{1,0:T(8,128)(2,1)}, u32[]{:S(2)}, u32[]{:S(2)}) collective-permute-start(bf16[64,1664]{1,0:T(8,128)(2,1)S(1)} %concatenate.7), channel_id=1, source_target_pairs={{0,6},{2,0},{4,2},{6,4},{1,7},{3,1},{5,3},{7,5},{8,14},{10,8},{12,... | collective-permute-start | bytes 638984 | tf_op jit(solution)/shard_map/ppermute | solution.py:437
  17.3 35.4 %collective-permute-start.1 = (bf16[64,1664]{1,0:T(8,128)(2,1)S(1)}, bf16[64,1664]{1,0:T(8,128)(2,1)}, u32[]{:S(2)}, u32[]{:S(2)}) collective-permute-start(bf16[64,1664]{1,0:T(8,128)(2,1)S(1)} %concatenate.7), channel_id=1, source_target_pairs={{0,4},{2,6},{4,0},{6,2},{1,5},{3,7},{5,1},{7,3},{8,12},{10,14},{12... | collective-permute-start | bytes 638984 | tf_op jit(solution)/shard_map/ppermute | solution.py:437
  17.3 25.8 %collective-permute-start = (bf16[64,1664]{1,0:T(8,128)(2,1)S(1)}, bf16[64,1664]{1,0:T(8,128)(2,1)}, u32[]{:S(2)}, u32[]{:S(2)}) collective-permute-start(bf16[64,1664]{1,0:T(8,128)(2,1)S(1)} %concatenate.7), channel_id=1, source_target_pairs={{0,2},{2,4},{4,6},{6,0},{1,3},{3,5},{5,7},{7,1},{8,10},{10,12},{12... | collective-permute-start | bytes 638984 | tf_op jit(solution)/shard_map/ppermute | solution.py:437
  18.3 36.4 %collective-permute-start.3 = (bf16[128,2048]{1,0:T(8,128)(2,1)}, bf16[128,2048]{1,0:T(8,128)(2,1)}, u32[]{:S(2)}, u32[]{:S(2)}) collective-permute-start(bf16[128,2048]{1,0:T(8,128)(2,1)} %param.24), channel_id=1, source_target_pairs={{0,8},{8,0},{16,24},{24,16},{1,9},{9,1},{17,25},{25,17},{2,10},{10... | collective-permute-start | bytes 1572872 | tf_op jit(solution)/shard_map/ppermute | solution.py:424
  19.8 36.0 %collective-permute-start.5 = (bf16[128,2048]{1,0:T(8,128)(2,1)}, bf16[128,2048]{1,0:T(8,128)(2,1)}, u32[]{:S(2)}, u32[]{:S(2)}) collective-permute-start(bf16[128,2048]{1,0:T(8,128)(2,1)} %param.24), channel_id=1, source_target_pairs={{0,24},{8,16},{16,8},{24,0},{1,25},{9,17},{17,9},{25,1},{2,26},{10... | collective-permute-start | bytes 1572872 | tf_op jit(solution)/shard_map/ppermute | solution.py:424
  23.5 38.0 %all-to-all-start = ((bf16[8,32,512]{2,1,0:T(8,128)(2,1)}), bf16[8,32,512]{2,1,0:T(8,128)(2,1)S(1)}, u32[]{:S(2)}, u32[]{:S(2)}) async-start(bf16[8,32,512]{2,1,0:T(8,128)(2,1)} %reshape.303), calls=%async_computation | async-start | bytes 524288 | tf_op jit(solution)/shard_map/all_to_all | solution.py:384
  38.3 17.5 %copy-start.12 = (bf16[8,2,64,704]{3,2,0,1:T(8,128)(2,1)}, bf16[8,2,64,704]{3,2,0,1:T(8,128)(2,1)S(1)}, u32[]{:S(2)}) copy-start(bf16[8,2,64,704]{3,2,0,1:T(8,128)(2,1)S(1)} %constant_dynamic-update-slice_fusion) | copy-start | bytes 4325380
  43.1 12.6 %collective-permute-start.4 = (bf16[128,2048]{1,0:T(8,128)(2,1)S(1)}, bf16[128,2048]{1,0:T(8,128)(2,1)S(1)}, u32[]{:S(2)}, u32[]{:S(2)}) collective-permute-start(bf16[128,2048]{1,0:T(8,128)(2,1)S(1)} %copy-done.24), channel_id=1, source_target_pairs={{0,16},{8,24},{16,0},{24,8},{1,17},{9,25},{17,1},{25,9},{2,18},{10... | collective-permute-start | bytes 1572872 | tf_op jit(solution)/shard_map/ppermute | solution.py:424
  56.9 6.7 copy-start.4
  63.6 40.1 %copy-start.26 = (s32[1,20]{1,0:T(1,128)S(1)}, s32[1,20]{1,0:T(1,128)}, u32[]{:S(2)}) copy-start(s32[1,20]{1,0:T(1,128)} %param.17) | copy-start | bytes 244
  63.6 40.1 %all-to-all-start.1 = ((bf16[4,4,64,1664]{3,2,1,0:T(8,128)(2,1)}), bf16[4,4,64,1664]{3,2,1,0:T(8,128)(2,1)S(1)}, u32[]{:S(2)}, u32[]{:S(2)}) async-start(bf16[4,4,64,1664]{3,2,1,0:T(8,128)(2,1)} %broadcast_in_dim.128), calls=%async_computation.1 | async-start | bytes 6815744 | tf_op jit(solution)/shard_map/all_to_all | solution.py:384
  67.6 129.8 %all-gather.7.cloned.1.call-start = ((), (), s32[]{:S(2)}) async-start(), calls=%async_computation.20 | async-start | bytes 7372800 | tf_op jit(solution)/shard_map/all_gather | solution.py:418
  103.7 7.6 collective-permute-start.6
  106.8 20.0 %all-to-all-start.2 = ((bf16[4,8,32,512]{3,2,1,0:T(8,128)(2,1)}), bf16[4,8,32,512]{3,2,1,0:T(8,128)(2,1)}, u32[]{:S(2)}, u32[]{:S(2)}) async-start(bf16[4,8,32,512]{3,2,1,0:T(8,128)(2,1)} %broadcast_in_dim.133), calls=%async_computation.2 | async-start | bytes 2097152 | tf_op jit(solution)/shard_map/all_to_all | solution.py:384
  128.1 69.3 %all-to-all-start.3 = ((bf16[8,2,64,704]{3,2,1,0:T(8,128)(2,1)}), bf16[8,2,64,704]{3,2,1,0:T(8,128)(2,1)}, u32[]{:S(2)}, u32[]{:S(2)}) async-start(bf16[8,2,64,704]{3,2,1,0:T(8,128)(2,1)} %copy.108), calls=%async_computation.3 | async-start | bytes 3145728 | tf_op jit(solution)/shard_map/all_to_all | solution.py:384
  144.4 123.9 %reduce-scatter.5.cloned.1.call-start = ((), (), s32[]{:S(2)}) async-start(), calls=%async_computation.21 | async-start | bytes 7372800 | tf_op jit(solution)/shard_map/reduce_scatter | solution.py:421
  144.5 19.1 %copy-start.5 = (bf16[4,128,2048]{2,1,0:T(8,128)(2,1)S(1)}, bf16[4,128,2048]{2,1,0:T(8,128)(2,1)}, u32[]{:S(2)}) copy-start(bf16[4,128,2048]{2,1,0:T(8,128)(2,1)} %copy-done.4) | copy-start | bytes 6291460
  163.7 3.0 collective-permute-start.7
  199.2 40.6 %copy-start.22 = (bf16[176,2048]{1,0:T(8,128)(2,1)S(1)}, bf16[176,2048]{1,0:T(8,128)(2,1)}, u32[]{:S(2)}) copy-start(bf16[176,2048]{1,0:T(8,128)(2,1)} %param.28) | copy-start | bytes 2162692
  241.8 37.1 %all-to-all-start.5 = ((bf16[4,176,2048]{2,1,0:T(8,128)(2,1)}), bf16[4,176,2048]{2,1,0:T(8,128)(2,1)}, u32[]{:S(2)}, u32[]{:S(2)}) async-start(bf16[4,176,2048]{2,1,0:T(8,128)(2,1)} %broadcast_in_dim.136), calls=%async_computation.6 | async-start | bytes 5767168 | tf_op jit(solution)/shard_map/all_to_all | solution.py:384
  246.5 99.7 %all-gather.9.cloned.1.call-start = ((), (), s32[]{:S(2)}) async-start(), calls=%async_computation.22 | async-start | bytes 7372800 | tf_op jit(solution)/shard_map/all_gather | solution.py:418
  281.8 172.2 %reduce-scatter.7.cloned.1.call-start = ((), (), s32[]{:S(2)}) async-start(), calls=%async_computation.23 | async-start | bytes 7372800 | tf_op jit(solution)/shard_map/reduce_scatter | solution.py:421
  392.9 63.5 %all-to-all-start.7 = ((bf16[4,704,512]{2,1,0:T(8,128)(2,1)}), bf16[4,704,512]{2,1,0:T(8,128)(2,1)}, u32[]{:S(2)}, u32[]{:S(2)}) async-start(bf16[4,704,512]{2,1,0:T(8,128)(2,1)} %unit_grads.2), calls=%async_computation.9 | async-start | bytes 5767168 | tf_op jit(solution)/shard_map/all_to_all | solution.py:384
  397.6 142.6 %all-gather.11.cloned.1.call-start = ((), (), s32[]{:S(2)}) async-start(), calls=%async_computation.24 | async-start | bytes 7372800 | tf_op jit(solution)/shard_map/all_gather | solution.py:418
  498.7 34.8 %all-to-all-start.9 = ((bf16[4,176,2048]{2,1,0:T(8,128)(2,1)}), bf16[4,176,2048]{2,1,0:T(8,128)(2,1)}, u32[]{:S(2)}, u32[]{:S(2)}) async-start(bf16[4,176,2048]{2,1,0:T(8,128)(2,1)} %bitcast.218), calls=%async_computation.11 | async-start | bytes 5767168 | tf_op jit(solution)/shard_map/all_to_all | solution.py:384
  540.2 45.3 %all-to-all-start.10 = ((bf16[8,2,64,704]{3,2,1,0:T(8,128)(2,1)}), bf16[8,2,64,704]{3,2,1,0:T(8,128)(2,1)}, u32[]{:S(2)}, u32[]{:S(2)}) async-start(bf16[8,2,64,704]{3,2,1,0:T(8,128)(2,1)} %maximum_bitcast_fusion), calls=%async_computation.12 | async-start | bytes 3145728 | tf_op jit(solution)/shard_map/all_to_all | solution.py:384
  547.5 105.2 %reduce-scatter.9.cloned.1.call-start = ((), (), s32[]{:S(2)}) async-start(), calls=%async_computation.25 | async-start | bytes 5529600 | tf_op jit(solution)/shard_map/reduce_scatter | solution.py:421
  598.7 2.7 collective-permute-start.8
  607.7 21.3 %all-to-all-start.11 = ((bf16[4,256,512]{2,1,0:T(8,128)(2,1)}), bf16[4,256,512]{2,1,0:T(8,128)(2,1)S(1)}, u32[]{:S(2)}, u32[]{:S(2)}) async-start(bf16[4,256,512]{2,1,0:T(8,128)(2,1)} %bitcast.222), calls=%async_computation.14 | async-start | bytes 2097152 | tf_op jit(solution)/shard_map/all_to_all | solution.py:384
  611.5 6.2 copy-start.7
  614.2 23.6 %collective-permute-start.9 = (bf16[128,2048]{1,0:T(8,128)(2,1)}, bf16[128,2048]{1,0:T(8,128)(2,1)}, u32[]{:S(2)}, u32[]{:S(2)}) collective-permute-start(bf16[128,2048]{1,0:T(8,128)(2,1)} %get-tuple-element.119), channel_id=1, source_target_pairs={{0,8},{8,0},{16,24},{24,16},{1,9},{9,1},{17,25},{25,17},{2,10},{10... | collective-permute-start | bytes 1572872 | tf_op jit(solution)/shard_map/ppermute | solution.py:424
  616.2 32.9 %collective-permute-start.11 = (bf16[128,2048]{1,0:T(8,128)(2,1)}, bf16[128,2048]{1,0:T(8,128)(2,1)}, u32[]{:S(2)}, u32[]{:S(2)}) collective-permute-start(bf16[128,2048]{1,0:T(8,128)(2,1)} %get-tuple-element.120), channel_id=1, source_target_pairs={{0,24},{8,16},{16,8},{24,0},{1,25},{9,17},{17,9},{25,1},{2,26},{10... | collective-permute-start | bytes 1572872 | tf_op jit(solution)/shard_map/ppermute | solution.py:424
  617.7 31.4 %collective-permute-start.10 = (bf16[128,2048]{1,0:T(8,128)(2,1)}, bf16[128,2048]{1,0:T(8,128)(2,1)}, u32[]{:S(2)}, u32[]{:S(2)}) collective-permute-start(bf16[128,2048]{1,0:T(8,128)(2,1)} %get-tuple-element.121), channel_id=1, source_target_pairs={{0,16},{8,24},{16,0},{24,8},{1,17},{9,25},{17,1},{25,9},{2,18},{10... | collective-permute-start | bytes 1572872 | tf_op jit(solution)/shard_map/ppermute | solution.py:424
  630.0 22.0 %all-to-all-start.12 = ((bf16[8,32,512]{2,1,0:T(8,128)(2,1)}), bf16[8,32,512]{2,1,0:T(8,128)(2,1)S(1)}, u32[]{:S(2)}, u32[]{:S(2)}) async-start(bf16[8,32,512]{2,1,0:T(8,128)(2,1)} %bitcast.221), calls=%async_computation.15 | async-start | bytes 524288 | tf_op jit(solution)/shard_map/all_to_all | solution.py:384
  633.4 118.8 %reduce-scatter.11.cloned.1.call-start = ((), (), s32[]{:S(2)}) async-start(), calls=%async_computation.26 | async-start | bytes 7372800 | tf_op jit(solution)/shard_map/reduce_scatter | solution.py:421
  663.0 6.0 collective-permute-start.12
  663.0 6.0 copy-start.11
  673.8 41.6 %all-to-all-start.13 = ((bf16[4,4,64,1536]{3,2,1,0:T(8,128)(2,1)}), bf16[4,4,64,1536]{3,2,1,0:T(8,128)(2,1)}, u32[]{:S(2)}, u32[]{:S(2)}) async-start(bf16[4,4,64,1536]{3,2,1,0:T(8,128)(2,1)} %bitcast.194), calls=%async_computation.17 | async-start | bytes 6291456 | tf_op jit(solution)/shard_map/all_to_all | solution.py:384
  694.4 6.7 collective-permute-start.13
  720.8 7.0 collective-permute-start.14
  722.2 7.3 collective-permute-start.16
  723.7 7.3 collective-permute-start.15
  724.3 26.4 %all-to-all-start.14 = ((bf16[4,64,1536]{2,1,0:T(8,128)(2,1)}), bf16[4,64,1536]{2,1,0:T(8,128)(2,1)S(1)}, u32[]{:S(2)}, u32[]{:S(2)}) async-start(bf16[4,64,1536]{2,1,0:T(8,128)(2,1)} %reduce_sum.150), calls=%async_computation.18 | async-start | bytes 1572864 | tf_op jit(solution)/shard_map/all_to_all | solution.py:384
  732.1 12.9 %collective-permute-start.17 = (bf16[64,128]{0,1:T(8,128)(2,1)S(1)}, bf16[64,128]{0,1:T(8,128)(2,1)S(1)}, u32[]{:S(2)}, u32[]{:S(2)}) collective-permute-start(bf16[64,128]{0,1:T(8,128)(2,1)S(1)} %get-tuple-element.134), channel_id=1, source_target_pairs={{0,2},{2,4},{4,6},{6,0},{1,3},{3,5},{5,7},{7,1},{8,10},{10,12},{12... | collective-permute-start | bytes 49160 | tf_op jit(solution)/shard_map/ppermute | solution.py:599
  732.2 12.8 %collective-permute-start.19 = (bf16[64,128]{0,1:T(8,128)(2,1)S(1)}, bf16[64,128]{0,1:T(8,128)(2,1)S(1)}, u32[]{:S(2)}, u32[]{:S(2)}) collective-permute-start(bf16[64,128]{0,1:T(8,128)(2,1)S(1)} %get-tuple-element.135), channel_id=1, source_target_pairs={{0,6},{2,0},{4,2},{6,4},{1,7},{3,1},{5,3},{7,5},{8,14},{10,8},{12,... | collective-permute-start | bytes 49160 | tf_op jit(solution)/shard_map/ppermute | solution.py:599
  736.0 13.7 %collective-permute-start.18 = (bf16[64,128]{0,1:T(8,128)(2,1)S(1)}, bf16[64,128]{0,1:T(8,128)(2,1)S(1)}, u32[]{:S(2)}, u32[]{:S(2)}) collective-permute-start(bf16[64,128]{0,1:T(8,128)(2,1)S(1)} %get-tuple-element.136), channel_id=1, source_target_pairs={{0,4},{2,6},{4,0},{6,2},{1,5},{3,7},{5,1},{7,3},{8,12},{10,14},{12... | collective-permute-start | bytes 49160 | tf_op jit(solution)/shard_map/ppermute | solution.py:599
  (21 other events, 49.0 us)
Sparse Core Ops, SparseCore 0:
  9.7 85.7 all-gather.4
  97.1 83.9 all-gather.6
  197.5 70.8 reduce-scatter.4
  281.9 64.2 all-gather.8
  383.0 70.9 reduce-scatter.6
  461.4 65.2 all-gather.10
  591.3 58.9 reduce-scatter.8
  655.1 69.3 reduce-scatter.10

commit v4 on v3

--- a/solution.py
+++ b/solution.py
@@ -501,7 +501,9 @@
     out_cols = jnp.swapaxes(exchange_share(after(out_cols, key_all)), 0, 1).reshape(heads * HD, model)
     attended, lse, out_part = attention(bits, query_all, key_all, value_all, out_cols, heads, seg_len)
     x = hidden_in.astype(F32)
-    out_part = after(out_part, cot, unit_cols)
+    down_sent = after(w_down, x_all)
+    down_got = [over_dp(down_sent, m) for m in range(1, dn)]
+    out_part, _, _, *down_got = lax.optimization_barrier((out_part, cot, unit_cols, *down_got))
     gate_cols = spread(unit_cols[:, 0], "dp").reshape(model, units)
     up_cols = spread(after(unit_cols[:, 1], out_part), "dp").reshape(model, units)
     scale_one = rms_scale(x)
@@ -514,7 +516,10 @@
         return at_index(a.reshape(a.shape[0], dn * zn, cn, per_row), core, 2).reshape(a.shape[0], dn * zn * per_row)
 
     normed_kept, normed_sent = per_core(normed_in, c_at), per_core(normed_in, 1 - c_at)
-    down_rows = spread(after(w_down, gate_cols), "dp").reshape(units, model)
+    down_rows = jnp.zeros((dn, unit_rows, model), BF)
+    for m, got in enumerate([after(w_down, out_part)] + down_got):
+        down_rows = lax.dynamic_update_index_in_dim(down_rows, got, d_at ^ m, 0)
+    down_rows = down_rows.reshape(units, model)
     mixed = x + after(tree_scatter(out_part), gate_cols, down_rows, scale_latent, normed_kept, normed_sent)
     mixed = lax.optimization_barrier(mixed)
 
@@ -529,28 +534,31 @@
     gate_parts = exchange(gate_parts, "dp")
     mid_grad = after(tree_scatter(mid_part), gate_parts, down_parts, up_parts)
     up_parts = exchange(after(up_parts, gate_parts), "dp")
-    down_parts = exchange(after(down_parts, up_parts), "dp")
     layer_part = dot32(after(activated, up_grad), down_rows).astype(BF)
     mixed_back = norm_back(mid_grad, normed_two, scale_two, gain_two)
     gain_two_cols = gain_column(mid_grad, normed_two, 1)
     mixed_grad = lax.optimization_barrier(cotangent.astype(F32) + mixed_back)
     branch_grad = mixed_grad.astype(BF)
 
-    grad_down = jnp.sum(down_parts.astype(F32), axis=0)
 
     def unit_sum(parts):
         return jnp.sum(parts.astype(F32), axis=0).astype(BF).reshape(units, fn, per_row)
 
     unit_own = jnp.stack([unit_sum(gate_parts), unit_sum(up_parts)])
     unit_own = plain(jnp.transpose(unit_own, (2, 0, 3, 1)))
-    branch, layer_part, gain_two_cols, unit_own, grad_down = lax.optimization_barrier(
-        (tree_gather(branch_grad), layer_part, gain_two_cols, unit_own, grad_down)
-    )
-    unit_own = exchange(unit_own, TREE).reshape(fn, 2, per_row, dn, unit_rows)
+    branch, layer_part, gain_two_cols, unit_own = lax.optimization_barrier(
+        (tree_gather(branch_grad), layer_part, gain_two_cols, unit_own)
+    )
+    down_sent = after(down_parts, branch)
+    down_got = [over_dp(at_index(down_sent, d_at ^ m), m) for m in range(1, dn)]
+    unit_got = exchange(unit_own, TREE)
     query_grad, back_part = attention_back(
         bits, lse, cosines, sines, query_all, key_all, value_all, attended, branch, out_cols, qup_cols, heads, seg_len
     )
-    back_part = after(back_part, unit_own)
+    back_part, unit_got, *down_got = lax.optimization_barrier((back_part, unit_got, *down_got))
+    grad_down = at_index(down_sent, d_at).astype(F32)
+    for got in down_got:
+        grad_down = grad_down + got.astype(F32)
     out_grads = jnp.swapaxes(
         dot_tn(attended, after(branch, back_part)).astype(BF).reshape(heads, sn, out_rows, model), 0, 1
     )
@@ -561,9 +569,10 @@
     grad_qup = dot_tn(latent_in, after(query_grad, back_part, out_grads))
     grad_qup = total(grad_qup.reshape(dn, fn * qup_rows, heads * HD), "dp").astype(BF)
     grad_qup = exchange(grad_qup.reshape(fn, qup_rows, heads * HD), TREE).reshape(qn, sn, qup_rows, heads, HD)
+    unit_own = after(unit_got, out_grads).reshape(fn, 2, per_row, dn, unit_rows)
     unit_own = jnp.transpose(unit_own, (1, 2, 3, 0, 4)).reshape(2, per_row, dn * fn * unit_rows).astype(F32)
-    back, grad_qup, grad_out, grad_gate, grad_up = lax.optimization_barrier(
-        (tree_scatter(back_part), grad_qup, grad_out, plain(unit_own[0]), plain(unit_own[1]))
+    back, grad_qup, grad_out, grad_down, grad_gate, grad_up = lax.optimization_barrier(
+        (tree_scatter(back_part), grad_qup, grad_out, grad_down, plain(unit_own[0]), plain(unit_own[1]))
     )
     layer_out = (mixed + tree_scatter(after(layer_part, back))).astype(BF)
     grad_qup = jnp.transpose(grad_qup, (2, 1, 3, 0, 4)).reshape(qup_rows, H * HD).astype(F32)

time: 771 us -> 752 us (0.975)
  blocking collectives: 118 us -> 38.3 us
  waiting for transfers between devices: 209 us -> 249 us
  local copies, waits for them, and re-layouts: 80.8 us -> 96.2 us
    all_to_all x3 -> x1, blocking collectives: 118 us -> 38.3 us  [exchange(): return lax.all_to_all(parts, axes, split_axis=0, concat_axis=0, tiled=True)]
    reduce_scatter x4, waiting for transfers between devices: 56.3 us -> 89.1 us  [tree_scatter(): lax.psum_scatter(parts, TREE, scatter_dimension=0, tiled=True).astype(F32)]
    all_gather x4, waiting for transfers between devices: 52.2 us -> 72.4 us  [tree_gather(): return lax.all_gather(block, TREE, axis=0, tiled=True)]
    convert_element_type x0 -> x2, local copies, waits for them, and re-layouts: none -> 10.6 us  [body(): jnp.transpose(unit_own, (1, 2, 3, 0, 4))]
    ppermute x9 -> x15, waiting for transfers between devices: 18.9 us -> 11.6 us  [over_dp(): return lax.ppermute(a, 'dp', [(d, d ^ m) for d in range(dn)])]
    ppermute x9 -> x15, starting transfers between devices: 11.3 us -> 18.3 us  [over_dp(): return lax.ppermute(a, 'dp', [(d, d ^ m) for d in range(dn)])]
  transfers between devices with their start and end apart: 40 -> 46, of which waited for: 22 -> 22; matrix products, arithmetic and copies ran while one was open for 23% -> 26% of each run, Pallas kernels for 13% -> 13%
where the time goes in v4:
time: 752 us; the launch traced here: 742 us
  waiting for transfers between devices  249 us (33%)
  Pallas kernels  132 us (18%)
  local copies, waits for them, and re-layouts  96.2 us (13%)
  starting transfers between devices  94.2 us (13%)
  other arithmetic  63.9 us (8%)
  matrix products  52.4 us (7%)
  blocking collectives  38.3 us (5%)
  between operations  15.5 us (2%)
    reduce_scatter x4, waiting for transfers between devices, tree_scatter(): lax.psum_scatter(parts, TREE, scatter_dimension=0, tiled=True).astype(F32)  89.1 us
    all_gather x4, waiting for transfers between devices, tree_gather(): return lax.all_gather(block, TREE, axis=0, tiled=True)  72.4 us
    all_to_all x12, starting transfers between devices, exchange(): return lax.all_to_all(parts, axes, split_axis=0, concat_axis=0, tiled=True)  64.6 us
    all_to_all x12, waiting for transfers between devices, exchange(): return lax.all_to_all(parts, axes, split_axis=0, concat_axis=0, tiled=True)  46.8 us
    all_to_all x1, blocking collectives, exchange(): return lax.all_to_all(parts, axes, split_axis=0, concat_axis=0, tiled=True)  38.3 us
    pallas_call x1, Pallas kernels, ffn(): pl.pallas_call(ffn_kernel, grid=(count // rows,), out_shape=[jax.ShapeDty...  36.7 us
    pallas_call x1, Pallas kernels, attention_back(): pl.pallas_call(functools.partial(attn_bwd_kernel, heads, seg_len), out_sh...  33.2 us
    dot_general x5, matrix products, dot_tn(): lax.dot_general(a, b, (((0,), (0,)), ((), ())), preferred_element_type=F32)  27.4 us
  transfers between devices with their start and end apart: 46, of which 22 were waited for; matrix products, arithmetic and copies ran while one was open for 26% of the time, Pallas kernels for 13%

profile of v4, /device:TPU:0, one launch (start us, length us, event | category | flops | bytes accessed | tf_op | source)
XLA Modules:
  0.0 742.2 jit_solution(5505129347679484653)
XLA Ops:
  12.2 5.1 collective-permute-start.2
  23.5 4.1 all-to-all-start
  38.4 4.7 collective-permute-done
  45.4 7.3 collective-permute-done.1
  56.9 4.6 all-to-all-done
  63.6 3.9 all-to-all-start.1
  67.6 27.9 %all-gather.5.cloned.1.call-done.x_ref = bf16[1600,2048]{1,0:T(8,128)(2,1)} async-done(((bf16[200,2048]{1,0:T(8,128)(2,1)}), bf16[1600,2048]{1,0:T(8,128)(2,1)}) %all-gather.5.cloned.1.call-update) | async-done | bytes 6553616 | tf_op jit(solution)/shard_map/all_gather | solution.py:418
  95.5 8.2 %all-to-all-done.1 = bf16[4,4,64,1664]{3,2,1,0:T(8,128)(2,1)S(1)} async-done(((bf16[4,4,64,1664]{3,2,1,0:T(8,128)(2,1)}), bf16[4,4,64,1664]{3,2,1,0:T(8,128)(2,1)S(1)}, u32[]{:S(2)}, u32[]{:S(2)}) %all-to-all-start.1) | async-done | bytes 3407904 | tf_op jit(solution)/shard_map/all_to_all | solution.py:384
  106.8 4.4 all-to-all-start.2
  111.2 4.3 select_bitcast_fusion.1
  127.2 16.2 %all-to-all-start.3 = ((bf16[8,2,64,704]{3,2,1,0:T(8,128)(2,1)}), bf16[8,2,64,704]{3,2,1,0:T(8,128)(2,1)}, u32[]{:S(2)}, u32[]{:S(2)}) async-start(bf16[8,2,64,704]{3,2,1,0:T(8,128)(2,1)} %copy.108), calls=%async_computation.3 | async-start | bytes 3145728 | tf_op jit(solution)/shard_map/all_to_all | solution.py:384
  143.5 19.0 %project.1 = (bf16[1600,512]{1,0:T(8,128)(2,1)}, bf16[1600,256]{1,0:T(8,128)(2,1)}, bf16[1600,256]{1,0:T(8,128)(2,1)}, bf16[1600,1024]{1,0:T(8,128)(2,1)}) custom-call(bf16[1600,2048]{1,0:T(8,128)(2,1)} %all-gather.5.cloned.1.call-done.x_ref, bf16[2048,1664]{1,0:T(8,128)(2,1)} %bitcast.220, bf16[1024,512]{1,0:T(8,128)(2,1)} %bitcast.23.qup_ref.wq_ref, ...), custom_call_target="tpu_custom_call" | custom-call | flops 11744051200 | bytes 22815744 | tf_op jit(solution)/shard_map/project/pallas_call | solution.py:273
  170.5 23.3 %attn_fwd.1 = (bf16[1600,512]{1,0:T(8,128)(2,1)}, f32[5,1,640]{2,1,0:T(1,128)}, bf16[1600,2048]{1,0:T(8,128)(2,1)}) custom-call(s32[5,1,640]{2,1,0:T(1,128)} %reshape.312.bits_ref, bf16[1600,512]{1,0:T(8,128)(2,1)} %get-tuple-element.72.q_ref, bf16[1600,256]{1,0:T(8,128)(2,1)} %get-tuple-element.73.k_ref, bf16[1600,256]{1,0:T(8,128)(2,1)} %get-tuple-element.74.v_ref, ...), custom_call_target="tpu_custom_call" | custom-call | flops 3932160000 | bytes 4915200 | tf_op jit(solution)/shard_map/attn_fwd/pallas_call | solution.py:204
  193.8 5.0 collective-permute-done.9
  204.1 4.8 all-to-all-start.4
  219.8 52.4 %reduce-scatter.5.cloned.1.call-done = bf16[200,2048]{1,0:T(8,128)(2,1)} async-done(((bf16[1600,2048]{1,0:T(8,128)(2,1)}), bf16[200,2048]{1,0:T(8,128)(2,1)}) %reduce-scatter.5.cloned.1.call-update) | async-done | bytes 819216 | tf_op jit(solution)/shard_map/reduce_scatter | solution.py:421
  278.1 38.3 %all_to_all.65 = bf16[4,8,64,704]{3,2,1,0:T(8,128)(2,1)} all-to-all(bf16[4,8,64,704]{3,2,1,0:T(8,128)(2,1)S(1)} %broadcast_in_dim.151), channel_id=1, replica_groups=mesh['dp'=4,'q'=4,'r'=1,'c'=2] {'dp'}, dimensions={0} | all-to-all | bytes 5767168 | tf_op jit(solution)/shard_map/all_to_all | solution.py:384
  316.4 26.7 %all-gather.9.cloned.1.call-done.mid_ref = bf16[1600,2048]{1,0:T(8,128)(2,1)} async-done(((bf16[200,2048]{1,0:T(8,128)(2,1)}), bf16[1600,2048]{1,0:T(8,128)(2,1)}) %all-gather.9.cloned.1.call-update) | async-done | bytes 6553616 | tf_op jit(solution)/shard_map/all_gather | solution.py:418
  343.1 36.7 %ffn.1 = (bf16[1600,704]{1,0:T(8,128)(2,1)}, bf16[1600,704]{1,0:T(8,128)(2,1)}, bf16[1600,704]{1,0:T(8,128)(2,1)}, bf16[1600,2048]{1,0:T(8,128)(2,1)}) custom-call(bf16[1600,2048]{1,0:T(8,128)(2,1)} %all-gather.9.cloned.1.call-done.mid_ref, bf16[1600,2048]{1,0:T(8,128)(2,1)} %all-gather.7.cloned.1.call-done.cot_ref, bf16[2048,704]{1,0:T(8,128)(2,1)} %bitcast.35.wg_ref, ...), custom_call_target="tpu_custom_call" | custom-call | flops 23068672000 | bytes 28311552 | tf_op jit(solution)/shard_map/ffn/pallas_call | solution.py:312
  379.8 10.1 %unit_grads.2 = bf16[4,704,512]{2,1,0:T(8,128)(2,1)} custom-call(bf16[1600,2048]{1,0:T(8,128)(2,1)} %all-gather.9.cloned.1.call-done.mid_ref, bf16[1600,704]{1,0:T(8,128)(2,1)} %get-tuple-element.90.grad_ref), custom_call_target="tpu_custom_call" | custom-call | flops 4613734400 | bytes 9437184 | tf_op jit(solution)/shard_map/unit_grads/pallas_call | solution.py:338
  389.9 4.6 all-to-all-start.6
  394.5 9.6 %convolution_convert_fusion.2 = bf16[704,2048]{1,0:T(8,128)(2,1)} fusion(bf16[1600,704]{1,0:T(8,128)(2,1)} %get-tuple-element.96, bf16[1600,2048]{1,0:T(8,128)(2,1)} %all-gather.7.cloned.1.call-done.cot_ref), kind=kOutput, calls=%fused_computation.11 | convolution fusion | flops 4615176192 | bytes 11689984 | tf_op jit(solution)/shard_map/dot_general | solution.py:37
  404.1 10.0 %unit_grads.3 = bf16[4,704,512]{2,1,0:T(8,128)(2,1)} custom-call(bf16[1600,2048]{1,0:T(8,128)(2,1)} %all-gather.9.cloned.1.call-done.mid_ref, bf16[1600,704]{1,0:T(8,128)(2,1)} %get-tuple-element.94.grad_ref), custom_call_target="tpu_custom_call" | custom-call | flops 4613734400 | bytes 9437184 | tf_op jit(solution)/shard_map/unit_grads/pallas_call | solution.py:338
  414.2 36.7 %reduce-scatter.7.cloned.1.call-done = bf16[200,2048]{1,0:T(8,128)(2,1)} async-done(((bf16[1600,2048]{1,0:T(8,128)(2,1)}), bf16[200,2048]{1,0:T(8,128)(2,1)}) %reduce-scatter.7.cloned.1.call-update) | async-done | bytes 819216 | tf_op jit(solution)/shard_map/reduce_scatter | solution.py:421
  458.3 5.0 all-to-all-start.7
  463.4 9.7 %convolution_convert_fusion = bf16[1600,2048]{1,0:T(8,128)(2,1)} fusion(bf16[1600,704]{1,0:T(8,128)(2,1)} %get-tuple-element.96, bf16[704,2048]{1,0:T(8,128)(2,1)} %bitcast.40.wd_ref), kind=kOutput, calls=%fused_computation | convolution fusion | flops 4617011200 | bytes 11689984 | tf_op jit(solution)/shard_map/dot_general | solution.py:29
  477.8 17.1 %all-to-all-done.7 = bf16[4,704,512]{2,1,0:T(8,128)(2,1)} async-done(((bf16[4,704,512]{2,1,0:T(8,128)(2,1)}), bf16[4,704,512]{2,1,0:T(8,128)(2,1)}, u32[]{:S(2)}, u32[]{:S(2)}) %all-to-all-start.7) | async-done | bytes 2883616 | tf_op jit(solution)/shard_map/all_to_all | solution.py:384
  506.0 17.8 %all-gather.11.cloned.1.call-done.branch_ref = bf16[1600,2048]{1,0:T(8,128)(2,1)} async-done(((bf16[200,2048]{1,0:T(8,128)(2,1)}), bf16[1600,2048]{1,0:T(8,128)(2,1)}) %all-gather.11.cloned.1.call-update) | async-done | bytes 6553616 | tf_op jit(solution)/shard_map/all_gather | solution.py:418
  523.8 4.3 all-to-all-start.8
  533.7 33.2 %attn_bwd.1 = (bf16[1600,512]{1,0:T(8,128)(2,1)}, bf16[1600,1536]{1,0:T(8,128)(2,1)}) custom-call(s32[5,1,640]{2,1,0:T(1,128)} %reshape.312.bits_ref, f32[5,1,640]{2,1,0:T(1,128)} %get-tuple-element.99.lse_ref, f32[1600,128]{1,0:T(8,128)} %bitcast.247, f32[1600,128]{1,0:T(8,128)} %bitcast.244, bf16[1600,512]{1,0:T(8,128)(2,1)} %get-tuple-element.72.q_ref, ...), custom_call_target="tpu_custom_call" | custom-call | flops 9175040000 | bytes 9830400 | tf_op jit(solution)/shard_map/attn_bwd/pallas_call | solution.py:224
  566.9 7.4 convolution_convert_fusion.3
  583.4 3.9 all-to-all-start.9
  593.3 3.4 fusion.19
  596.7 6.0 reshape.332
  602.7 4.7 copy.126
  617.2 5.0 all-to-all-start.10
  627.6 4.3 all-to-all-done.10
  635.0 3.6 multiply_reduce_fusion.3
  644.8 4.0 collective-permute-done.18
  648.9 4.7 add_convert_fusion
  653.6 4.9 all-to-all-start.11
  664.6 5.0 fusion.9
  683.2 12.6 %all-to-all-done.11 = bf16[4,4,64,1536]{3,2,1,0:T(8,128)(2,1)} async-done(((bf16[4,4,64,1536]{3,2,1,0:T(8,128)(2,1)}), bf16[4,4,64,1536]{3,2,1,0:T(8,128)(2,1)}, u32[]{:S(2)}, u32[]{:S(2)}) %all-to-all-start.11) | async-done | bytes 3145760 | tf_op jit(solution)/shard_map/all_to_all | solution.py:384
  695.7 3.5 reduce_sum.140
  704.6 3.5 all-to-all-start.12
  712.9 3.8 collective-permute-start.25
  720.0 5.5 collective-permute-done.23
  725.5 4.7 collective-permute-done.24
  (279 shorter events, 181.3 us)
Async XLA Ops:
  7.2 20.4 %copy-start.20 = (bf16[64,5632]{1,0:T(8,128)(2,1)S(1)}, bf16[64,5632]{1,0:T(8,128)(2,1)}, u32[]{:S(2)}) copy-start(bf16[64,5632]{1,0:T(8,128)(2,1)} %param.26) | copy-start | bytes 2162692
  7.2 88.3 %all-gather.5.cloned.1.call-start = ((), (), s32[]{:S(2)}) async-start(), calls=%async_computation.17 | async-start | bytes 7372800 | tf_op jit(solution)/shard_map/all_gather | solution.py:418
  12.2 41.5 %collective-permute-start.2 = (bf16[64,1664]{1,0:T(8,128)(2,1)S(1)}, bf16[64,1664]{1,0:T(8,128)(2,1)}, u32[]{:S(2)}, u32[]{:S(2)}) collective-permute-start(bf16[64,1664]{1,0:T(8,128)(2,1)S(1)} %concatenate.7), channel_id=1, source_target_pairs={{0,6},{2,0},{4,2},{6,4},{1,7},{3,1},{5,3},{7,5},{8,14},{10,8},{12,... | collective-permute-start | bytes 638984 | tf_op jit(solution)/shard_map/ppermute | solution.py:437
  17.3 35.4 %collective-permute-start.1 = (bf16[64,1664]{1,0:T(8,128)(2,1)S(1)}, bf16[64,1664]{1,0:T(8,128)(2,1)}, u32[]{:S(2)}, u32[]{:S(2)}) collective-permute-start(bf16[64,1664]{1,0:T(8,128)(2,1)S(1)} %concatenate.7), channel_id=1, source_target_pairs={{0,4},{2,6},{4,0},{6,2},{1,5},{3,7},{5,1},{7,3},{8,12},{10,14},{12... | collective-permute-start | bytes 638984 | tf_op jit(solution)/shard_map/ppermute | solution.py:437
  17.3 25.8 %collective-permute-start = (bf16[64,1664]{1,0:T(8,128)(2,1)S(1)}, bf16[64,1664]{1,0:T(8,128)(2,1)}, u32[]{:S(2)}, u32[]{:S(2)}) collective-permute-start(bf16[64,1664]{1,0:T(8,128)(2,1)S(1)} %concatenate.7), channel_id=1, source_target_pairs={{0,2},{2,4},{4,6},{6,0},{1,3},{3,5},{5,7},{7,1},{8,10},{10,12},{12... | collective-permute-start | bytes 638984 | tf_op jit(solution)/shard_map/ppermute | solution.py:437
  18.3 36.4 %collective-permute-start.3 = (bf16[128,2048]{1,0:T(8,128)(2,1)}, bf16[128,2048]{1,0:T(8,128)(2,1)}, u32[]{:S(2)}, u32[]{:S(2)}) collective-permute-start(bf16[128,2048]{1,0:T(8,128)(2,1)} %param.24), channel_id=1, source_target_pairs={{0,8},{8,0},{16,24},{24,16},{1,9},{9,1},{17,25},{25,17},{2,10},{10... | collective-permute-start | bytes 1572872 | tf_op jit(solution)/shard_map/ppermute | solution.py:424
  19.8 36.0 %collective-permute-start.5 = (bf16[128,2048]{1,0:T(8,128)(2,1)}, bf16[128,2048]{1,0:T(8,128)(2,1)}, u32[]{:S(2)}, u32[]{:S(2)}) collective-permute-start(bf16[128,2048]{1,0:T(8,128)(2,1)} %param.24), channel_id=1, source_target_pairs={{0,24},{8,16},{16,8},{24,0},{1,25},{9,17},{17,9},{25,1},{2,26},{10... | collective-permute-start | bytes 1572872 | tf_op jit(solution)/shard_map/ppermute | solution.py:424
  23.5 38.0 %all-to-all-start = ((bf16[8,32,512]{2,1,0:T(8,128)(2,1)}), bf16[8,32,512]{2,1,0:T(8,128)(2,1)S(1)}, u32[]{:S(2)}, u32[]{:S(2)}) async-start(bf16[8,32,512]{2,1,0:T(8,128)(2,1)} %reshape.304), calls=%async_computation | async-start | bytes 524288 | tf_op jit(solution)/shard_map/all_to_all | solution.py:384
  43.1 12.6 %collective-permute-start.4 = (bf16[128,2048]{1,0:T(8,128)(2,1)S(1)}, bf16[128,2048]{1,0:T(8,128)(2,1)S(1)}, u32[]{:S(2)}, u32[]{:S(2)}) collective-permute-start(bf16[128,2048]{1,0:T(8,128)(2,1)S(1)} %copy-done.24), channel_id=1, source_target_pairs={{0,16},{8,24},{16,0},{24,8},{1,17},{9,25},{17,1},{25,9},{2,18},{10... | collective-permute-start | bytes 1572872 | tf_op jit(solution)/shard_map/ppermute | solution.py:424
  63.6 40.1 %copy-start.26 = (s32[1,20]{1,0:T(1,128)S(1)}, s32[1,20]{1,0:T(1,128)}, u32[]{:S(2)}) copy-start(s32[1,20]{1,0:T(1,128)} %param.17) | copy-start | bytes 244
  63.6 40.1 %all-to-all-start.1 = ((bf16[4,4,64,1664]{3,2,1,0:T(8,128)(2,1)}), bf16[4,4,64,1664]{3,2,1,0:T(8,128)(2,1)S(1)}, u32[]{:S(2)}, u32[]{:S(2)}) async-start(bf16[4,4,64,1664]{3,2,1,0:T(8,128)(2,1)} %broadcast_in_dim.138), calls=%async_computation.1 | async-start | bytes 6815744 | tf_op jit(solution)/shard_map/all_to_all | solution.py:384
  67.5 131.6 %all-gather.7.cloned.1.call-start = ((), (), s32[]{:S(2)}) async-start(), calls=%async_computation.18 | async-start | bytes 7372800 | tf_op jit(solution)/shard_map/all_gather | solution.py:418
  103.7 7.5 %collective-permute-start.6 = (bf16[4,4,64,1664]{3,2,1,0:T(8,128)(2,1)S(1)}, bf16[4,4,64,1664]{3,2,1,0:T(8,128)(2,1)}, u32[]{:S(2)}, u32[]{:S(2)}) collective-permute-start(bf16[4,4,64,1664]{3,2,1,0:T(8,128)(2,1)S(1)} %all-to-all-done.1), channel_id=1, source_target_pairs={{0,1},{1,0},{2,3},{3,2},{4,5},{5,4},{6,7},{7,6},{8,9},{9,8},{10,11... | collective-permute-start | bytes 10223624 | tf_op jit(solution)/shard_map/ppermute | solution.py:393
  106.8 19.0 %all-to-all-start.2 = ((bf16[4,8,32,512]{3,2,1,0:T(8,128)(2,1)}), bf16[4,8,32,512]{3,2,1,0:T(8,128)(2,1)}, u32[]{:S(2)}, u32[]{:S(2)}) async-start(bf16[4,8,32,512]{3,2,1,0:T(8,128)(2,1)} %broadcast_in_dim.143), calls=%async_computation.2 | async-start | bytes 2097152 | tf_op jit(solution)/shard_map/all_to_all | solution.py:384
  127.2 72.0 %all-to-all-start.3 = ((bf16[8,2,64,704]{3,2,1,0:T(8,128)(2,1)}), bf16[8,2,64,704]{3,2,1,0:T(8,128)(2,1)}, u32[]{:S(2)}, u32[]{:S(2)}) async-start(bf16[8,2,64,704]{3,2,1,0:T(8,128)(2,1)} %copy.108), calls=%async_computation.3 | async-start | bytes 3145728 | tf_op jit(solution)/shard_map/all_to_all | solution.py:384
  143.4 128.7 %reduce-scatter.5.cloned.1.call-start = ((), (), s32[]{:S(2)}) async-start(), calls=%async_computation.19 | async-start | bytes 7372800 | tf_op jit(solution)/shard_map/reduce_scatter | solution.py:421
  162.6 4.9 collective-permute-start.7
  164.1 29.8 %collective-permute-start.10 = (bf16[176,2048]{1,0:T(8,128)(2,1)}, bf16[176,2048]{1,0:T(8,128)(2,1)}, u32[]{:S(2)}, u32[]{:S(2)}) collective-permute-start(bf16[176,2048]{1,0:T(8,128)(2,1)} %param.28), channel_id=1, source_target_pairs={{0,24},{8,16},{16,8},{24,0},{1,25},{9,17},{17,9},{25,1},{2,26},{10... | collective-permute-start | bytes 2162696 | tf_op jit(solution)/shard_map/ppermute | solution.py:424
  166.8 32.1 %collective-permute-start.9 = (bf16[176,2048]{1,0:T(8,128)(2,1)}, bf16[176,2048]{1,0:T(8,128)(2,1)}, u32[]{:S(2)}, u32[]{:S(2)}) collective-permute-start(bf16[176,2048]{1,0:T(8,128)(2,1)} %param.28), channel_id=1, source_target_pairs={{0,16},{8,24},{16,0},{24,8},{1,17},{9,25},{17,1},{25,9},{2,18},{10... | collective-permute-start | bytes 2162696 | tf_op jit(solution)/shard_map/ppermute | solution.py:424
  167.3 31.8 %collective-permute-start.8 = (bf16[176,2048]{1,0:T(8,128)(2,1)}, bf16[176,2048]{1,0:T(8,128)(2,1)}, u32[]{:S(2)}, u32[]{:S(2)}) collective-permute-start(bf16[176,2048]{1,0:T(8,128)(2,1)} %param.28), channel_id=1, source_target_pairs={{0,8},{8,0},{16,24},{24,16},{1,9},{9,1},{17,25},{25,17},{2,10},{10... | collective-permute-start | bytes 2162696 | tf_op jit(solution)/shard_map/ppermute | solution.py:424
  204.1 70.7 %all-to-all-start.4 = ((bf16[4,8,64,704]{3,2,1,0:T(8,128)(2,1)}), bf16[4,8,64,704]{3,2,1,0:T(8,128)(2,1)}, u32[]{:S(2)}, u32[]{:S(2)}) async-start(bf16[4,8,64,704]{3,2,1,0:T(8,128)(2,1)} %broadcast_in_dim.145), calls=%async_computation.5 | async-start | bytes 6291456 | tf_op jit(solution)/shard_map/all_to_all | solution.py:384
  208.9 134.3 %all-gather.9.cloned.1.call-start = ((), (), s32[]{:S(2)}) async-start(), calls=%async_computation.20 | async-start | bytes 7372800 | tf_op jit(solution)/shard_map/all_gather | solution.py:418
  277.7 173.2 %reduce-scatter.7.cloned.1.call-start = ((), (), s32[]{:S(2)}) async-start(), calls=%async_computation.21 | async-start | bytes 7372800 | tf_op jit(solution)/shard_map/reduce_scatter | solution.py:421
  389.9 63.6 %all-to-all-start.6 = ((bf16[4,704,512]{2,1,0:T(8,128)(2,1)}), bf16[4,704,512]{2,1,0:T(8,128)(2,1)}, u32[]{:S(2)}, u32[]{:S(2)}) async-start(bf16[4,704,512]{2,1,0:T(8,128)(2,1)} %unit_grads.2), calls=%async_computation.8 | async-start | bytes 5767168 | tf_op jit(solution)/shard_map/all_to_all | solution.py:384
  394.5 129.3 %all-gather.11.cloned.1.call-start = ((), (), s32[]{:S(2)}) async-start(), calls=%async_computation.22 | async-start | bytes 7372800 | tf_op jit(solution)/shard_map/all_gather | solution.py:418
  458.3 36.5 %all-to-all-start.7 = ((bf16[4,704,512]{2,1,0:T(8,128)(2,1)}), bf16[4,704,512]{2,1,0:T(8,128)(2,1)}, u32[]{:S(2)}, u32[]{:S(2)}) async-start(bf16[4,704,512]{2,1,0:T(8,128)(2,1)} %unit_grads.3), calls=%async_computation.9 | async-start | bytes 5767168 | tf_op jit(solution)/shard_map/all_to_all | solution.py:384
  523.8 43.1 %all-to-all-start.8 = ((bf16[8,2,64,704]{3,2,1,0:T(8,128)(2,1)}), bf16[8,2,64,704]{3,2,1,0:T(8,128)(2,1)}, u32[]{:S(2)}, u32[]{:S(2)}) async-start(bf16[8,2,64,704]{3,2,1,0:T(8,128)(2,1)} %maximum_bitcast_fusion), calls=%async_computation.10 | async-start | bytes 3145728 | tf_op jit(solution)/shard_map/all_to_all | solution.py:384
  528.1 104.6 %reduce-scatter.9.cloned.1.call-start = ((), (), s32[]{:S(2)}) async-start(), calls=%async_computation.23 | async-start | bytes 5529600 | tf_op jit(solution)/shard_map/reduce_scatter | solution.py:421
  530.1 36.7 %collective-permute-start.13 = (bf16[176,2048]{1,0:T(8,128)(2,1)S(1)}, bf16[176,2048]{1,0:T(8,128)(2,1)}, u32[]{:S(2)}, u32[]{:S(2)}) collective-permute-start(bf16[176,2048]{1,0:T(8,128)(2,1)S(1)} %get-tuple-element.135), channel_id=1, source_target_pairs={{0,24},{8,16},{16,8},{24,0},{1,25},{9,17},{17,9},{25,1},{2,26},{10... | collective-permute-start | bytes 2162696 | tf_op jit(solution)/shard_map/ppermute | solution.py:424
  532.6 34.3 %collective-permute-start.12 = (bf16[176,2048]{1,0:T(8,128)(2,1)S(1)}, bf16[176,2048]{1,0:T(8,128)(2,1)}, u32[]{:S(2)}, u32[]{:S(2)}) collective-permute-start(bf16[176,2048]{1,0:T(8,128)(2,1)S(1)} %get-tuple-element.136), channel_id=1, source_target_pairs={{0,16},{8,24},{16,0},{24,8},{1,17},{9,25},{17,1},{25,9},{2,18},{10... | collective-permute-start | bytes 2162696 | tf_op jit(solution)/shard_map/ppermute | solution.py:424
  533.1 33.7 %collective-permute-start.11 = (bf16[176,2048]{1,0:T(8,128)(2,1)S(1)}, bf16[176,2048]{1,0:T(8,128)(2,1)}, u32[]{:S(2)}, u32[]{:S(2)}) collective-permute-start(bf16[176,2048]{1,0:T(8,128)(2,1)S(1)} %get-tuple-element.137), channel_id=1, source_target_pairs={{0,8},{8,0},{16,24},{24,16},{1,9},{9,1},{17,25},{25,17},{2,10},{10... | collective-permute-start | bytes 2162696 | tf_op jit(solution)/shard_map/ppermute | solution.py:424
  574.4 2.7 collective-permute-start.14
  583.4 32.9 %all-to-all-start.9 = ((bf16[4,256,512]{2,1,0:T(8,128)(2,1)}), bf16[4,256,512]{2,1,0:T(8,128)(2,1)S(1)}, u32[]{:S(2)}, u32[]{:S(2)}) async-start(bf16[4,256,512]{2,1,0:T(8,128)(2,1)} %bitcast.241), calls=%async_computation.12 | async-start | bytes 2097152 | tf_op jit(solution)/shard_map/all_to_all | solution.py:384
  589.8 32.4 %collective-permute-start.15 = (bf16[128,2048]{1,0:T(8,128)(2,1)}, bf16[128,2048]{1,0:T(8,128)(2,1)}, u32[]{:S(2)}, u32[]{:S(2)}) collective-permute-start(bf16[128,2048]{1,0:T(8,128)(2,1)} %get-tuple-element.140), channel_id=1, source_target_pairs={{0,8},{8,0},{16,24},{24,16},{1,9},{9,1},{17,25},{25,17},{2,10},{10... | collective-permute-start | bytes 1572872 | tf_op jit(solution)/shard_map/ppermute | solution.py:424
  591.9 32.9 %collective-permute-start.17 = (bf16[128,2048]{1,0:T(8,128)(2,1)}, bf16[128,2048]{1,0:T(8,128)(2,1)}, u32[]{:S(2)}, u32[]{:S(2)}) collective-permute-start(bf16[128,2048]{1,0:T(8,128)(2,1)} %get-tuple-element.141), channel_id=1, source_target_pairs={{0,24},{8,16},{16,8},{24,0},{1,25},{9,17},{17,9},{25,1},{2,26},{10... | collective-permute-start | bytes 1572872 | tf_op jit(solution)/shard_map/ppermute | solution.py:424
  593.3 31.5 %collective-permute-start.16 = (bf16[128,2048]{1,0:T(8,128)(2,1)}, bf16[128,2048]{1,0:T(8,128)(2,1)}, u32[]{:S(2)}, u32[]{:S(2)}) collective-permute-start(bf16[128,2048]{1,0:T(8,128)(2,1)} %get-tuple-element.142), channel_id=1, source_target_pairs={{0,16},{8,24},{16,0},{24,8},{1,17},{9,25},{17,1},{25,9},{2,18},{10... | collective-permute-start | bytes 1572872 | tf_op jit(solution)/shard_map/ppermute | solution.py:424
  617.2 14.7 %all-to-all-start.10 = ((bf16[8,32,512]{2,1,0:T(8,128)(2,1)}), bf16[8,32,512]{2,1,0:T(8,128)(2,1)S(1)}, u32[]{:S(2)}, u32[]{:S(2)}) async-start(bf16[8,32,512]{2,1,0:T(8,128)(2,1)} %bitcast.240), calls=%async_computation.13 | async-start | bytes 524288 | tf_op jit(solution)/shard_map/all_to_all | solution.py:384
  622.2 110.5 %reduce-scatter.11.cloned.1.call-start = ((), (), s32[]{:S(2)}) async-start(), calls=%async_computation.24 | async-start | bytes 7372800 | tf_op jit(solution)/shard_map/reduce_scatter | solution.py:421
  642.9 6.0 collective-permute-start.18
  653.6 42.1 %all-to-all-start.11 = ((bf16[4,4,64,1536]{3,2,1,0:T(8,128)(2,1)}), bf16[4,4,64,1536]{3,2,1,0:T(8,128)(2,1)}, u32[]{:S(2)}, u32[]{:S(2)}) async-start(bf16[4,4,64,1536]{3,2,1,0:T(8,128)(2,1)} %bitcast.212), calls=%async_computation.15 | async-start | bytes 6291456 | tf_op jit(solution)/shard_map/all_to_all | solution.py:384
  674.3 6.8 collective-permute-start.19
  701.1 7.0 collective-permute-start.20
  702.7 7.6 %collective-permute-start.22 = (bf16[4,64,128]{1,2,0:T(8,128)(2,1)}, bf16[4,64,128]{1,2,0:T(8,128)(2,1)S(1)}, u32[]{:S(2)}, u32[]{:S(2)}) collective-permute-start(bf16[4,64,128]{1,2,0:T(8,128)(2,1)} %get-tuple-element.146), channel_id=1, source_target_pairs={{0,24},{8,16},{16,8},{24,0},{1,25},{9,17},{17,9},{25,1},{2,26},{10... | collective-permute-start | bytes 196616 | tf_op jit(solution)/shard_map/ppermute | solution.py:424
  704.2 7.5 %collective-permute-start.21 = (bf16[4,64,128]{1,2,0:T(8,128)(2,1)}, bf16[4,64,128]{1,2,0:T(8,128)(2,1)}, u32[]{:S(2)}, u32[]{:S(2)}) collective-permute-start(bf16[4,64,128]{1,2,0:T(8,128)(2,1)} %get-tuple-element.147), channel_id=1, source_target_pairs={{0,16},{8,24},{16,0},{24,8},{1,17},{9,25},{17,1},{25,9},{2,18},{10... | collective-permute-start | bytes 196616 | tf_op jit(solution)/shard_map/ppermute | solution.py:424
  704.6 26.6 %all-to-all-start.12 = ((bf16[4,64,1536]{2,1,0:T(8,128)(2,1)}), bf16[4,64,1536]{2,1,0:T(8,128)(2,1)S(1)}, u32[]{:S(2)}, u32[]{:S(2)}) async-start(bf16[4,64,1536]{2,1,0:T(8,128)(2,1)} %reduce_sum.140), calls=%async_computation.16 | async-start | bytes 1572864 | tf_op jit(solution)/shard_map/all_to_all | solution.py:384
  712.8 12.7 %collective-permute-start.23 = (bf16[64,128]{0,1:T(8,128)(2,1)S(1)}, bf16[64,128]{0,1:T(8,128)(2,1)S(1)}, u32[]{:S(2)}, u32[]{:S(2)}) collective-permute-start(bf16[64,128]{0,1:T(8,128)(2,1)S(1)} %get-tuple-element.155), channel_id=1, source_target_pairs={{0,2},{2,4},{4,6},{6,0},{1,3},{3,5},{5,7},{7,1},{8,10},{10,12},{12... | collective-permute-start | bytes 49160 | tf_op jit(solution)/shard_map/ppermute | solution.py:608
  712.9 12.6 %collective-permute-start.25 = (bf16[64,128]{0,1:T(8,128)(2,1)S(1)}, bf16[64,128]{0,1:T(8,128)(2,1)S(1)}, u32[]{:S(2)}, u32[]{:S(2)}) collective-permute-start(bf16[64,128]{0,1:T(8,128)(2,1)S(1)} %get-tuple-element.156), channel_id=1, source_target_pairs={{0,6},{2,0},{4,2},{6,4},{1,7},{3,1},{5,3},{7,5},{8,14},{10,8},{12,... | collective-permute-start | bytes 49160 | tf_op jit(solution)/shard_map/ppermute | solution.py:608
  716.7 13.5 %collective-permute-start.24 = (bf16[64,128]{0,1:T(8,128)(2,1)S(1)}, bf16[64,128]{0,1:T(8,128)(2,1)S(1)}, u32[]{:S(2)}, u32[]{:S(2)}) collective-permute-start(bf16[64,128]{0,1:T(8,128)(2,1)S(1)} %get-tuple-element.157), channel_id=1, source_target_pairs={{0,4},{2,6},{4,0},{6,2},{1,5},{3,7},{5,1},{7,3},{8,12},{10,14},{12... | collective-permute-start | bytes 49160 | tf_op jit(solution)/shard_map/ppermute | solution.py:608
  (27 other events, 97.6 us)
Sparse Core Ops, SparseCore 0:
  9.7 85.7 all-gather.4
  97.1 84.4 all-gather.6
  199.3 72.8 reduce-scatter.4
  277.8 65.2 all-gather.8
  380.0 70.8 reduce-scatter.6
  458.5 65.2 all-gather.10
  567.0 58.0 reduce-scatter.8
  635.1 71.7 reduce-scatter.10

commit v5 on v4

--- a/solution.py
+++ b/solution.py
@@ -546,17 +546,17 @@
 
     unit_own = jnp.stack([unit_sum(gate_parts), unit_sum(up_parts)])
     unit_own = plain(jnp.transpose(unit_own, (2, 0, 3, 1)))
-    branch, layer_part, gain_two_cols, unit_own = lax.optimization_barrier(
-        (tree_gather(branch_grad), layer_part, gain_two_cols, unit_own)
-    )
-    down_sent = after(down_parts, branch)
-    down_got = [over_dp(at_index(down_sent, d_at ^ m), m) for m in range(1, dn)]
+    down_sent = [at_index(down_parts, d_at ^ m) for m in range(dn)]
+    branch, layer_part, gain_two_cols, unit_own, *down_sent = lax.optimization_barrier(
+        (tree_gather(branch_grad), layer_part, gain_two_cols, unit_own, *down_sent)
+    )
+    down_got = [over_dp(down_sent[m], m) for m in range(1, dn)]
     unit_got = exchange(unit_own, TREE)
     query_grad, back_part = attention_back(
         bits, lse, cosines, sines, query_all, key_all, value_all, attended, branch, out_cols, qup_cols, heads, seg_len
     )
     back_part, unit_got, *down_got = lax.optimization_barrier((back_part, unit_got, *down_got))
-    grad_down = at_index(down_sent, d_at).astype(F32)
+    grad_down = down_sent[0].astype(F32)
     for got in down_got:
         grad_down = grad_down + got.astype(F32)
     out_grads = jnp.swapaxes(

time: 752 us -> 750 us (level)
  transfers between devices with their start and end apart: 46 -> 46, of which waited for: 22 -> 23; matrix products, arithmetic and copies ran while one was open for 26% -> 26% of each run, Pallas kernels for 13% -> 13%
where the time goes in v5:
time: 750 us; the launch traced here: 740 us
  waiting for transfers between devices  247 us (33%)
  Pallas kernels  132 us (18%)
  local copies, waits for them, and re-layouts  98.4 us (13%)
  starting transfers between devices  92.9 us (12%)
  other arithmetic  63.6 us (8%)
  matrix products  51.7 us (7%)
  blocking collectives  38.5 us (5%)
  between operations  15.2 us (2%)
    reduce_scatter x4, waiting for transfers between devices, tree_scatter(): lax.psum_scatter(parts, TREE, scatter_dimension=0, tiled=True).astype(F32)  89 us
    all_gather x4, waiting for transfers between devices, tree_gather(): return lax.all_gather(block, TREE, axis=0, tiled=True)  72.4 us
    all_to_all x12, starting transfers between devices, exchange(): return lax.all_to_all(parts, axes, split_axis=0, concat_axis=0, tiled=True)  63.5 us
    all_to_all x12, waiting for transfers between devices, exchange(): return lax.all_to_all(parts, axes, split_axis=0, concat_axis=0, tiled=True)  43.4 us
    all_to_all x1, blocking collectives, exchange(): return lax.all_to_all(parts, axes, split_axis=0, concat_axis=0, tiled=True)  38.5 us
    pallas_call x1, Pallas kernels, ffn(): pl.pallas_call(ffn_kernel, grid=(count // rows,), out_shape=[jax.ShapeDty...  36.7 us
    pallas_call x1, Pallas kernels, attention_back(): pl.pallas_call(functools.partial(attn_bwd_kernel, heads, seg_len), out_sh...  33.2 us
    dot_general x5, matrix products, dot_tn(): lax.dot_general(a, b, (((0,), (0,)), ((), ())), preferred_element_type=F32)  27.3 us
  transfers between devices with their start and end apart: 46, of which 23 were waited for; matrix products, arithmetic and copies ran while one was open for 26% of the time, Pallas kernels for 13%

profile of v5, /device:TPU:0, one launch (start us, length us, event | category | flops | bytes accessed | tf_op | source)
XLA Modules:
  0.0 740.0 jit_solution(7356110522180667105)
XLA Ops:
  12.2 5.1 collective-permute-start.2
  23.5 4.1 all-to-all-start
  38.4 4.7 collective-permute-done
  45.4 7.3 collective-permute-done.1
  56.9 4.6 all-to-all-done
  63.6 3.9 all-to-all-start.1
  67.6 27.8 %all-gather.5.cloned.1.call-done.x_ref = bf16[1600,2048]{1,0:T(8,128)(2,1)} async-done(((bf16[200,2048]{1,0:T(8,128)(2,1)}), bf16[1600,2048]{1,0:T(8,128)(2,1)}) %all-gather.5.cloned.1.call-update) | async-done | bytes 6553616 | tf_op jit(solution)/shard_map/all_gather | solution.py:418
  95.5 8.2 %all-to-all-done.1 = bf16[4,4,64,1664]{3,2,1,0:T(8,128)(2,1)S(1)} async-done(((bf16[4,4,64,1664]{3,2,1,0:T(8,128)(2,1)}), bf16[4,4,64,1664]{3,2,1,0:T(8,128)(2,1)S(1)}, u32[]{:S(2)}, u32[]{:S(2)}) %all-to-all-start.1) | async-done | bytes 3407904 | tf_op jit(solution)/shard_map/all_to_all | solution.py:384
  106.8 4.4 all-to-all-start.2
  111.2 4.3 select_bitcast_fusion.1
  127.2 16.2 %all-to-all-start.3 = ((bf16[8,2,64,704]{3,2,1,0:T(8,128)(2,1)}), bf16[8,2,64,704]{3,2,1,0:T(8,128)(2,1)}, u32[]{:S(2)}, u32[]{:S(2)}) async-start(bf16[8,2,64,704]{3,2,1,0:T(8,128)(2,1)} %copy.108), calls=%async_computation.3 | async-start | bytes 3145728 | tf_op jit(solution)/shard_map/all_to_all | solution.py:384
  143.5 19.0 %project.1 = (bf16[1600,512]{1,0:T(8,128)(2,1)}, bf16[1600,256]{1,0:T(8,128)(2,1)}, bf16[1600,256]{1,0:T(8,128)(2,1)}, bf16[1600,1024]{1,0:T(8,128)(2,1)}) custom-call(bf16[1600,2048]{1,0:T(8,128)(2,1)} %all-gather.5.cloned.1.call-done.x_ref, bf16[2048,1664]{1,0:T(8,128)(2,1)} %bitcast.219, bf16[1024,512]{1,0:T(8,128)(2,1)} %bitcast.23.qup_ref.wq_ref, ...), custom_call_target="tpu_custom_call" | custom-call | flops 11744051200 | bytes 22815744 | tf_op jit(solution)/shard_map/project/pallas_call | solution.py:273
  170.6 23.3 %attn_fwd.1 = (bf16[1600,512]{1,0:T(8,128)(2,1)}, f32[5,1,640]{2,1,0:T(1,128)}, bf16[1600,2048]{1,0:T(8,128)(2,1)}) custom-call(s32[5,1,640]{2,1,0:T(1,128)} %reshape.310.bits_ref, bf16[1600,512]{1,0:T(8,128)(2,1)} %get-tuple-element.75.q_ref, bf16[1600,256]{1,0:T(8,128)(2,1)} %get-tuple-element.76.k_ref, bf16[1600,256]{1,0:T(8,128)(2,1)} %get-tuple-element.77.v_ref, ...), custom_call_target="tpu_custom_call" | custom-call | flops 3932160000 | bytes 4915200 | tf_op jit(solution)/shard_map/attn_fwd/pallas_call | solution.py:204
  193.9 5.0 collective-permute-done.9
  204.1 4.8 all-to-all-start.4
  219.9 52.3 %reduce-scatter.5.cloned.1.call-done = bf16[200,2048]{1,0:T(8,128)(2,1)} async-done(((bf16[1600,2048]{1,0:T(8,128)(2,1)}), bf16[200,2048]{1,0:T(8,128)(2,1)}) %reduce-scatter.5.cloned.1.call-update) | async-done | bytes 819216 | tf_op jit(solution)/shard_map/reduce_scatter | solution.py:421
  278.1 38.5 %all_to_all.65 = bf16[4,8,64,704]{3,2,1,0:T(8,128)(2,1)} all-to-all(bf16[4,8,64,704]{3,2,1,0:T(8,128)(2,1)S(1)} %broadcast_in_dim.151), channel_id=1, replica_groups=mesh['dp'=4,'q'=4,'r'=1,'c'=2] {'dp'}, dimensions={0} | all-to-all | bytes 5767168 | tf_op jit(solution)/shard_map/all_to_all | solution.py:384
  316.6 26.5 %all-gather.9.cloned.1.call-done.mid_ref = bf16[1600,2048]{1,0:T(8,128)(2,1)} async-done(((bf16[200,2048]{1,0:T(8,128)(2,1)}), bf16[1600,2048]{1,0:T(8,128)(2,1)}) %all-gather.9.cloned.1.call-update) | async-done | bytes 6553616 | tf_op jit(solution)/shard_map/all_gather | solution.py:418
  343.1 36.7 %ffn.1 = (bf16[1600,704]{1,0:T(8,128)(2,1)}, bf16[1600,704]{1,0:T(8,128)(2,1)}, bf16[1600,704]{1,0:T(8,128)(2,1)}, bf16[1600,2048]{1,0:T(8,128)(2,1)}) custom-call(bf16[1600,2048]{1,0:T(8,128)(2,1)} %all-gather.9.cloned.1.call-done.mid_ref, bf16[1600,2048]{1,0:T(8,128)(2,1)} %all-gather.7.cloned.1.call-done.cot_ref, bf16[2048,704]{1,0:T(8,128)(2,1)} %bitcast.35.wg_ref, ...), custom_call_target="tpu_custom_call" | custom-call | flops 23068672000 | bytes 28311552 | tf_op jit(solution)/shard_map/ffn/pallas_call | solution.py:312
  379.8 10.1 %unit_grads.2 = bf16[4,704,512]{2,1,0:T(8,128)(2,1)} custom-call(bf16[1600,2048]{1,0:T(8,128)(2,1)} %all-gather.9.cloned.1.call-done.mid_ref, bf16[1600,704]{1,0:T(8,128)(2,1)} %get-tuple-element.93.grad_ref), custom_call_target="tpu_custom_call" | custom-call | flops 4613734400 | bytes 9437184 | tf_op jit(solution)/shard_map/unit_grads/pallas_call | solution.py:338
  389.9 4.6 all-to-all-start.6
  394.6 9.6 %convolution_convert_fusion.2 = bf16[704,2048]{1,0:T(8,128)(2,1)} fusion(bf16[1600,704]{1,0:T(8,128)(2,1)} %get-tuple-element.99, bf16[1600,2048]{1,0:T(8,128)(2,1)} %all-gather.7.cloned.1.call-done.cot_ref), kind=kOutput, calls=%fused_computation.11 | convolution fusion | flops 4615176192 | bytes 11689984 | tf_op jit(solution)/shard_map/dot_general | solution.py:37
  404.1 10.0 %unit_grads.3 = bf16[4,704,512]{2,1,0:T(8,128)(2,1)} custom-call(bf16[1600,2048]{1,0:T(8,128)(2,1)} %all-gather.9.cloned.1.call-done.mid_ref, bf16[1600,704]{1,0:T(8,128)(2,1)} %get-tuple-element.97.grad_ref), custom_call_target="tpu_custom_call" | custom-call | flops 4613734400 | bytes 9437184 | tf_op jit(solution)/shard_map/unit_grads/pallas_call | solution.py:338
  414.1 36.8 %reduce-scatter.7.cloned.1.call-done = bf16[200,2048]{1,0:T(8,128)(2,1)} async-done(((bf16[1600,2048]{1,0:T(8,128)(2,1)}), bf16[200,2048]{1,0:T(8,128)(2,1)}) %reduce-scatter.7.cloned.1.call-update) | async-done | bytes 819216 | tf_op jit(solution)/shard_map/reduce_scatter | solution.py:421
  458.3 4.8 all-to-all-start.7
  463.2 3.9 dynamic-slice_bitcast_fusion.2
  467.1 9.0 %convolution_convert_fusion = bf16[1600,2048]{1,0:T(8,128)(2,1)} fusion(bf16[1600,704]{1,0:T(8,128)(2,1)S(1)} %copy-done.31, bf16[704,2048]{1,0:T(8,128)(2,1)} %bitcast.40.wd_ref), kind=kOutput, calls=%fused_computation | convolution fusion | flops 4617011200 | bytes 11689984 | tf_op jit(solution)/shard_map/dot_general | solution.py:29
  480.8 13.8 %all-to-all-done.7 = bf16[4,704,512]{2,1,0:T(8,128)(2,1)} async-done(((bf16[4,704,512]{2,1,0:T(8,128)(2,1)}), bf16[4,704,512]{2,1,0:T(8,128)(2,1)}, u32[]{:S(2)}, u32[]{:S(2)}) %all-to-all-start.7) | async-done | bytes 2883616 | tf_op jit(solution)/shard_map/all_to_all | solution.py:384
  505.7 18.1 %all-gather.11.cloned.1.call-done.branch_ref = bf16[1600,2048]{1,0:T(8,128)(2,1)} async-done(((bf16[200,2048]{1,0:T(8,128)(2,1)}), bf16[1600,2048]{1,0:T(8,128)(2,1)}) %all-gather.11.cloned.1.call-update) | async-done | bytes 6553616 | tf_op jit(solution)/shard_map/all_gather | solution.py:418
  523.8 4.3 all-to-all-start.8
  531.7 33.2 %attn_bwd.1 = (bf16[1600,512]{1,0:T(8,128)(2,1)}, bf16[1600,1536]{1,0:T(8,128)(2,1)}) custom-call(s32[5,1,640]{2,1,0:T(1,128)} %reshape.310.bits_ref, f32[5,1,640]{2,1,0:T(1,128)} %get-tuple-element.102.lse_ref, f32[1600,128]{1,0:T(8,128)} %bitcast.245, f32[1600,128]{1,0:T(8,128)} %bitcast.242, bf16[1600,512]{1,0:T(8,128)(2,1)} %get-tuple-element.75.q_ref, ...), custom_call_target="tpu_custom_call" | custom-call | flops 9175040000 | bytes 9830400 | tf_op jit(solution)/shard_map/attn_bwd/pallas_call | solution.py:224
  565.9 7.4 convolution_convert_fusion.3
  582.5 4.0 all-to-all-start.9
  595.8 6.0 reshape.329
  601.8 4.7 copy.126
  616.2 3.9 all-to-all-start.10
  620.2 3.9 collective-permute-done.17
  633.0 3.6 multiply_reduce_fusion.3
  642.8 4.0 collective-permute-done.18
  646.8 4.7 add_convert_fusion
  651.5 4.9 all-to-all-start.11
  662.4 5.0 fusion.9
  681.0 12.7 %all-to-all-done.11 = bf16[4,4,64,1536]{3,2,1,0:T(8,128)(2,1)} async-done(((bf16[4,4,64,1536]{3,2,1,0:T(8,128)(2,1)}), bf16[4,4,64,1536]{3,2,1,0:T(8,128)(2,1)}, u32[]{:S(2)}, u32[]{:S(2)}) %all-to-all-start.11) | async-done | bytes 3145760 | tf_op jit(solution)/shard_map/all_to_all | solution.py:384
  693.7 3.5 reduce_sum.140
  702.5 3.5 all-to-all-start.12
  710.7 3.8 collective-permute-start.25
  717.8 5.7 collective-permute-done.23
  723.5 4.7 collective-permute-done.24
  (285 shorter events, 183.8 us)
Async XLA Ops:
  7.2 88.3 %all-gather.5.cloned.1.call-start = ((), (), s32[]{:S(2)}) async-start(), calls=%async_computation.17 | async-start | bytes 7372800 | tf_op jit(solution)/shard_map/all_gather | solution.py:418
  12.2 41.5 %collective-permute-start.2 = (bf16[64,1664]{1,0:T(8,128)(2,1)S(1)}, bf16[64,1664]{1,0:T(8,128)(2,1)}, u32[]{:S(2)}, u32[]{:S(2)}) collective-permute-start(bf16[64,1664]{1,0:T(8,128)(2,1)S(1)} %concatenate.7), channel_id=1, source_target_pairs={{0,6},{2,0},{4,2},{6,4},{1,7},{3,1},{5,3},{7,5},{8,14},{10,8},{12,... | collective-permute-start | bytes 638984 | tf_op jit(solution)/shard_map/ppermute | solution.py:437
  17.3 35.4 %collective-permute-start.1 = (bf16[64,1664]{1,0:T(8,128)(2,1)S(1)}, bf16[64,1664]{1,0:T(8,128)(2,1)}, u32[]{:S(2)}, u32[]{:S(2)}) collective-permute-start(bf16[64,1664]{1,0:T(8,128)(2,1)S(1)} %concatenate.7), channel_id=1, source_target_pairs={{0,4},{2,6},{4,0},{6,2},{1,5},{3,7},{5,1},{7,3},{8,12},{10,14},{12... | collective-permute-start | bytes 638984 | tf_op jit(solution)/shard_map/ppermute | solution.py:437
  17.3 25.8 %collective-permute-start = (bf16[64,1664]{1,0:T(8,128)(2,1)S(1)}, bf16[64,1664]{1,0:T(8,128)(2,1)}, u32[]{:S(2)}, u32[]{:S(2)}) collective-permute-start(bf16[64,1664]{1,0:T(8,128)(2,1)S(1)} %concatenate.7), channel_id=1, source_target_pairs={{0,2},{2,4},{4,6},{6,0},{1,3},{3,5},{5,7},{7,1},{8,10},{10,12},{12... | collective-permute-start | bytes 638984 | tf_op jit(solution)/shard_map/ppermute | solution.py:437
  18.3 36.4 %collective-permute-start.3 = (bf16[128,2048]{1,0:T(8,128)(2,1)}, bf16[128,2048]{1,0:T(8,128)(2,1)}, u32[]{:S(2)}, u32[]{:S(2)}) collective-permute-start(bf16[128,2048]{1,0:T(8,128)(2,1)} %param.24), channel_id=1, source_target_pairs={{0,8},{8,0},{16,24},{24,16},{1,9},{9,1},{17,25},{25,17},{2,10},{10... | collective-permute-start | bytes 1572872 | tf_op jit(solution)/shard_map/ppermute | solution.py:424
  19.8 36.0 %collective-permute-start.5 = (bf16[128,2048]{1,0:T(8,128)(2,1)}, bf16[128,2048]{1,0:T(8,128)(2,1)}, u32[]{:S(2)}, u32[]{:S(2)}) collective-permute-start(bf16[128,2048]{1,0:T(8,128)(2,1)} %param.24), channel_id=1, source_target_pairs={{0,24},{8,16},{16,8},{24,0},{1,25},{9,17},{17,9},{25,1},{2,26},{10... | collective-permute-start | bytes 1572872 | tf_op jit(solution)/shard_map/ppermute | solution.py:424
  23.5 38.0 %all-to-all-start = ((bf16[8,32,512]{2,1,0:T(8,128)(2,1)}), bf16[8,32,512]{2,1,0:T(8,128)(2,1)S(1)}, u32[]{:S(2)}, u32[]{:S(2)}) async-start(bf16[8,32,512]{2,1,0:T(8,128)(2,1)} %reshape.302), calls=%async_computation | async-start | bytes 524288 | tf_op jit(solution)/shard_map/all_to_all | solution.py:384
  43.1 12.6 %collective-permute-start.4 = (bf16[128,2048]{1,0:T(8,128)(2,1)S(1)}, bf16[128,2048]{1,0:T(8,128)(2,1)S(1)}, u32[]{:S(2)}, u32[]{:S(2)}) collective-permute-start(bf16[128,2048]{1,0:T(8,128)(2,1)S(1)} %copy-done.26), channel_id=1, source_target_pairs={{0,16},{8,24},{16,0},{24,8},{1,17},{9,25},{17,1},{25,9},{2,18},{10... | collective-permute-start | bytes 1572872 | tf_op jit(solution)/shard_map/ppermute | solution.py:424
  63.6 40.1 %copy-start.28 = (s32[1,20]{1,0:T(1,128)S(1)}, s32[1,20]{1,0:T(1,128)}, u32[]{:S(2)}) copy-start(s32[1,20]{1,0:T(1,128)} %param.17) | copy-start | bytes 244
  63.6 40.1 %all-to-all-start.1 = ((bf16[4,4,64,1664]{3,2,1,0:T(8,128)(2,1)}), bf16[4,4,64,1664]{3,2,1,0:T(8,128)(2,1)S(1)}, u32[]{:S(2)}, u32[]{:S(2)}) async-start(bf16[4,4,64,1664]{3,2,1,0:T(8,128)(2,1)} %broadcast_in_dim.138), calls=%async_computation.1 | async-start | bytes 6815744 | tf_op jit(solution)/shard_map/all_to_all | solution.py:384
  67.5 131.7 %all-gather.7.cloned.1.call-start = ((), (), s32[]{:S(2)}) async-start(), calls=%async_computation.18 | async-start | bytes 7372800 | tf_op jit(solution)/shard_map/all_gather | solution.py:418
  103.7 7.6 %collective-permute-start.6 = (bf16[4,4,64,1664]{3,2,1,0:T(8,128)(2,1)S(1)}, bf16[4,4,64,1664]{3,2,1,0:T(8,128)(2,1)}, u32[]{:S(2)}, u32[]{:S(2)}) collective-permute-start(bf16[4,4,64,1664]{3,2,1,0:T(8,128)(2,1)S(1)} %all-to-all-done.1), channel_id=1, source_target_pairs={{0,1},{1,0},{2,3},{3,2},{4,5},{5,4},{6,7},{7,6},{8,9},{9,8},{10,11... | collective-permute-start | bytes 10223624 | tf_op jit(solution)/shard_map/ppermute | solution.py:393
  106.8 19.1 %all-to-all-start.2 = ((bf16[4,8,32,512]{3,2,1,0:T(8,128)(2,1)}), bf16[4,8,32,512]{3,2,1,0:T(8,128)(2,1)}, u32[]{:S(2)}, u32[]{:S(2)}) async-start(bf16[4,8,32,512]{3,2,1,0:T(8,128)(2,1)} %broadcast_in_dim.143), calls=%async_computation.2 | async-start | bytes 2097152 | tf_op jit(solution)/shard_map/all_to_all | solution.py:384
  127.2 72.0 %all-to-all-start.3 = ((bf16[8,2,64,704]{3,2,1,0:T(8,128)(2,1)}), bf16[8,2,64,704]{3,2,1,0:T(8,128)(2,1)}, u32[]{:S(2)}, u32[]{:S(2)}) async-start(bf16[8,2,64,704]{3,2,1,0:T(8,128)(2,1)} %copy.108), calls=%async_computation.3 | async-start | bytes 3145728 | tf_op jit(solution)/shard_map/all_to_all | solution.py:384
  143.5 128.7 %reduce-scatter.5.cloned.1.call-start = ((), (), s32[]{:S(2)}) async-start(), calls=%async_computation.19 | async-start | bytes 7372800 | tf_op jit(solution)/shard_map/reduce_scatter | solution.py:421
  162.6 4.9 collective-permute-start.7
  164.1 29.8 %collective-permute-start.10 = (bf16[176,2048]{1,0:T(8,128)(2,1)}, bf16[176,2048]{1,0:T(8,128)(2,1)}, u32[]{:S(2)}, u32[]{:S(2)}) collective-permute-start(bf16[176,2048]{1,0:T(8,128)(2,1)} %param.28), channel_id=1, source_target_pairs={{0,24},{8,16},{16,8},{24,0},{1,25},{9,17},{17,9},{25,1},{2,26},{10... | collective-permute-start | bytes 2162696 | tf_op jit(solution)/shard_map/ppermute | solution.py:424
  166.8 32.1 %collective-permute-start.9 = (bf16[176,2048]{1,0:T(8,128)(2,1)}, bf16[176,2048]{1,0:T(8,128)(2,1)}, u32[]{:S(2)}, u32[]{:S(2)}) collective-permute-start(bf16[176,2048]{1,0:T(8,128)(2,1)} %param.28), channel_id=1, source_target_pairs={{0,16},{8,24},{16,0},{24,8},{1,17},{9,25},{17,1},{25,9},{2,18},{10... | collective-permute-start | bytes 2162696 | tf_op jit(solution)/shard_map/ppermute | solution.py:424
  167.4 31.8 %collective-permute-start.8 = (bf16[176,2048]{1,0:T(8,128)(2,1)}, bf16[176,2048]{1,0:T(8,128)(2,1)}, u32[]{:S(2)}, u32[]{:S(2)}) collective-permute-start(bf16[176,2048]{1,0:T(8,128)(2,1)} %param.28), channel_id=1, source_target_pairs={{0,8},{8,0},{16,24},{24,16},{1,9},{9,1},{17,25},{25,17},{2,10},{10... | collective-permute-start | bytes 2162696 | tf_op jit(solution)/shard_map/ppermute | solution.py:424
  204.1 70.6 %all-to-all-start.4 = ((bf16[4,8,64,704]{3,2,1,0:T(8,128)(2,1)}), bf16[4,8,64,704]{3,2,1,0:T(8,128)(2,1)}, u32[]{:S(2)}, u32[]{:S(2)}) async-start(bf16[4,8,64,704]{3,2,1,0:T(8,128)(2,1)} %broadcast_in_dim.145), calls=%async_computation.5 | async-start | bytes 6291456 | tf_op jit(solution)/shard_map/all_to_all | solution.py:384
  209.0 134.2 %all-gather.9.cloned.1.call-start = ((), (), s32[]{:S(2)}) async-start(), calls=%async_computation.20 | async-start | bytes 7372800 | tf_op jit(solution)/shard_map/all_gather | solution.py:418
  277.7 173.2 %reduce-scatter.7.cloned.1.call-start = ((), (), s32[]{:S(2)}) async-start(), calls=%async_computation.21 | async-start | bytes 7372800 | tf_op jit(solution)/shard_map/reduce_scatter | solution.py:421
  389.9 63.6 %all-to-all-start.6 = ((bf16[4,704,512]{2,1,0:T(8,128)(2,1)}), bf16[4,704,512]{2,1,0:T(8,128)(2,1)}, u32[]{:S(2)}, u32[]{:S(2)}) async-start(bf16[4,704,512]{2,1,0:T(8,128)(2,1)} %unit_grads.2), calls=%async_computation.8 | async-start | bytes 5767168 | tf_op jit(solution)/shard_map/all_to_all | solution.py:384
  394.5 129.3 %all-gather.11.cloned.1.call-start = ((), (), s32[]{:S(2)}) async-start(), calls=%async_computation.22 | async-start | bytes 7372800 | tf_op jit(solution)/shard_map/all_gather | solution.py:418
  458.3 36.3 %all-to-all-start.7 = ((bf16[4,704,512]{2,1,0:T(8,128)(2,1)}), bf16[4,704,512]{2,1,0:T(8,128)(2,1)}, u32[]{:S(2)}, u32[]{:S(2)}) async-start(bf16[4,704,512]{2,1,0:T(8,128)(2,1)} %unit_grads.3), calls=%async_computation.9 | async-start | bytes 5767168 | tf_op jit(solution)/shard_map/all_to_all | solution.py:384
  505.7 25.4 %copy-start.24 = (bf16[176,2048]{1,0:T(8,128)(2,1)S(1)}, bf16[176,2048]{1,0:T(8,128)(2,1)}, u32[]{:S(2)}) copy-start(bf16[176,2048]{1,0:T(8,128)(2,1)} %get-tuple-element.109) | copy-start | bytes 2162692
  523.8 42.1 %all-to-all-start.8 = ((bf16[8,2,64,704]{3,2,1,0:T(8,128)(2,1)}), bf16[8,2,64,704]{3,2,1,0:T(8,128)(2,1)}, u32[]{:S(2)}, u32[]{:S(2)}) async-start(bf16[8,2,64,704]{3,2,1,0:T(8,128)(2,1)} %maximum_bitcast_fusion), calls=%async_computation.10 | async-start | bytes 3145728 | tf_op jit(solution)/shard_map/all_to_all | solution.py:384
  528.1 102.5 %reduce-scatter.9.cloned.1.call-start = ((), (), s32[]{:S(2)}) async-start(), calls=%async_computation.23 | async-start | bytes 5529600 | tf_op jit(solution)/shard_map/reduce_scatter | solution.py:421
  528.1 36.7 %collective-permute-start.11 = (bf16[176,2048]{1,0:T(8,128)(2,1)}, bf16[176,2048]{1,0:T(8,128)(2,1)}, u32[]{:S(2)}, u32[]{:S(2)}) collective-permute-start(bf16[176,2048]{1,0:T(8,128)(2,1)} %get-tuple-element.107), channel_id=1, source_target_pairs={{0,8},{8,0},{16,24},{24,16},{1,9},{9,1},{17,25},{25,17},{2,10},{10... | collective-permute-start | bytes 2162696 | tf_op jit(solution)/shard_map/ppermute | solution.py:424
  529.7 35.2 %collective-permute-start.12 = (bf16[176,2048]{1,0:T(8,128)(2,1)}, bf16[176,2048]{1,0:T(8,128)(2,1)}, u32[]{:S(2)}, u32[]{:S(2)}) collective-permute-start(bf16[176,2048]{1,0:T(8,128)(2,1)} %get-tuple-element.108), channel_id=1, source_target_pairs={{0,16},{8,24},{16,0},{24,8},{1,17},{9,25},{17,1},{25,9},{2,18},{10... | collective-permute-start | bytes 2162696 | tf_op jit(solution)/shard_map/ppermute | solution.py:424
  531.2 33.7 %collective-permute-start.13 = (bf16[176,2048]{1,0:T(8,128)(2,1)S(1)}, bf16[176,2048]{1,0:T(8,128)(2,1)}, u32[]{:S(2)}, u32[]{:S(2)}) collective-permute-start(bf16[176,2048]{1,0:T(8,128)(2,1)S(1)} %copy-done.24), channel_id=1, source_target_pairs={{0,24},{8,16},{16,8},{24,0},{1,25},{9,17},{17,9},{25,1},{2,26},{10... | collective-permute-start | bytes 2162696 | tf_op jit(solution)/shard_map/ppermute | solution.py:424
  573.4 2.7 collective-permute-start.14
  582.5 32.9 %all-to-all-start.9 = ((bf16[4,256,512]{2,1,0:T(8,128)(2,1)}), bf16[4,256,512]{2,1,0:T(8,128)(2,1)S(1)}, u32[]{:S(2)}, u32[]{:S(2)}) async-start(bf16[4,256,512]{2,1,0:T(8,128)(2,1)} %bitcast.239), calls=%async_computation.12 | async-start | bytes 2097152 | tf_op jit(solution)/shard_map/all_to_all | solution.py:384
  589.2 31.0 %collective-permute-start.15 = (bf16[128,2048]{1,0:T(8,128)(2,1)}, bf16[128,2048]{1,0:T(8,128)(2,1)}, u32[]{:S(2)}, u32[]{:S(2)}) collective-permute-start(bf16[128,2048]{1,0:T(8,128)(2,1)} %get-tuple-element.147), channel_id=1, source_target_pairs={{0,8},{8,0},{16,24},{24,16},{1,9},{9,1},{17,25},{25,17},{2,10},{10... | collective-permute-start | bytes 1572872 | tf_op jit(solution)/shard_map/ppermute | solution.py:424
  591.2 32.9 %collective-permute-start.17 = (bf16[128,2048]{1,0:T(8,128)(2,1)}, bf16[128,2048]{1,0:T(8,128)(2,1)}, u32[]{:S(2)}, u32[]{:S(2)}) collective-permute-start(bf16[128,2048]{1,0:T(8,128)(2,1)} %get-tuple-element.148), channel_id=1, source_target_pairs={{0,24},{8,16},{16,8},{24,0},{1,25},{9,17},{17,9},{25,1},{2,26},{10... | collective-permute-start | bytes 1572872 | tf_op jit(solution)/shard_map/ppermute | solution.py:424
  592.6 31.4 %collective-permute-start.16 = (bf16[128,2048]{1,0:T(8,128)(2,1)}, bf16[128,2048]{1,0:T(8,128)(2,1)}, u32[]{:S(2)}, u32[]{:S(2)}) collective-permute-start(bf16[128,2048]{1,0:T(8,128)(2,1)} %get-tuple-element.149), channel_id=1, source_target_pairs={{0,16},{8,24},{16,0},{24,8},{1,17},{9,25},{17,1},{25,9},{2,18},{10... | collective-permute-start | bytes 1572872 | tf_op jit(solution)/shard_map/ppermute | solution.py:424
  616.2 13.6 %all-to-all-start.10 = ((bf16[8,32,512]{2,1,0:T(8,128)(2,1)}), bf16[8,32,512]{2,1,0:T(8,128)(2,1)S(1)}, u32[]{:S(2)}, u32[]{:S(2)}) async-start(bf16[8,32,512]{2,1,0:T(8,128)(2,1)} %bitcast.238), calls=%async_computation.13 | async-start | bytes 524288 | tf_op jit(solution)/shard_map/all_to_all | solution.py:384
  620.1 110.6 %reduce-scatter.11.cloned.1.call-start = ((), (), s32[]{:S(2)}) async-start(), calls=%async_computation.24 | async-start | bytes 7372800 | tf_op jit(solution)/shard_map/reduce_scatter | solution.py:421
  640.8 6.0 collective-permute-start.18
  651.5 42.2 %all-to-all-start.11 = ((bf16[4,4,64,1536]{3,2,1,0:T(8,128)(2,1)}), bf16[4,4,64,1536]{3,2,1,0:T(8,128)(2,1)}, u32[]{:S(2)}, u32[]{:S(2)}) async-start(bf16[4,4,64,1536]{3,2,1,0:T(8,128)(2,1)} %bitcast.211), calls=%async_computation.15 | async-start | bytes 6291456 | tf_op jit(solution)/shard_map/all_to_all | solution.py:384
  672.1 6.7 collective-permute-start.19
  699.1 7.0 collective-permute-start.20
  700.5 7.6 %collective-permute-start.22 = (bf16[4,64,128]{1,2,0:T(8,128)(2,1)}, bf16[4,64,128]{1,2,0:T(8,128)(2,1)S(1)}, u32[]{:S(2)}, u32[]{:S(2)}) collective-permute-start(bf16[4,64,128]{1,2,0:T(8,128)(2,1)} %get-tuple-element.153), channel_id=1, source_target_pairs={{0,24},{8,16},{16,8},{24,0},{1,25},{9,17},{17,9},{25,1},{2,26},{10... | collective-permute-start | bytes 196616 | tf_op jit(solution)/shard_map/ppermute | solution.py:424
  702.0 7.5 %collective-permute-start.21 = (bf16[4,64,128]{1,2,0:T(8,128)(2,1)}, bf16[4,64,128]{1,2,0:T(8,128)(2,1)}, u32[]{:S(2)}, u32[]{:S(2)}) collective-permute-start(bf16[4,64,128]{1,2,0:T(8,128)(2,1)} %get-tuple-element.154), channel_id=1, source_target_pairs={{0,16},{8,24},{16,0},{24,8},{1,17},{9,25},{17,1},{25,9},{2,18},{10... | collective-permute-start | bytes 196616 | tf_op jit(solution)/shard_map/ppermute | solution.py:424
  702.5 26.7 %all-to-all-start.12 = ((bf16[4,64,1536]{2,1,0:T(8,128)(2,1)}), bf16[4,64,1536]{2,1,0:T(8,128)(2,1)S(1)}, u32[]{:S(2)}, u32[]{:S(2)}) async-start(bf16[4,64,1536]{2,1,0:T(8,128)(2,1)} %reduce_sum.140), calls=%async_computation.16 | async-start | bytes 1572864 | tf_op jit(solution)/shard_map/all_to_all | solution.py:384
  710.7 12.8 %collective-permute-start.23 = (bf16[64,128]{0,1:T(8,128)(2,1)S(1)}, bf16[64,128]{0,1:T(8,128)(2,1)S(1)}, u32[]{:S(2)}, u32[]{:S(2)}) collective-permute-start(bf16[64,128]{0,1:T(8,128)(2,1)S(1)} %get-tuple-element.162), channel_id=1, source_target_pairs={{0,2},{2,4},{4,6},{6,0},{1,3},{3,5},{5,7},{7,1},{8,10},{10,12},{12... | collective-permute-start | bytes 49160 | tf_op jit(solution)/shard_map/ppermute | solution.py:608
  710.7 12.7 %collective-permute-start.25 = (bf16[64,128]{0,1:T(8,128)(2,1)S(1)}, bf16[64,128]{0,1:T(8,128)(2,1)S(1)}, u32[]{:S(2)}, u32[]{:S(2)}) collective-permute-start(bf16[64,128]{0,1:T(8,128)(2,1)S(1)} %get-tuple-element.163), channel_id=1, source_target_pairs={{0,6},{2,0},{4,2},{6,4},{1,7},{3,1},{5,3},{7,5},{8,14},{10,8},{12,... | collective-permute-start | bytes 49160 | tf_op jit(solution)/shard_map/ppermute | solution.py:608
  714.5 13.6 %collective-permute-start.24 = (bf16[64,128]{0,1:T(8,128)(2,1)S(1)}, bf16[64,128]{0,1:T(8,128)(2,1)S(1)}, u32[]{:S(2)}, u32[]{:S(2)}) collective-permute-start(bf16[64,128]{0,1:T(8,128)(2,1)S(1)} %get-tuple-element.164), channel_id=1, source_target_pairs={{0,4},{2,6},{4,0},{6,2},{1,5},{3,7},{5,1},{7,3},{8,12},{10,14},{12... | collective-permute-start | bytes 49160 | tf_op jit(solution)/shard_map/ppermute | solution.py:608
  (30 other events, 128.1 us)
Sparse Core Ops, SparseCore 0:
  9.7 85.7 all-gather.4
  97.1 84.5 all-gather.6
  199.4 72.7 reduce-scatter.4
  277.8 65.2 all-gather.8
  380.0 70.8 reduce-scatter.6
  458.5 65.2 all-gather.10
  566.1 56.9 reduce-scatter.8
  633.0 71.7 reduce-scatter.10
